TPU v7x, 256 devices: a whole 4x4x8 slice. The times are simulated.
256 devices in a mesh: seq: 32 (over z, y), mp: 4 (over x), req: 2 (over core).
Axes of the slice: x: 4, y: 4, z: 8, core: 2. Of those that a mesh axis runs over, the one named last changes fastest.
Arguments:
- hidden: bfloat16 [2, 8192, 3072], P('req', 'seq', 'mp'), may hold values from -6 to 6
- norm_gain: bfloat16 [3072], replicated, may hold values from 0.5 to 1.5
- w_query: bfloat16 [3072, 1024], P(None, 'mp'), may hold values from -0.109375 to 0.109375
- w_keyval: bfloat16 [3072, 512], P(None, 'mp'), may hold values from -0.109375 to 0.109375
- w_attn_out: bfloat16 [1024, 3072], P('mp'), may hold values from -1.5 to 1.5
- w_inner: bfloat16 [3072, 2, 1536], P(None, None, 'mp'), may hold values from -0.109375 to 0.109375
- w_bc: bfloat16 [3072, 512], P(None, 'mp'), may hold values from -0.109375 to 0.109375
- w_dt: bfloat16 [3072, 12], P(None, 'mp'), may hold values from -0.109375 to 0.109375
- dt_bias: float32 [12], P('mp'), may hold values from -4 to 0
- a_log: float32 [12], P('mp'), may hold values from -12 to 0
- d_skip: float32 [12], P('mp'), may hold values from 0.1 to 10
- conv_x: bfloat16 [4, 1536], P(None, 'mp'), may hold values from -3 to 3
- conv_bc: bfloat16 [4, 512], replicated, may hold values from -3 to 3
- mamba_gain: bfloat16 [1536], P('mp'), may hold values from 0.5 to 1.5
- w_mamba_out: bfloat16 [1536, 3072], P('mp'), may hold values from -0.15625 to 0.15625
- cache: bfloat16 [2, 8192, 512], P('req', 'seq', 'mp'), may hold values from -70 to 70, as said below
- cache_len: int32 [2], P('req'), may hold values from 256 to 8192
- tail_x: bfloat16 [2, 3, 1536], P('req', None, 'mp'), may hold values from -6 to 6
- tail_bc: bfloat16 [2, 3, 512], P('req'), may hold values from -6 to 6
- ssm_init: float32 [2, 12, 128, 256], P('req', 'mp'), may hold values from -6 to 6
Outputs:
- layer_out: bfloat16 [2, 8192, 3072], P('req', 'seq', 'mp')
- new_keyval: bfloat16 [2, 8192, 512], P('req', 'seq', 'mp')
- block_states: float32 [2, 32, 12, 128, 256], P('req', 'seq', 'mp')
Inputs may be any that keep to these rules, and one draw needn't show every extreme that they name: Rows of the cache at or past cache_len are unused.
All inputs are finite; a program needn't handle non-finite values.
Results may differ from a plain program's by a relative error of at most 0.0097.
Values may be sent and summed in bfloat16 or wider, within the bound.
A program may use at most 192 MiB of HBM per device.

v0:
```python
import jax
import jax.numpy as jnp
from jax import lax
from jax.sharding import PartitionSpec as P

HD = 128
QH = 8
KVH = 2
NS = 256
CONV = 4


epsilon = 1e-05
rope_base = 100000000000.0
negative = -1e30


def shifted(block, axis, distance):
    devices = range(lax.axis_size(axis))
    route = [(i - distance, i) for i in devices if i - distance in devices]
    return lax.ppermute(block, axis, route)


def prefix(part, axis, combine, identity):
    place = lax.axis_index(axis)
    gathered = jax.tree.map(lambda a: lax.all_gather(a, axis), part)
    state = jax.tree.map(lambda a, e: jnp.zeros_like(a) + jnp.asarray(e, a.dtype), part, identity)

    def one(turn, state):
        return combine(
            state, jax.tree.map(lambda a: lax.dynamic_index_in_dim(a, turn, 0, False), gathered)
        )

    return lax.fori_loop(0, place, one, state)


def rotate(values, positions):
    half = HD // 2
    freqs = rope_base ** (-jnp.arange(half, dtype=jnp.float32) * 2.0 / HD)
    angles = positions.astype(jnp.float32)[:, None] * freqs[None, :]
    cosine = jnp.cos(angles)[:, None, :]
    sine = jnp.sin(angles)[:, None, :]
    first = values[..., :half]
    second = values[..., half:]
    return jnp.concatenate(
        [first * cosine - second * sine, second * cosine + first * sine], axis=-1
    )


def rms_scale(values):
    mean_sq = jnp.mean(values * values, axis=-1, keepdims=True)
    return values * lax.rsqrt(mean_sq + epsilon)


def causal_conv(tail, inputs, taps):
    padded = jnp.concatenate([tail, inputs], axis=0).astype(jnp.float32)
    count = inputs.shape[0]
    total = jnp.zeros(inputs.shape, jnp.float32)
    for offset in range(CONV):
        total = total + taps[offset].astype(jnp.float32)[None, :] * padded[offset : offset + count]
    return jax.nn.silu(total)


def join_states(earlier, later):
    return (earlier[0] * later[0], later[0][:, None, None] * earlier[1] + later[1])


def shards(
    hidden,
    norm_gain,
    w_query,
    w_keyval,
    w_attn_out,
    w_inner,
    w_bc,
    w_dt,
    dt_bias,
    a_log,
    d_skip,
    conv_x,
    conv_bc,
    mamba_gain,
    w_mamba_out,
    cache,
    cache_len,
    tail_x,
    tail_bc,
    ssm_init,
):
    high = lax.Precision.HIGHEST
    own_rows = hidden[0]
    tokens = own_rows.shape[0]
    seq_pos = lax.axis_index("seq")
    mp_pos = lax.axis_index("mp")
    length = cache_len[0]
    whole = lax.all_gather(own_rows, "mp", axis=1, tiled=True)
    normed = (rms_scale(whole.astype(jnp.float32)) * norm_gain.astype(jnp.float32)).astype(
        jnp.bfloat16
    )
    positions = length + seq_pos * tokens + jnp.arange(tokens, dtype=jnp.int32)
    local_heads = w_query.shape[1] // HD
    query = rotate(
        jnp.dot(normed, w_query, preferred_element_type=jnp.float32).reshape(
            tokens, local_heads, HD
        ),
        positions,
    ).astype(jnp.bfloat16)
    projected = jnp.dot(normed, w_keyval, preferred_element_type=jnp.float32)
    roped = rotate(projected[:, None, :], positions)[:, 0, :]
    kv_block = jnp.where(mp_pos % 2 == 0, roped, projected).astype(jnp.bfloat16)
    bc_block = jnp.dot(normed, w_bc, preferred_element_type=jnp.float32).astype(jnp.bfloat16)
    kv_all, bc_all, cache_all = (
        lax.all_gather(kv_block, "mp", axis=1, tiled=True),
        lax.all_gather(bc_block, "mp", axis=1, tiled=True),
        lax.all_gather(cache[0], "mp", axis=1, tiled=True),
    )
    inner = jnp.einsum("td,dkc->tkc", normed, w_inner, preferred_element_type=jnp.float32).astype(
        jnp.bfloat16
    )
    rim = CONV - 1
    prev_x, prev_bc = shifted((inner[tokens - rim :, 1], bc_all[tokens - rim :]), "seq", 1)
    first_block = seq_pos == 0
    prev_x = jnp.where(first_block, tail_x[0], prev_x)
    prev_bc = jnp.where(first_block, tail_bc[0], prev_bc)
    mamba_heads = dt_bias.shape[0]
    x_conv = causal_conv(prev_x, inner[:, 1], conv_x).reshape(tokens, mamba_heads, HD)
    bc_conv = causal_conv(prev_bc, bc_all, conv_bc)
    b_mat = bc_conv[:, :NS]
    c_mat = bc_conv[:, NS:]
    step_size = jax.nn.softplus(jnp.dot(normed, w_dt, preferred_element_type=jnp.float32) + dt_bias)
    log_decay = -step_size * jnp.exp(a_log)[None, :]
    cumulative = jnp.cumsum(log_decay, axis=0)
    pairs = jnp.dot(c_mat, b_mat.T, precision=high)
    gap = cumulative[:, None, :] - cumulative[None, :, :]
    token_ids = jnp.arange(tokens)
    lower = (token_ids[:, None] >= token_ids[None, :])[:, :, None]
    decay = jnp.where(lower, jnp.exp(jnp.where(lower, gap, 0.0)), 0.0)
    mixing = decay * pairs[:, :, None] * step_size[None, :, :]
    inner_out = jnp.einsum("tsh,shp->thp", mixing, x_conv, precision=high)
    to_end = jnp.exp(cumulative[-1][None, :] - cumulative) * step_size
    own_state = jnp.einsum("sh,shp,sn->hpn", to_end, x_conv, b_mat, precision=high)
    block_decay = jnp.exp(cumulative[-1])
    prior_decay, prior_state = prefix(
        (block_decay, own_state),
        "seq",
        join_states,
        (jnp.ones_like(block_decay), jnp.zeros_like(own_state)),
    )
    incoming = prior_state + prior_decay[:, None, None] * ssm_init[0]
    carried = jnp.exp(cumulative)[:, :, None] * jnp.einsum(
        "tn,hpn->thp", c_mat, incoming, precision=high
    )
    mamba_y = inner_out + carried + d_skip[None, :, None] * x_conv
    state_after = block_decay[:, None, None] * incoming + own_state
    gated = mamba_y * jax.nn.silu(inner[:, 0].astype(jnp.float32).reshape(tokens, mamba_heads, HD))
    mixed = (
        rms_scale(gated).reshape(tokens, mamba_heads * HD) * mamba_gain.astype(jnp.float32)
    ).astype(jnp.bfloat16)
    cache_rows = cache_all.shape[0]
    shard_rows = cache_rows + tokens
    local_rows = jnp.concatenate([cache_all, kv_all], axis=0)
    group = mp_pos * local_heads // (QH // KVH)
    query_index = seq_pos * tokens + jnp.arange(tokens, dtype=jnp.int32)
    scale = 1.0 / float(HD) ** 0.5
    piece = lax.all_gather(local_rows, "seq", axis=0, tiled=True)
    top = jnp.full((local_heads, tokens), negative, jnp.float32)
    piece = lax.dynamic_slice_in_dim(piece, group * 2 * HD, 2 * HD, 1)
    count = piece.shape[0]
    index = jnp.arange(count, dtype=jnp.int32)
    owner = index // shard_rows
    offset = index % shard_rows
    in_cache = offset < cache_rows
    slot_ok = in_cache & (owner * cache_rows + offset < length)
    new_index = owner * tokens + offset - cache_rows
    valid = slot_ok[None, :] | (~in_cache)[None, :] & (new_index[None, :] <= query_index[:, None])
    scores = (
        jnp.einsum("qhd,kd->hqk", query, piece[:, :HD], preferred_element_type=jnp.float32) * scale
    )
    masked = jnp.where(valid[None], scores, negative)
    new_top = jnp.maximum(top, jnp.max(masked, axis=-1))
    weights = jnp.where(valid[None], jnp.exp(masked - new_top[:, :, None]), 0.0)
    total = jnp.sum(weights, axis=-1)
    accum = jnp.einsum(
        "hqk,kd->hqd",
        weights.astype(jnp.bfloat16),
        piece[:, HD : 2 * HD],
        preferred_element_type=jnp.float32,
    )
    top, total, accum = (new_top, total, accum)
    attended = jnp.transpose(accum / total[:, :, None], (1, 0, 2)).reshape(tokens, local_heads * HD)
    attended = attended.astype(jnp.bfloat16)
    term = jnp.dot(attended, w_attn_out, preferred_element_type=jnp.float32)
    term = term + jnp.dot(mixed, w_mamba_out, preferred_element_type=jnp.float32)
    summed = lax.psum_scatter(term, "mp", scatter_dimension=1, tiled=True)
    layer = (summed + own_rows.astype(jnp.float32)).astype(jnp.bfloat16)
    return (layer[None], kv_block[None], state_after[None, None])


def solution(mesh):
    placed = (
        P("req", "seq", "mp"),
        P(),
        P(None, "mp"),
        P(None, "mp"),
        P("mp", None),
        P(None, None, "mp"),
        P(None, "mp"),
        P(None, "mp"),
        P("mp"),
        P("mp"),
        P("mp"),
        P(None, "mp"),
        P(),
        P("mp"),
        P("mp", None),
        P("req", "seq", "mp"),
        P("req"),
        P("req", None, "mp"),
        P("req", None, None),
        P("req", "mp", None, None),
    )
    return jax.shard_map(
        shards,
        mesh=mesh,
        in_specs=placed,
        out_specs=(P("req", "seq", "mp"), P("req", "seq", "mp"), P("req", "seq", "mp", None, None)),
        check_vma=False,
    )
```

profile of v0, /device:TPU:1, one launch (start us, length us, event | category | flops | bytes accessed | tf_op | source)
XLA Modules:
  0.0 449.3 jit_solution(8750988892536039679)
XLA Ops:
  7.2 0.0 all-gather.10.cloned.1.call-start
  7.2 0.7 all-gather.10.cloned.1.call-update
  7.9 0.0 all-gather.12.cloned.1.call-start
  8.0 0.7 convert_element_type.78
  8.7 0.7 exp.47
  9.3 0.9 convert_reduce_fusion.3
  10.2 0.8 slice_convert_fusion.4
  11.0 31.7 %all-gather.10.cloned.1.call-done = bf16[1,256,3072]{2,1,0:T(8,128)(2,1)} async-done(((bf16[1,256,768]{2,1,0:T(8,128)(2,1)}), bf16[1,256,3072]{2,1,0:T(8,128)(2,1)}) %all-gather.10.cloned.1.call-update) | async-done | bytes 1572880 | tf_op jit(solution)/shard_map/all_gather | solution.py:96
  42.7 1.9 fusion.9
  44.7 1.9 fusion.11
  46.6 1.4 fusion.13
  48.1 0.9 slice_convert_fusion
  49.0 0.5 fusion.85
  49.5 0.9 reduce-window.6
  50.5 0.1 slice.135
  50.5 0.1 copy.59
  50.7 0.1 copy.60
  50.8 0.1 add_bitcast_fusion.1
  50.9 0.7 slice_reduce_fusion
  51.6 3.1 collective-permute-start
  54.7 2.0 convolution_convert_fusion
  56.7 9.4 %all_gather.29 = bf16[256,512]{1,0:T(8,128)(2,1)S(1)} all-gather(bf16[256,128]{1,0:T(8,128)(2,1)S(1)} %convolution_convert_fusion), channel_id=1, replica_groups=mesh['seq'=32,'mp'=4,'req'=2] {'mp'}, dimensions={1}, use_global_device_ids=true | all-gather | bytes 327680 | tf_op jit(solution)/shard_map/all_gather | solution.py:114
  66.1 3.2 collective-permute-start.1
  69.3 0.6 compare_select_fusion
  69.9 1.0 maximum_convert_fusion.1
  70.9 0.2 divide_multiply_fusion.1
  71.1 0.2 copy.58
  71.3 0.1 maximum_convert_fusion
  71.4 0.3 divide_multiply_fusion
  71.8 1.3 fusion.46
  73.0 0.0 all-gather.12.cloned.1.call-update
  73.0 0.0 all-gather.8.cloned.1.call-start
  73.8 0.1 copy.52
  73.9 9.4 %all-gather = bf16[1,256,512]{1,2,0:T(8,128)(2,1)S(1)} all-gather(bf16[1,256,128]{1,2,0:T(8,128)(2,1)S(1)} %copy.52), channel_id=2, replica_groups=mesh['seq'=32,'mp'=4,'req'=2] {'mp'}, dimensions={2}, use_global_device_ids=true | all-gather | bytes 327680 | tf_op jit(solution)/shard_map/all_gather | solution.py:115
  83.3 2.3 fusion.100
  85.5 0.3 fusion.71
  85.9 9.8 %all_gather.27 = bf16[256,512]{0,1:T(8,128)(2,1)S(1)} all-gather(bf16[256,128]{0,1:T(8,128)(2,1)S(1)} %fusion.63), channel_id=1, replica_groups=mesh['seq'=32,'mp'=4,'req'=2] {'mp'}, dimensions={1}, use_global_device_ids=true | all-gather | bytes 327680 | tf_op jit(solution)/shard_map/all_gather | solution.py:113
  95.7 0.8 pad_maximum_fusion
  96.5 0.0 all-gather.8.cloned.1.call-update
  96.5 0.0 reduce-scatter.2.cloned.1.call-start
  96.6 0.7 iota_compare_fusion
  97.4 1.3 multiply_cosine_fusion
  98.6 15.5 %and_or_fusion = pred[256,16384]{0,1:T(8,128)(4,1)} fusion(s32[256]{0:T(256)S(1)} %iota_add_fusion, s32[16384]{0:T(1024)S(1)} %fusion.82, pred[16384]{0:T(1024)(128)(4,1)S(1)} %get-tuple-element.110, pred[16384]{0:T(1024)(128)(4,1)S(1)} %get-tuple-element.109), kind=kLoop, calls=%fused_computation.9 | loop fusion | flops 12582912 | bytes 4293632 | tf_op jit(solution)/shard_map/or | solution.py:175
  114.1 1.9 copy.63
  116.0 2.6 fusion.101
  118.7 0.1 copy.69
  118.8 0.1 copy.70
  119.0 37.4 %all-gather.3 = f32[32,1,3]{2,1,0:T(1,128)} all-gather(f32[1,1,3]{2,1,0:T(1,128)S(1)} %bitcast.181), channel_id=1, replica_groups=mesh['seq'=32,'mp'=4,'req'=2] {'seq'}, dimensions={0}, use_global_device_ids=true | all-gather | bytes 396 | tf_op jit(solution)/shard_map/all_gather | solution.py:26
  156.4 1.7 subtract_convert_fusion
  158.1 0.4 fusion.57
  158.5 39.1 %all-gather.12.cloned.1.call-done = f32[96,128,256]{2,1,0:T(8,128)} async-done(((f32[3,128,256]{2,1,0:T(8,128)}), f32[96,128,256]{2,1,0:T(8,128)}) %all-gather.12.cloned.1.call-update) | async-done | bytes 12582928 | tf_op jit(solution)/shard_map/all_gather | solution.py:26
  197.7 1.5 convolution_multiply_fusion
  199.2 2.5 multiply_reduce_fusion
  201.8 0.1 fusion.44
  201.9 143.7 %all-gather.8.cloned.1.call-done = bf16[16384,512]{0,1:T(8,128)(2,1)} async-done(((bf16[512,512]{0,1:T(8,128)(2,1)}), bf16[16384,512]{0,1:T(8,128)(2,1)}) %all-gather.8.cloned.1.call-update) | async-done | bytes 16777232 | tf_op jit(solution)/shard_map/all_gather | solution.py:165
  345.7 17.5 %fusion = (f32[2,256]{1,0:T(2,128)S(1)}, f32[16384,256,2]{1,0,2:T(8,128)}) fusion(pred[256,16384]{0,1:T(8,128)(4,1)} %and_or_fusion, bf16[256,2,64]{2,0,1:T(8,128)(2,1)S(1)} %copy-done.8, bf16[256,2,64]{2,0,1:T(8,128)(2,1)S(1)} %copy-done.7, bf16[16384,512]{0,1:T(8,128)(2,1)} %all-gather.8.cloned.1.call-done, s32[]{:T(128)S(6)} %select_n.107), kind=kOutput, calls=%fused_computation.4 | convolution fusion | flops 2172911104 | bytes 42076164 | tf_op jit(solution)/shard_map/qhd,kd->hqk/dot_general | solution.py:177
  363.2 15.6 %fusion.1 = f32[2,256]{1,0:T(2,128)S(1)} fusion(f32[16384,256,2]{1,0,2:T(8,128)} %get-tuple-element.104, f32[2,256]{1,0:T(2,128)S(1)} %broadcast_maximum_fusion, pred[256,16384]{0,1:T(8,128)(4,1)} %and_or_fusion), kind=kLoop, calls=%fused_computation.5 | loop fusion | flops 41942528 | bytes 37752832 | tf_op jit(solution)/shard_map/reduce_sum | solution.py:182
  378.8 17.1 %fusion.27 = bf16[256,2,128]{0,2,1:T(8,128)(2,1)S(1)} fusion(f32[16384,256,2]{1,0,2:T(8,128)} %get-tuple-element.104, f32[2,256]{1,0:T(2,128)S(1)} %broadcast_maximum_fusion, pred[256,16384]{0,1:T(8,128)(4,1)} %and_or_fusion, bf16[16384,512]{0,1:T(8,128)(2,1)} %all-gather.8.cloned.1.call-done, s32[]{:T(128)S(6)} %add.229, f32[256,2]{0,1:T(2,128)S(1)} %bitcast.180), kind=kOutput, calls=%fused_computation.32 | convolution fusion | flops 2189557760 | bytes 42078212 | tf_op jit(solution)/shard_map/hqk,kd->hqd/dot_general | solution.py:183
  395.9 2.0 fusion.102
  397.9 2.7 convolution_add_fusion
  400.7 1.6 copy.64
  402.3 1.9 add_bitcast_fusion
  404.2 36.7 %reduce-scatter.2.cloned.1.call-done = f32[256,768]{1,0:T(8,128)} async-done(((f32[256,3072]{1,0:T(8,128)}), f32[256,768]{1,0:T(8,128)}) %reduce-scatter.2.cloned.1.call-update) | async-done | bytes 786448 | tf_op jit(solution)/shard_map/reduce_scatter | solution.py:194
  440.9 1.9 fusion.40
  (65 shorter events, 0.4 us)
Async XLA Ops:
  7.2 390.7 %copy-start = (bf16[384,3072]{1,0:T(8,128)(2,1)S(1)}, bf16[384,3072]{1,0:T(8,128)(2,1)}, u32[]{:S(2)}) copy-start(bf16[384,3072]{1,0:T(8,128)(2,1)} %param.36) | copy-start | bytes 7077892
  7.2 35.5 %all-gather.10.cloned.1.call-start = ((), (), s32[]{:S(2)}) async-start(), calls=%async_computation.3 | async-start | bytes 1966080 | tf_op jit(solution)/shard_map/all_gather | solution.py:96
  7.9 189.7 %all-gather.12.cloned.1.call-start = ((), (), s32[]{:S(2)}) async-start(), calls=%async_computation.4 | async-start | bytes 12976128 | tf_op jit(solution)/shard_map/all_gather | solution.py:26
  42.7 3.9 copy-start.18
  46.6 2.4 copy-start.1
  46.6 2.4 copy-start.10
  46.6 2.4 copy-start.17
  46.6 8.1 %copy-start.5 = (bf16[3072,128]{1,0:T(8,128)(2,1)S(1)}, bf16[3072,128]{1,0:T(8,128)(2,1)}, u32[]{:S(2)}) copy-start(bf16[3072,128]{1,0:T(8,128)(2,1)} %param.28) | copy-start | bytes 2359300
  48.1 21.8 %copy-start.12 = (bf16[1,3,384]{2,1,0:T(4,128)(2,1)S(1)}, bf16[1,3,384]{2,1,0:T(4,128)(2,1)}, u32[]{:S(2)}) copy-start(bf16[1,3,384]{2,1,0:T(4,128)(2,1)} %param.39) | copy-start | bytes 6916
  48.1 23.2 %copy-start.11 = (bf16[1,3,512]{2,1,0:T(4,128)(2,1)S(1)}, bf16[1,3,512]{2,1,0:T(4,128)(2,1)}, u32[]{:S(2)}) copy-start(bf16[1,3,512]{2,1,0:T(4,128)(2,1)} %param.40) | copy-start | bytes 9220
  51.6 20.1 %copy-start.13 = (f32[3]{0:T(128)}, f32[3]{0:T(128)S(1)}, u32[]{:S(2)}) copy-start(f32[3]{0:T(128)S(1)} %get-tuple-element.66) | copy-start | bytes 40
  51.6 18.3 %collective-permute-start = (bf16[3,384]{1,0:T(4,128)(2,1)S(1)}, bf16[3,384]{1,0:T(4,128)(2,1)S(1)}, u32[]{:S(2)}, u32[]{:S(2)}) collective-permute-start(bf16[3,384]{1,0:T(4,128)(2,1)S(1)} %slice_bitcast_fusion.1), channel_id=1, source_target_pairs={{0,8},{8,16},{16,24},{24,32},{32,40},{40,48},{48,56},{56,64},{64,7... | collective-permute-start | bytes 6920 | tf_op jit(solution)/shard_map/ppermute | solution.py:21
  66.0 7.7 %copy-start.9 = (bf16[1,256,128]{2,1,0:T(8,128)(2,1)S(1)}, bf16[1,256,128]{2,1,0:T(8,128)(2,1)}, u32[]{:S(2)}) copy-start(bf16[1,256,128]{2,1,0:T(8,128)(2,1)} %param.37) | copy-start | bytes 196612
  66.1 5.2 %collective-permute-start.1 = (bf16[3,512]{1,0:T(4,128)(2,1)S(1)}, bf16[3,512]{1,0:T(4,128)(2,1)S(1)}, u32[]{:S(2)}, u32[]{:S(2)}) collective-permute-start(bf16[3,512]{1,0:T(4,128)(2,1)S(1)} %slice.136), channel_id=1, source_target_pairs={{0,8},{8,16},{16,24},{24,32},{32,40},{40,48},{48,56},{56,64},{64,7... | collective-permute-start | bytes 9224 | tf_op jit(solution)/shard_map/ppermute | solution.py:21
  71.3 24.4 %copy-start.4 = (f32[256,384]{0,1:T(8,128)}, f32[256,384]{0,1:T(8,128)S(1)}, u32[]{:S(2)}) copy-start(f32[256,384]{0,1:T(8,128)S(1)} %copy.58) | copy-start | bytes 1179652
  71.4 25.2 %copy-start.16 = (bf16[384]{0:T(512)(128)(2,1)S(1)}, bf16[384]{0:T(512)(128)(2,1)}, u32[]{:S(2)}) copy-start(bf16[384]{0:T(512)(128)(2,1)} %param.35) | copy-start | bytes 2308
  73.0 272.6 %all-gather.8.cloned.1.call-start = ((), (), s32[]{:S(2)}) async-start(), calls=%async_computation.1 | async-start | bytes 17301504 | tf_op jit(solution)/shard_map/all_gather | solution.py:165
  85.9 9.8 %copy-start.6 = (bf16[256,128]{0,1:T(8,128)(2,1)}, bf16[256,128]{0,1:T(8,128)(2,1)S(1)}, u32[]{:S(2)}) copy-start(bf16[256,128]{0,1:T(8,128)(2,1)S(1)} %fusion.63) | copy-start | bytes 196612
  96.5 344.3 %reduce-scatter.2.cloned.1.call-start = ((), (), s32[]{:S(2)}) async-start(), calls=%async_computation.2 | async-start | bytes 3932160 | tf_op jit(solution)/shard_map/reduce_scatter | solution.py:194
  98.6 20.3 %copy-start.15 = (f32[3]{0:T(128)S(1)}, f32[3]{0:T(128)}, u32[]{:S(2)}) copy-start(f32[3]{0:T(128)} %get-tuple-element.67) | copy-start | bytes 40
  199.2 146.5 %copy-start.7 = (bf16[256,2,64]{2,0,1:T(8,128)(2,1)S(1)}, bf16[256,2,64]{2,0,1:T(8,128)(2,1)}, u32[]{:S(2)}) copy-start(bf16[256,2,64]{2,0,1:T(8,128)(2,1)} %get-tuple-element.86) | copy-start | bytes 196612
  199.2 146.5 %copy-start.8 = (bf16[256,2,64]{2,0,1:T(8,128)(2,1)S(1)}, bf16[256,2,64]{2,0,1:T(8,128)(2,1)}, u32[]{:S(2)}) copy-start(bf16[256,2,64]{2,0,1:T(8,128)(2,1)} %get-tuple-element.87) | copy-start | bytes 196612
  397.9 2.7 copy-start.14
  397.9 4.4 copy-start.2
  400.6 40.2 %copy-start.3 = (bf16[1,256,768]{2,1,0:T(8,128)(2,1)S(1)}, bf16[1,256,768]{2,1,0:T(8,128)(2,1)}, u32[]{:S(2)}) copy-start(bf16[1,256,768]{2,1,0:T(8,128)(2,1)} %param.22) | copy-start | bytes 1179652
Sparse Core Ops, SparseCore 0:
  9.8 32.8 all-gather.9
  73.2 124.4 all-gather.11
  200.1 145.5 all-gather.7
  400.8 40.0 reduce-scatter.1
where the time goes:
time: 452 us; the launch traced here: 449 us
  waiting for transfers between devices  252 us (56%)
  blocking collectives  65.9 us (15%)
  matrix products  53.8 us (12%)
  other arithmetic  50.4 us (11%)
  between operations  14.9 us (3%)
  starting transfers between devices  6.45 us (1%)
  local copies, waits for them, and re-layouts  5.89 us (1%)
    all_gather x1, waiting for transfers between devices, shards(): piece = lax.all_gather(local_rows, 'seq', axis=0, tiled=True)  144 us
    all_gather x1, waiting for transfers between devices, prefix(): gathered = jax.tree.map(lambda a: lax.all_gather(a, axis), part)  39.1 us
    all_gather x1, blocking collectives, prefix(): gathered = jax.tree.map(lambda a: lax.all_gather(a, axis), part)  37.4 us
    reduce_scatter x1, waiting for transfers between devices, shards(): summed = lax.psum_scatter(term, 'mp', scatter_dimension=1, tiled=True)  36.7 us
    all_gather x1, waiting for transfers between devices, shards(): whole = lax.all_gather(own_rows, 'mp', axis=1, tiled=True)  31.7 us
    dot_general x1, matrix products, shards(): jnp.einsum('qhd,kd->hqk', query, piece[:, :HD], preferred_element_type=jn...  17.5 us
    dot_general x1, matrix products, shards(): jnp.einsum('hqk,kd->hqd', weights.astype(jnp.bfloat16), piece[:, HD:2 * H...  17.1 us
    reduce_sum x1, other arithmetic, shards(): total = jnp.sum(weights, axis=-1)  15.6 us
  transfers between devices with their start and end apart: 6, of which 4 were waited for; matrix products, arithmetic and copies ran while one was open for 10% of the time, Pallas kernels for 0%

commit v1 on v0

--- a/solution.py
+++ b/solution.py
@@ -109,10 +109,15 @@
     roped = rotate(projected[:, None, :], positions)[:, 0, :]
     kv_block = jnp.where(mp_pos % 2 == 0, roped, projected).astype(jnp.bfloat16)
     bc_block = jnp.dot(normed, w_bc, preferred_element_type=jnp.float32).astype(jnp.bfloat16)
-    kv_all, bc_all, cache_all = (
-        lax.all_gather(kv_block, "mp", axis=1, tiled=True),
-        lax.all_gather(bc_block, "mp", axis=1, tiled=True),
-        lax.all_gather(cache[0], "mp", axis=1, tiled=True),
+    bc_all = lax.all_gather(bc_block, "mp", axis=1, tiled=True)
+    own_rows_kv = jnp.concatenate([cache[0], kv_block], axis=0)
+    mp_size = lax.axis_size("mp")
+    partner = lax.ppermute(own_rows_kv, "mp", [(i, i ^ 1) for i in range(mp_size)])
+    is_key_block = mp_pos % 2 == 0
+    group_rows = jnp.where(
+        is_key_block,
+        jnp.concatenate([own_rows_kv, partner], axis=1),
+        jnp.concatenate([partner, own_rows_kv], axis=1),
     )
     inner = jnp.einsum("td,dkc->tkc", normed, w_inner, preferred_element_type=jnp.float32).astype(
         jnp.bfloat16
@@ -140,31 +145,32 @@
     to_end = jnp.exp(cumulative[-1][None, :] - cumulative) * step_size
     own_state = jnp.einsum("sh,shp,sn->hpn", to_end, x_conv, b_mat, precision=high)
     block_decay = jnp.exp(cumulative[-1])
-    prior_decay, prior_state = prefix(
-        (block_decay, own_state),
-        "seq",
-        join_states,
-        (jnp.ones_like(block_decay), jnp.zeros_like(own_state)),
-    )
-    incoming = prior_state + prior_decay[:, None, None] * ssm_init[0]
+    scan_decay = block_decay
+    scan_state = jnp.where(first_block, block_decay[:, None, None] * ssm_init[0] + own_state, own_state)
+    distance = 1
+    while distance < lax.axis_size("seq"):
+        earlier_decay, earlier_state = shifted((scan_decay, scan_state), "seq", distance)
+        reach = seq_pos >= distance
+        scan_state = jnp.where(reach, scan_decay[:, None, None] * earlier_state + scan_state, scan_state)
+        scan_decay = jnp.where(reach, earlier_decay * scan_decay, scan_decay)
+        distance *= 2
+    incoming = jnp.where(first_block, ssm_init[0], shifted(scan_state, "seq", 1))
     carried = jnp.exp(cumulative)[:, :, None] * jnp.einsum(
         "tn,hpn->thp", c_mat, incoming, precision=high
     )
     mamba_y = inner_out + carried + d_skip[None, :, None] * x_conv
-    state_after = block_decay[:, None, None] * incoming + own_state
+    state_after = scan_state
     gated = mamba_y * jax.nn.silu(inner[:, 0].astype(jnp.float32).reshape(tokens, mamba_heads, HD))
     mixed = (
         rms_scale(gated).reshape(tokens, mamba_heads * HD) * mamba_gain.astype(jnp.float32)
     ).astype(jnp.bfloat16)
-    cache_rows = cache_all.shape[0]
+    cache_rows = cache.shape[1]
     shard_rows = cache_rows + tokens
-    local_rows = jnp.concatenate([cache_all, kv_all], axis=0)
     group = mp_pos * local_heads // (QH // KVH)
     query_index = seq_pos * tokens + jnp.arange(tokens, dtype=jnp.int32)
     scale = 1.0 / float(HD) ** 0.5
-    piece = lax.all_gather(local_rows, "seq", axis=0, tiled=True)
+    piece = lax.all_gather(group_rows, "seq", axis=0, tiled=True)
     top = jnp.full((local_heads, tokens), negative, jnp.float32)
-    piece = lax.dynamic_slice_in_dim(piece, group * 2 * HD, 2 * HD, 1)
     count = piece.shape[0]
     index = jnp.arange(count, dtype=jnp.int32)
     owner = index // shard_rows

time: 452 us -> 326 us (0.72)
  waiting for transfers between devices: 252 us -> 109 us
  starting transfers between devices: 6.45 us -> 66.4 us
  blocking collectives: 65.9 us -> 10.1 us
  other arithmetic: 50.4 us -> 60.3 us
    all_gather x2 -> x1, waiting for transfers between devices: 183 us -> 0.02 us  [shards(): piece = lax.all_gather(group_rows, 'seq', axis=0, tiled=True)]
    ppermute x2 -> x12, starting transfers between devices: 6.29 us -> 66 us  [shifted(): return lax.ppermute(block, axis, route)]
    all_gather x4 -> x1, blocking collectives: 65.9 us -> 10.1 us  [shards(): bc_all = lax.all_gather(bc_block, 'mp', axis=1, tiled=True)]
    reduce_scatter x1, waiting for transfers between devices: 36.7 us -> 56.5 us  [shards(): summed = lax.psum_scatter(term, 'mp', scatter_dimension=1, tiled=True)]
    ppermute x2 -> x12, waiting for transfers between devices: 0.01 us -> 15.1 us  [shifted(): return lax.ppermute(block, axis, route)]
    or x1, other arithmetic: 15.5 us -> 21.5 us  [shards(): slot_ok[None, :]]
    select_n x1 -> x10, other arithmetic: 0.61 us -> 6.22 us  [the longest x5 5.44 us: shards(): jnp.where(reach, scan_decay[:, None, None] * earlier_state + scan_state,...]
  transfers between devices with their start and end apart: 6 -> 16, of which waited for: 4 -> 10; matrix products, arithmetic and copies ran while one was open for 10% -> 19% of each run, Pallas kernels for 0% -> 0%
where the time goes in v1:
time: 326 us; the launch traced here: 325 us
  waiting for transfers between devices  109 us (33%)
  starting transfers between devices  66.4 us (20%)
  other arithmetic  60.3 us (18%)
  matrix products  55.2 us (17%)
  between operations  15.1 us (5%)
  blocking collectives  10.1 us (3%)
  local copies, waits for them, and re-layouts  9.6 us (3%)
    ppermute x12, starting transfers between devices, shifted(): return lax.ppermute(block, axis, route)  66 us
    reduce_scatter x1, waiting for transfers between devices, shards(): summed = lax.psum_scatter(term, 'mp', scatter_dimension=1, tiled=True)  56.5 us
    all_gather x1, waiting for transfers between devices, shards(): whole = lax.all_gather(own_rows, 'mp', axis=1, tiled=True)  32.3 us
    or x1, other arithmetic, shards(): slot_ok[None, :]  21.5 us
    dot_general x1, matrix products, shards(): jnp.einsum('qhd,kd->hqk', query, piece[:, :HD], preferred_element_type=jn...  17.3 us
    dot_general x1, matrix products, shards(): jnp.einsum('hqk,kd->hqd', weights.astype(jnp.bfloat16), piece[:, HD:2 * H...  17.3 us
    reduce_sum x1, other arithmetic, shards(): total = jnp.sum(weights, axis=-1)  15.6 us
    ppermute x12, waiting for transfers between devices, shifted(): return lax.ppermute(block, axis, route)  15.1 us
  transfers between devices with their start and end apart: 16, of which 10 were waited for; matrix products, arithmetic and copies ran while one was open for 19% of the time, Pallas kernels for 0%

profile of v1, /device:TPU:1, one launch (start us, length us, event | category | flops | bytes accessed | tf_op | source)
XLA Modules:
  0.0 325.4 jit_solution(4323313037297703430)
XLA Ops:
  7.2 0.7 all-gather.6.cloned.1.call-update
  8.7 0.7 convert_element_type.78
  9.4 0.9 copy.37
  10.4 32.3 %all-gather.6.cloned.1.call-done = bf16[1,256,3072]{2,1,0:T(8,128)(2,1)} async-done(((bf16[1,256,768]{2,1,0:T(8,128)(2,1)}), bf16[1,256,3072]{2,1,0:T(8,128)(2,1)}) %all-gather.6.cloned.1.call-update) | async-done | bytes 1572880 | tf_op jit(solution)/shard_map/all_gather | solution.py:96
  42.7 1.8 fusion.9
  44.5 1.9 fusion.11
  46.4 1.2 copy-done.1
  47.6 0.7 fusion.95
  48.9 4.2 %collective-permute-done = bf16[512,128]{0,1:T(8,128)(2,1)S(1)} collective-permute-done((bf16[512,128]{0,1:T(8,128)(2,1)S(1)}, bf16[512,128]{0,1:T(8,128)(2,1)S(1)}, u32[]{:S(2)}, u32[]{:S(2)}) %collective-permute-start) | collective-permute-done | bytes 131104 | tf_op jit(solution)/shard_map/ppermute | solution.py:115
  53.1 0.8 maximum_select_fusion
  54.0 0.6 iota_add_fusion
  54.6 0.6 slice_convert_fusion.4
  55.2 0.6 compare_and_fusion
  55.9 0.6 fusion.80
  56.5 1.9 fusion.83
  58.5 0.9 reduce-window.6
  59.8 4.3 %fusion.13 = bf16[256,2,384]{2,0,1:T(8,128)(2,1)S(1)} fusion(bf16[3072,2,384]{2,1,0:T(2,128)(2,1)} %param.25, bf16[256,3072]{1,0:T(8,128)(2,1)} %copy-done.1), kind=kOutput, calls=%fused_computation.20 | convolution fusion | flops 1208156160 | bytes 6684672 | tf_op jit(solution)/shard_map/td,dkc->tkc/dot_general | solution.py:122
  64.2 3.1 collective-permute-start.1
  67.5 0.7 exponential_multiply_fusion
  68.2 0.8 slice_convert_fusion
  69.0 0.6 convolution_convert_fusion
  69.6 10.1 %all_gather.11 = bf16[256,512]{1,0:T(8,128)(2,1)S(1)} all-gather(bf16[256,128]{1,0:T(8,128)(2,1)S(1)} %convolution_convert_fusion), channel_id=1, replica_groups=mesh['seq'=32,'mp'=4,'req'=2] {'mp'}, dimensions={1}, use_global_device_ids=true | all-gather | bytes 327680 | tf_op jit(solution)/shard_map/all_gather | solution.py:112
  80.2 3.0 collective-permute-start.2
  84.1 1.0 divide_multiply_fusion
  85.1 2.2 add_select_fusion.5
  87.3 4.4 %collective-permute-start.7 = (f32[3,128,256]{2,1,0:T(8,128)}, f32[3,128,256]{2,1,0:T(8,128)}, u32[]{:S(2)}, u32[]{:S(2)}) collective-permute-start(f32[3,128,256]{2,1,0:T(8,128)} %add_select_fusion.5), channel_id=1, source_target_pairs={{0,8},{8,16},{16,24},{24,32},{32,40},{40,48},{48,56},{56,64},{64,7... | collective-permute-start | bytes 1179656 | tf_op jit(solution)/shard_map/ppermute | solution.py:21
  91.7 21.5 %and_or_fusion = pred[256,16384]{0,1:T(8,128)(4,1)} fusion(s32[256]{0:T(256)} %iota_add_fusion, s32[16384]{0:T(1024)} %fusion.80, pred[16384]{0:T(1024)(128)(4,1)} %get-tuple-element.37, pred[16384]{0:T(1024)(128)(4,1)S(1)} %get-tuple-element.36), kind=kLoop, calls=%fused_computation.7 | loop fusion | flops 12582912 | bytes 4293632 | tf_op jit(solution)/shard_map/or | solution.py:181
  113.2 2.0 add_select_fusion.4
  115.2 4.4 %collective-permute-start.8 = (f32[3,128,256]{2,1,0:T(8,128)}, f32[3,128,256]{2,1,0:T(8,128)}, u32[]{:S(2)}, u32[]{:S(2)}) collective-permute-start(f32[3,128,256]{2,1,0:T(8,128)} %add_select_fusion.4), channel_id=1, source_target_pairs={{0,16},{8,24},{16,32},{24,40},{32,48},{40,56},{48,64},{56,72},{64,... | collective-permute-start | bytes 1179656 | tf_op jit(solution)/shard_map/ppermute | solution.py:21
  119.6 1.2 multiply_cosine_fusion
  120.8 0.7 iota_compare_fusion
  121.4 4.7 %collective-permute-start.3 = (f32[3]{0:T(128)S(1)}, f32[3]{0:T(128)S(1)}, u32[]{:S(2)}, u32[]{:S(2)}) collective-permute-start(f32[3]{0:T(128)S(1)} %copy-done.26), channel_id=1, source_target_pairs={{0,8},{8,16},{16,24},{24,32},{32,40},{40,48},{48,56},{56,64},{64,7... | collective-permute-start | bytes 44 | tf_op jit(solution)/shard_map/ppermute | solution.py:21
  126.2 2.2 collective-permute-done.3
  128.4 1.2 add_select_fusion.3
  129.6 11.3 %collective-permute-start.9 = (f32[3,128,256]{2,1,0:T(8,128)S(1)}, f32[3,128,256]{2,1,0:T(8,128)S(1)}, u32[]{:S(2)}, u32[]{:S(2)}) collective-permute-start(f32[3,128,256]{2,1,0:T(8,128)S(1)} %add_select_fusion.3), channel_id=1, source_target_pairs={{0,32},{8,40},{16,48},{24,56},{32,64},{40,72},{48,80},{56,88},{64,... | collective-permute-start | bytes 1179656 | tf_op jit(solution)/shard_map/ppermute | solution.py:21
  141.0 2.7 fusion.96
  143.6 1.3 collective-permute-start.4
  144.9 0.7 collective-permute-done.4
  145.7 6.9 %collective-permute-done.9 = f32[3,128,256]{2,1,0:T(8,128)S(1)} collective-permute-done((f32[3,128,256]{2,1,0:T(8,128)S(1)}, f32[3,128,256]{2,1,0:T(8,128)S(1)}, u32[]{:S(2)}, u32[]{:S(2)}) %collective-permute-start.9) | collective-permute-done | bytes 393248 | tf_op jit(solution)/shard_map/ppermute | solution.py:21
  152.6 0.9 add_select_fusion.2
  153.4 3.0 collective-permute-start.10
  156.5 0.7 fusion.94
  157.2 1.0 copy.52
  158.2 1.9 copy.46
  160.1 1.7 copy.51
  161.9 8.0 %collective-permute-start.5 = (f32[3]{0:T(128)S(1)}, f32[3]{0:T(128)S(1)}, u32[]{:S(2)}, u32[]{:S(2)}) collective-permute-start(f32[3]{0:T(128)S(1)} %broadcast_select_fusion.1), channel_id=1, source_target_pairs={{0,32},{8,40},{16,48},{24,56},{32,64},{40,72},{48,80},{56,88},{64,... | collective-permute-start | bytes 44 | tf_op jit(solution)/shard_map/ppermute | solution.py:21
  169.9 1.4 collective-permute-done.5
  171.3 1.2 add_select_fusion.1
  172.5 19.0 %collective-permute-start.11 = (f32[3,128,256]{2,1,0:T(8,128)S(1)}, f32[3,128,256]{2,1,0:T(8,128)S(1)}, u32[]{:S(2)}, u32[]{:S(2)}) collective-permute-start(f32[3,128,256]{2,1,0:T(8,128)S(1)} %add_select_fusion.1), channel_id=1, source_target_pairs={{0,128},{8,136},{16,144},{24,152},{32,160},{40,168},{48,176},{56,1... | collective-permute-start | bytes 1179656 | tf_op jit(solution)/shard_map/ppermute | solution.py:21
  191.6 1.8 subtract_convert_fusion
  193.4 1.4 collective-permute-start.6
  194.8 1.5 collective-permute-done.6
  196.4 2.4 collective-permute-start.12
  199.2 1.8 convolution_bitcast_fusion
  201.1 2.2 collective-permute-done.12
  203.3 1.3 multiply_reduce_fusion
  204.8 17.3 %fusion = (f32[2,256]{1,0:T(2,128)S(1)}, f32[16384,256,2]{1,0,2:T(8,128)}) fusion(pred[256,16384]{0,1:T(8,128)(4,1)} %and_or_fusion, bf16[256,2,64]{2,0,1:T(8,128)(2,1)S(1)} %copy-done.12, bf16[256,2,64]{2,0,1:T(8,128)(2,1)S(1)} %copy-done.11, bf16[16384,256]{0,1:T(8,128)(2,1)} %all-gather.4.cloned.1.call-done), kind=kOutput, calls=%fused_computation.2 | convolution fusion | flops 2172911104 | bytes 42076160 | tf_op jit(solution)/shard_map/qhd,kd->hqk/dot_general | solution.py:183
  222.1 15.6 %fusion.1 = f32[2,256]{1,0:T(2,128)S(1)} fusion(f32[16384,256,2]{1,0,2:T(8,128)} %get-tuple-element.31, f32[2,256]{1,0:T(2,128)S(1)} %broadcast_maximum_fusion, pred[256,16384]{0,1:T(8,128)(4,1)} %and_or_fusion), kind=kLoop, calls=%fused_computation.3 | loop fusion | flops 41942528 | bytes 37752832 | tf_op jit(solution)/shard_map/reduce_sum | solution.py:188
  237.7 17.3 %fusion.27 = bf16[256,2,128]{0,2,1:T(8,128)(2,1)S(1)} fusion(f32[16384,256,2]{1,0,2:T(8,128)} %get-tuple-element.31, f32[2,256]{1,0:T(2,128)S(1)} %broadcast_maximum_fusion, pred[256,16384]{0,1:T(8,128)(4,1)} %and_or_fusion, bf16[16384,256]{0,1:T(8,128)(2,1)} %all-gather.4.cloned.1.call-done, f32[256,2]{0,1:T(2,128)S(1)} %bitcast.167), kind=kOutput, calls=%fused_computation.30 | convolution fusion | flops 2189557760 | bytes 42078208 | tf_op jit(solution)/shard_map/hqk,kd->hqd/dot_general | solution.py:189
  255.0 2.0 fusion.97
  257.0 2.7 convolution_add_fusion
  259.7 0.7 copy.47
  260.5 56.5 %reduce-scatter.2.cloned.1.call-done = f32[256,768]{1,0:T(8,128)} async-done(((f32[256,3072]{1,0:T(8,128)}), f32[256,768]{1,0:T(8,128)}) %reduce-scatter.2.cloned.1.call-update) | async-done | bytes 786448 | tf_op jit(solution)/shard_map/reduce_scatter | solution.py:200
  317.0 1.9 fusion.40
  (113 shorter events, 3.6 us)
Async XLA Ops:
  7.2 249.8 %copy-start = (bf16[384,3072]{1,0:T(8,128)(2,1)S(1)}, bf16[384,3072]{1,0:T(8,128)(2,1)}, u32[]{:S(2)}) copy-start(bf16[384,3072]{1,0:T(8,128)(2,1)} %param.34) | copy-start | bytes 7077892
  7.2 40.5 %copy-start.6 = (bf16[3072,128]{1,0:T(8,128)(2,1)S(1)}, bf16[3072,128]{1,0:T(8,128)(2,1)}, u32[]{:S(2)}) copy-start(bf16[3072,128]{1,0:T(8,128)(2,1)} %param.23) | copy-start | bytes 2359300
  7.2 35.5 %all-gather.6.cloned.1.call-start = ((), (), s32[]{:S(2)}) async-start(), calls=%async_computation.3 | async-start | bytes 1966080 | tf_op jit(solution)/shard_map/all_gather | solution.py:96
  7.9 196.8 %all-gather.4.cloned.1.call-start = ((), (), s32[]{:S(2)}) async-start(), calls=%async_computation.1 | async-start | bytes 8650752 | tf_op jit(solution)/shard_map/all_gather | solution.py:172
  10.3 43.6 %copy-start.27 = (f32[64]{0:T(128)}, f32[64]{0:T(128)S(1)}, u32[]{:S(2)}) copy-start(f32[64]{0:T(128)S(1)} %multiply_power_fusion) | copy-start | bytes 772
  10.4 43.6 %copy-start.21 = (f32[256]{0:T(256)}, f32[256]{0:T(256)S(1)}, u32[]{:S(2)}) copy-start(f32[256]{0:T(256)S(1)} %add_convert_fusion.1) | copy-start | bytes 3076
  10.4 43.6 %copy-start.31 = (f32[3]{0:T(128)S(1)}, f32[3]{0:T(128)}, u32[]{:S(2)}) copy-start(f32[3]{0:T(128)} %param.29) | copy-start | bytes 40
  10.4 44.2 %copy-start.16 = (bf16[4,384]{1,0:T(4,128)(2,1)S(1)}, bf16[4,384]{1,0:T(4,128)(2,1)}, u32[]{:S(2)}) copy-start(bf16[4,384]{1,0:T(4,128)(2,1)} %param.31) | copy-start | bytes 9220
  10.4 44.2 %copy-start.15 = (bf16[4,512]{1,0:T(4,128)(2,1)S(1)}, bf16[4,512]{1,0:T(4,128)(2,1)}, u32[]{:S(2)}) copy-start(bf16[4,512]{1,0:T(4,128)(2,1)} %param.32) | copy-start | bytes 12292
  10.4 46.1 %copy-start.14 = (bf16[3072,3]{0,1:T(4,128)(2,1)S(1)}, bf16[3072,3]{0,1:T(4,128)(2,1)}, u32[]{:S(2)}) copy-start(bf16[3072,3]{0,1:T(4,128)(2,1)} %param.27) | copy-start | bytes 55300
  10.4 46.1 %copy-start.30 = (f32[3]{0:T(128)S(1)}, f32[3]{0:T(128)}, u32[]{:S(2)}) copy-start(f32[3]{0:T(128)} %param.28) | copy-start | bytes 40
  46.4 1.2 copy-start.1
  48.7 4.5 %copy-start.4 = (bf16[256,128]{0,1:T(8,128)(2,1)}, bf16[256,128]{0,1:T(8,128)(2,1)S(1)}, u32[]{:S(2)}) copy-start(bf16[256,128]{0,1:T(8,128)(2,1)S(1)} %fusion.62) | copy-start | bytes 196612
  48.7 4.4 %collective-permute-start = (bf16[512,128]{0,1:T(8,128)(2,1)S(1)}, bf16[512,128]{0,1:T(8,128)(2,1)S(1)}, u32[]{:S(2)}, u32[]{:S(2)}) collective-permute-start(bf16[512,128]{0,1:T(8,128)(2,1)S(1)} %pad_maximum_fusion), channel_id=1, source_target_pairs={{0,2},{2,0},{4,6},{6,4},{1,3},{3,1},{5,7},{7,5},{8,10},{10,8},{12,... | collective-permute-start | bytes 393224 | tf_op jit(solution)/shard_map/ppermute | solution.py:115
  54.0 263.0 %reduce-scatter.2.cloned.1.call-start = ((), (), s32[]{:S(2)}) async-start(), calls=%async_computation.2 | async-start | bytes 3932160 | tf_op jit(solution)/shard_map/reduce_scatter | solution.py:200
  59.8 7.5 %copy-start.17 = (f32[1,3,2,128]{3,1,2,0:T(4,128)}, f32[1,3,2,128]{3,1,2,0:T(4,128)S(1)}, u32[]{:S(2)}) copy-start(f32[1,3,2,128]{3,1,2,0:T(4,128)S(1)} %copy.63) | copy-start | bytes 9220
  59.8 9.2 %copy-start.2 = (bf16[256,3072]{1,0:T(8,128)(2,1)S(1)}, bf16[256,3072]{1,0:T(8,128)(2,1)}, u32[]{:S(2)}) copy-start(bf16[256,3072]{1,0:T(8,128)(2,1)} %copy-done.1) | copy-start | bytes 4718596
  59.8 9.2 %copy-start.7 = (bf16[3072,128]{1,0:T(8,128)(2,1)S(1)}, bf16[3072,128]{1,0:T(8,128)(2,1)}, u32[]{:S(2)}) copy-start(bf16[3072,128]{1,0:T(8,128)(2,1)} %param.26) | copy-start | bytes 2359300
  59.8 23.4 %copy-start.25 = (bf16[1,3,384]{2,1,0:T(4,128)(2,1)S(1)}, bf16[1,3,384]{2,1,0:T(4,128)(2,1)}, u32[]{:S(2)}) copy-start(bf16[1,3,384]{2,1,0:T(4,128)(2,1)} %param.37) | copy-start | bytes 6916
  64.2 19.7 %copy-start.23 = (bf16[1,3,512]{2,1,0:T(4,128)(2,1)S(1)}, bf16[1,3,512]{2,1,0:T(4,128)(2,1)}, u32[]{:S(2)}) copy-start(bf16[1,3,512]{2,1,0:T(4,128)(2,1)} %param.38) | copy-start | bytes 9220
  64.2 19.0 %collective-permute-start.1 = (bf16[3,384]{1,0:T(4,128)(2,1)S(1)}, bf16[3,384]{1,0:T(4,128)(2,1)S(1)}, u32[]{:S(2)}, u32[]{:S(2)}) collective-permute-start(bf16[3,384]{1,0:T(4,128)(2,1)S(1)} %slice_bitcast_fusion.11), channel_id=1, source_target_pairs={{0,8},{8,16},{16,24},{24,32},{32,40},{40,48},{48,56},{56,64},{64,7... | collective-permute-start | bytes 6920 | tf_op jit(solution)/shard_map/ppermute | solution.py:21
  67.5 15.8 %copy-start.19 = (f32[3]{0:T(128)}, f32[3]{0:T(128)S(1)}, u32[]{:S(2)}) copy-start(f32[3]{0:T(128)S(1)} %slice_reduce_fusion) | copy-start | bytes 40
  80.2 3.7 %collective-permute-start.2 = (bf16[3,512]{1,0:T(4,128)(2,1)S(1)}, bf16[3,512]{1,0:T(4,128)(2,1)S(1)}, u32[]{:S(2)}, u32[]{:S(2)}) collective-permute-start(bf16[3,512]{1,0:T(4,128)(2,1)S(1)} %slice.138), channel_id=1, source_target_pairs={{0,8},{8,16},{16,24},{24,32},{32,40},{40,48},{48,56},{56,64},{64,7... | collective-permute-start | bytes 9224 | tf_op jit(solution)/shard_map/ppermute | solution.py:21
  84.0 29.2 %copy-start.26 = (f32[3]{0:T(128)S(1)}, f32[3]{0:T(128)}, u32[]{:S(2)}) copy-start(f32[3]{0:T(128)} %exp.49) | copy-start | bytes 40
  84.0 35.5 %copy-start.22 = (f32[256]{0:T(256)S(1)}, f32[256]{0:T(256)}, u32[]{:S(2)}) copy-start(f32[256]{0:T(256)} %copy-done.21) | copy-start | bytes 3076
  84.0 35.5 %copy-start.28 = (f32[64]{0:T(128)S(1)}, f32[64]{0:T(128)}, u32[]{:S(2)}) copy-start(f32[64]{0:T(128)} %copy-done.27) | copy-start | bytes 772
  85.1 35.7 %copy-start.29 = (bf16[384]{0:T(512)(128)(2,1)S(1)}, bf16[384]{0:T(512)(128)(2,1)}, u32[]{:S(2)}) copy-start(bf16[384]{0:T(512)(128)(2,1)} %param.33) | copy-start | bytes 2308
  85.1 43.3 %copy-start.20 = (f32[3]{0:T(128)S(1)}, f32[3]{0:T(128)}, u32[]{:S(2)}) copy-start(f32[3]{0:T(128)} %copy-done.19) | copy-start | bytes 40
  87.3 25.8 %collective-permute-start.7 = (f32[3,128,256]{2,1,0:T(8,128)}, f32[3,128,256]{2,1,0:T(8,128)}, u32[]{:S(2)}, u32[]{:S(2)}) collective-permute-start(f32[3,128,256]{2,1,0:T(8,128)} %add_select_fusion.5), channel_id=1, source_target_pairs={{0,8},{8,16},{16,24},{24,32},{32,40},{40,48},{48,56},{56,64},{64,7... | collective-permute-start | bytes 1179656 | tf_op jit(solution)/shard_map/ppermute | solution.py:21
  115.2 13.2 %collective-permute-start.8 = (f32[3,128,256]{2,1,0:T(8,128)}, f32[3,128,256]{2,1,0:T(8,128)}, u32[]{:S(2)}, u32[]{:S(2)}) collective-permute-start(f32[3,128,256]{2,1,0:T(8,128)} %add_select_fusion.4), channel_id=1, source_target_pairs={{0,16},{8,24},{16,32},{24,40},{32,48},{40,56},{48,64},{56,72},{64,... | collective-permute-start | bytes 1179656 | tf_op jit(solution)/shard_map/ppermute | solution.py:21
  121.4 6.9 %collective-permute-start.3 = (f32[3]{0:T(128)S(1)}, f32[3]{0:T(128)S(1)}, u32[]{:S(2)}, u32[]{:S(2)}) collective-permute-start(f32[3]{0:T(128)S(1)} %copy-done.26), channel_id=1, source_target_pairs={{0,8},{8,16},{16,24},{24,32},{32,40},{40,48},{48,56},{56,64},{64,7... | collective-permute-start | bytes 44 | tf_op jit(solution)/shard_map/ppermute | solution.py:21
  129.6 22.9 %collective-permute-start.9 = (f32[3,128,256]{2,1,0:T(8,128)S(1)}, f32[3,128,256]{2,1,0:T(8,128)S(1)}, u32[]{:S(2)}, u32[]{:S(2)}) collective-permute-start(f32[3,128,256]{2,1,0:T(8,128)S(1)} %add_select_fusion.3), channel_id=1, source_target_pairs={{0,32},{8,40},{16,48},{24,56},{32,64},{40,72},{48,80},{56,88},{64,... | collective-permute-start | bytes 1179656 | tf_op jit(solution)/shard_map/ppermute | solution.py:21
  143.6 55.6 %copy-start.18 = (f32[1,3,2,128]{3,1,2,0:T(4,128)S(1)}, f32[1,3,2,128]{3,1,2,0:T(4,128)}, u32[]{:S(2)}) copy-start(f32[1,3,2,128]{3,1,2,0:T(4,128)} %copy-done.17) | copy-start | bytes 9220
  143.6 2.0 collective-permute-start.4
  153.4 49.8 %copy-start.24 = (f32[256,3]{0,1:T(4,128)S(1)}, f32[256,3]{0,1:T(4,128)}, u32[]{:S(2)}) copy-start(f32[256,3]{0,1:T(4,128)} %get-tuple-element.27) | copy-start | bytes 9220
  153.4 17.9 %collective-permute-start.10 = (f32[3,128,256]{2,1,0:T(8,128)}, f32[3,128,256]{2,1,0:T(8,128)}, u32[]{:S(2)}, u32[]{:S(2)}) collective-permute-start(f32[3,128,256]{2,1,0:T(8,128)} %add_select_fusion.2), channel_id=1, source_target_pairs={{0,64},{8,72},{16,80},{24,88},{32,96},{40,104},{48,112},{56,120},{... | collective-permute-start | bytes 1179656 | tf_op jit(solution)/shard_map/ppermute | solution.py:21
  161.9 37.3 %copy-start.13 = (pred[256,256]{1,0:T(8,128)(4,1)S(1)}, pred[256,256]{1,0:T(8,128)(4,1)}, u32[]{:S(2)}) copy-start(pred[256,256]{1,0:T(8,128)(4,1)} %iota_compare_fusion) | copy-start | bytes 196612
  161.9 41.4 %copy-start.8 = (f32[256,1,384]{0,2,1:T(8,128)S(1)}, f32[256,1,384]{0,2,1:T(8,128)}, u32[]{:S(2)}) copy-start(f32[256,1,384]{0,2,1:T(8,128)} %copy.46) | copy-start | bytes 1179652
  161.9 41.4 %copy-start.9 = (f32[1,3,128,256]{3,2,1,0:T(8,128)S(1)}, f32[1,3,128,256]{3,2,1,0:T(8,128)}, u32[]{:S(2)}) copy-start(f32[1,3,128,256]{3,2,1,0:T(8,128)} %param.39) | copy-start | bytes 1179652
  161.9 9.4 %collective-permute-start.5 = (f32[3]{0:T(128)S(1)}, f32[3]{0:T(128)S(1)}, u32[]{:S(2)}, u32[]{:S(2)}) collective-permute-start(f32[3]{0:T(128)S(1)} %broadcast_select_fusion.1), channel_id=1, source_target_pairs={{0,32},{8,40},{16,48},{24,56},{32,64},{40,72},{48,80},{56,88},{64,... | collective-permute-start | bytes 44 | tf_op jit(solution)/shard_map/ppermute | solution.py:21
  172.5 23.7 %collective-permute-start.11 = (f32[3,128,256]{2,1,0:T(8,128)S(1)}, f32[3,128,256]{2,1,0:T(8,128)S(1)}, u32[]{:S(2)}, u32[]{:S(2)}) collective-permute-start(f32[3,128,256]{2,1,0:T(8,128)S(1)} %add_select_fusion.1), channel_id=1, source_target_pairs={{0,128},{8,136},{16,144},{24,152},{32,160},{40,168},{48,176},{56,1... | collective-permute-start | bytes 1179656 | tf_op jit(solution)/shard_map/ppermute | solution.py:21
  193.4 11.4 %copy-start.11 = (bf16[256,2,64]{2,0,1:T(8,128)(2,1)S(1)}, bf16[256,2,64]{2,0,1:T(8,128)(2,1)}, u32[]{:S(2)}) copy-start(bf16[256,2,64]{2,0,1:T(8,128)(2,1)} %get-tuple-element.13) | copy-start | bytes 196612
  193.4 11.4 %copy-start.12 = (bf16[256,2,64]{2,0,1:T(8,128)(2,1)S(1)}, bf16[256,2,64]{2,0,1:T(8,128)(2,1)}, u32[]{:S(2)}) copy-start(bf16[256,2,64]{2,0,1:T(8,128)(2,1)} %get-tuple-element.14) | copy-start | bytes 196612
  193.4 2.9 collective-permute-start.6
  196.4 6.9 %copy-start.10 = (f32[3,128,256]{2,1,0:T(8,128)}, f32[3,128,256]{2,1,0:T(8,128)S(1)}, u32[]{:S(2)}) copy-start(f32[3,128,256]{2,1,0:T(8,128)S(1)} %add_select_fusion) | copy-start | bytes 1179652
  196.4 6.9 %collective-permute-start.12 = (f32[3,128,256]{2,1,0:T(8,128)S(1)}, f32[3,128,256]{2,1,0:T(8,128)S(1)}, u32[]{:S(2)}, u32[]{:S(2)}) collective-permute-start(f32[3,128,256]{2,1,0:T(8,128)S(1)} %add_select_fusion), channel_id=1, source_target_pairs={{0,8},{8,16},{16,24},{24,32},{32,40},{40,48},{48,56},{56,64},{64,7... | collective-permute-start | bytes 1179656 | tf_op jit(solution)/shard_map/ppermute | solution.py:21
  257.0 2.7 copy-start.5
  257.0 60.0 %copy-start.3 = (bf16[1,256,768]{2,1,0:T(8,128)(2,1)S(1)}, bf16[1,256,768]{2,1,0:T(8,128)(2,1)}, u32[]{:S(2)}) copy-start(bf16[1,256,768]{2,1,0:T(8,128)(2,1)} %param.20) | copy-start | bytes 1179652
Sparse Core Ops, SparseCore 0:
  9.8 32.8 all-gather.5
  54.1 117.6 all-gather.3
  259.8 57.0 reduce-scatter.1

commit v2 on v1

--- a/solution.py
+++ b/solution.py
@@ -145,21 +145,24 @@
     to_end = jnp.exp(cumulative[-1][None, :] - cumulative) * step_size
     own_state = jnp.einsum("sh,shp,sn->hpn", to_end, x_conv, b_mat, precision=high)
     block_decay = jnp.exp(cumulative[-1])
-    scan_decay = block_decay
-    scan_state = jnp.where(first_block, block_decay[:, None, None] * ssm_init[0] + own_state, own_state)
-    distance = 1
-    while distance < lax.axis_size("seq"):
-        earlier_decay, earlier_state = shifted((scan_decay, scan_state), "seq", distance)
-        reach = seq_pos >= distance
-        scan_state = jnp.where(reach, scan_decay[:, None, None] * earlier_state + scan_state, scan_state)
-        scan_decay = jnp.where(reach, earlier_decay * scan_decay, scan_decay)
-        distance *= 2
-    incoming = jnp.where(first_block, ssm_init[0], shifted(scan_state, "seq", 1))
+    seq_size = lax.axis_size("seq")
+    rows = HD // seq_size
+    pieces = jnp.transpose(own_state.reshape(mamba_heads, seq_size, rows, NS), (1, 0, 2, 3))
+    decays = jnp.broadcast_to(block_decay[None, :, None, None], (seq_size, mamba_heads, 1, NS))
+    columns = lax.all_to_all(jnp.concatenate([pieces, decays], axis=2), "seq", 0, 0, tiled=True)
+    carry = lax.dynamic_slice_in_dim(ssm_init[0], seq_pos * rows, rows, 1)
+    entering = []
+    for source in range(seq_size):
+        entering.append(carry)
+        part = columns[source]
+        carry = part[:, rows:, :] * carry + part[:, :rows, :]
+    entering = lax.all_to_all(jnp.stack(entering, axis=0), "seq", 0, 0, tiled=True)
+    incoming = jnp.transpose(entering, (1, 0, 2, 3)).reshape(mamba_heads, HD, NS)
     carried = jnp.exp(cumulative)[:, :, None] * jnp.einsum(
         "tn,hpn->thp", c_mat, incoming, precision=high
     )
     mamba_y = inner_out + carried + d_skip[None, :, None] * x_conv
-    state_after = scan_state
+    state_after = block_decay[:, None, None] * incoming + own_state
     gated = mamba_y * jax.nn.silu(inner[:, 0].astype(jnp.float32).reshape(tokens, mamba_heads, HD))
     mixed = (
         rms_scale(gated).reshape(tokens, mamba_heads * HD) * mamba_gain.astype(jnp.float32)

time: 326 us -> 308 us (0.945)
  starting transfers between devices: 66.4 us -> 25.2 us
  other arithmetic: 60.3 us -> 75.5 us
  local copies, waits for them, and re-layouts: 9.6 us -> 19.5 us
    ppermute x12 -> x2, starting transfers between devices: 66 us -> 6.2 us  [shifted(): return lax.ppermute(block, axis, route)]
    all_gather x1, waiting for transfers between devices: 0.02 us -> 40.1 us  [shards(): piece = lax.all_gather(group_rows, 'seq', axis=0, tiled=True)]
    all_to_all x0 -> x2, starting transfers between devices: none -> 18.6 us  [the longest x1 9.28 us: shards(): lax.all_to_all(jnp.stack(entering, axis=0), 'seq', 0, 0, tiled=True)]
    unnamed x1 -> x31, other arithmetic: 0.07 us -> 18.3 us
    reduce_scatter x1, waiting for transfers between devices: 56.5 us -> 40 us  [shards(): summed = lax.psum_scatter(term, 'mp', scatter_dimension=1, tiled=True)]
    ppermute x12 -> x2, waiting for transfers between devices: 15.1 us -> 0.01 us  [shifted(): return lax.ppermute(block, axis, route)]
    or x1, other arithmetic: 21.5 us -> 15.6 us  [shards(): slot_ok[None, :]]
    all_gather x1, waiting for transfers between devices: 32.3 us -> 27 us  [shards(): whole = lax.all_gather(own_rows, 'mp', axis=1, tiled=True)]
  transfers between devices with their start and end apart: 16 -> 8, of which waited for: 10 -> 4; matrix products, arithmetic and copies ran while one was open for 19% -> 25% of each run, Pallas kernels for 0% -> 0%
where the time goes in v2:
time: 308 us; the launch traced here: 306 us
  waiting for transfers between devices  108 us (35%)
  other arithmetic  75.5 us (25%)
  matrix products  53 us (17%)
  starting transfers between devices  25.2 us (8%)
  local copies, waits for them, and re-layouts  19.5 us (6%)
  between operations  15.1 us (5%)
  blocking collectives  9.69 us (3%)
    all_gather x1, waiting for transfers between devices, shards(): piece = lax.all_gather(group_rows, 'seq', axis=0, tiled=True)  40.1 us
    reduce_scatter x1, waiting for transfers between devices, shards(): summed = lax.psum_scatter(term, 'mp', scatter_dimension=1, tiled=True)  40 us
    all_gather x1, waiting for transfers between devices, shards(): whole = lax.all_gather(own_rows, 'mp', axis=1, tiled=True)  27 us
    unnamed x31, other arithmetic  18.3 us
    dot_general x1, matrix products, shards(): jnp.einsum('hqk,kd->hqd', weights.astype(jnp.bfloat16), piece[:, HD:2 * H...  17.2 us
    reduce_sum x1, other arithmetic, shards(): total = jnp.sum(weights, axis=-1)  15.7 us
    dot_general x1, matrix products, shards(): jnp.einsum('qhd,kd->hqk', query, piece[:, :HD], preferred_element_type=jn...  15.7 us
    or x1, other arithmetic, shards(): slot_ok[None, :]  15.6 us
  transfers between devices with their start and end apart: 8, of which 4 were waited for; matrix products, arithmetic and copies ran while one was open for 25% of the time, Pallas kernels for 0%

profile of v2, /device:TPU:1, one launch (start us, length us, event | category | flops | bytes accessed | tf_op | source)
XLA Modules:
  0.0 306.3 jit_solution(14901815859498077116)
XLA Ops:
  7.2 0.7 all-gather.6.cloned.1.call-update
  8.6 0.7 exp.48
  9.2 0.7 convert_element_type.78
  9.9 0.9 copy.66
  11.5 1.5 convert_reduce_fusion.3
  13.0 1.4 slice_convert_fusion.4
  14.4 0.6 compare_and_fusion
  15.1 0.6 fusion.80
  15.7 27.0 %all-gather.6.cloned.1.call-done = bf16[1,256,3072]{2,1,0:T(8,128)(2,1)} async-done(((bf16[1,256,768]{2,1,0:T(8,128)(2,1)}), bf16[1,256,3072]{2,1,0:T(8,128)(2,1)}) %all-gather.6.cloned.1.call-update) | async-done | bytes 1572880 | tf_op jit(solution)/shard_map/all_gather | solution.py:96
  42.7 1.9 fusion.9
  44.7 1.9 fusion.11
  46.6 1.4 fusion.13
  48.7 0.8 slice_convert_fusion
  50.0 0.9 reduce-window.6
  52.1 0.7 compare_select_fusion
  52.8 2.2 convolution_convert_fusion
  55.0 2.1 fusion.98
  57.5 0.7 pad_maximum_fusion.1
  58.3 3.1 %collective-permute-start.1 = (bf16[3,384]{1,0:T(4,128)(2,1)S(1)}, bf16[3,384]{1,0:T(4,128)(2,1)S(1)}, u32[]{:S(2)}, u32[]{:S(2)}) collective-permute-start(bf16[3,384]{1,0:T(4,128)(2,1)S(1)} %copy-done.18), channel_id=1, source_target_pairs={{0,8},{8,16},{16,24},{24,32},{32,40},{40,48},{48,56},{56,64},{64,7... | collective-permute-start | bytes 6920 | tf_op jit(solution)/shard_map/ppermute | solution.py:21
  61.4 9.7 %all_gather.11 = bf16[256,512]{1,0:T(8,128)(2,1)S(1)} all-gather(bf16[256,128]{1,0:T(8,128)(2,1)S(1)} %convolution_convert_fusion), channel_id=1, replica_groups=mesh['seq'=32,'mp'=4,'req'=2] {'mp'}, dimensions={1}, use_global_device_ids=true | all-gather | bytes 327680 | tf_op jit(solution)/shard_map/all_gather | solution.py:112
  71.1 3.1 %collective-permute-start.2 = (bf16[3,512]{1,0:T(4,128)(2,1)S(1)}, bf16[3,512]{1,0:T(4,128)(2,1)S(1)}, u32[]{:S(2)}, u32[]{:S(2)}) collective-permute-start(bf16[3,512]{1,0:T(4,128)(2,1)S(1)} %slice.510), channel_id=1, source_target_pairs={{0,8},{8,16},{16,24},{24,32},{32,40},{40,48},{48,56},{56,64},{64,7... | collective-permute-start | bytes 9224 | tf_op jit(solution)/shard_map/ppermute | solution.py:21
  74.2 0.7 bitcast_select_fusion.2
  75.0 0.9 divide_multiply_fusion.1
  75.9 0.9 copy.72
  76.8 0.7 bitcast_select_fusion.1
  78.1 1.5 fusion.45
  79.9 1.0 pad_maximum_fusion
  80.9 9.3 %all-to-all-start = ((f32[32,3,5,256]{3,1,2,0:T(4,128)}), f32[32,3,5,256]{3,1,2,0:T(4,128)}, u32[]{:S(2)}, u32[]{:S(2)}) async-start(f32[32,3,5,256]{3,1,2,0:T(4,128)} %pad_maximum_fusion), calls=%async_computation | async-start | bytes 1310720 | tf_op jit(solution)/shard_map/all_to_all | solution.py:152
  90.3 1.8 maximum_select_fusion
  92.1 15.6 %and_or_fusion = pred[256,16384]{0,1:T(8,128)(4,1)} fusion(s32[256]{0:T(256)S(1)} %copy-done.22, s32[16384]{0:T(1024)S(1)} %copy-done.6, pred[16384]{0:T(1024)(128)(4,1)S(1)} %copy-done.7, pred[16384]{0:T(1024)(128)(4,1)S(1)} %get-tuple-element.103), kind=kLoop, calls=%fused_computation.7 | loop fusion | flops 12582912 | bytes 4293632 | tf_op jit(solution)/shard_map/or | solution.py:184
  107.7 0.7 constant_dynamic-slice_fusion
  109.1 1.9 multiply_cosine_fusion
  111.1 1.0 slice_bitcast_fusion.11
  112.1 0.9 slice_bitcast_fusion.30
  116.3 0.6 constant_dynamic-update-slice_fusion.25
  118.7 0.6 constant_dynamic-update-slice_fusion.21
  119.9 0.6 constant_dynamic-update-slice_fusion.19
  124.2 0.6 constant_dynamic-update-slice_fusion.12
  126.0 0.6 constant_dynamic-update-slice_fusion.9
  128.4 0.6 constant_dynamic-update-slice_fusion.5
  131.4 0.6 constant_dynamic-update-slice_fusion
  132.1 1.9 copy.77
  134.0 9.3 %all-to-all-start.1 = ((f32[32,3,4,256]{3,2,1,0:T(4,128)}), f32[32,3,4,256]{3,2,1,0:T(4,128)}, u32[]{:S(2)}, u32[]{:S(2)}) async-start(f32[32,3,4,256]{3,2,1,0:T(4,128)} %copy.77), calls=%async_computation.1 | async-start | bytes 786432 | tf_op jit(solution)/shard_map/all_to_all | solution.py:159
  143.5 2.6 fusion.99
  146.1 0.7 fusion.97
  146.8 1.7 copy.86
  148.5 1.9 copy.79
  150.4 0.8 copy.85
  151.3 1.9 subtract_convert_fusion
  153.2 1.1 fusion.56
  154.8 1.8 copy.78
  156.6 1.9 reshape.294
  158.5 1.5 convolution_multiply_fusion
  160.0 2.5 multiply_reduce_fusion
  162.7 40.1 %all-gather.4.cloned.1.call-done = bf16[16384,256]{0,1:T(8,128)(2,1)} async-done(((bf16[512,256]{0,1:T(8,128)(2,1)}), bf16[16384,256]{0,1:T(8,128)(2,1)}) %all-gather.4.cloned.1.call-update) | async-done | bytes 8388624 | tf_op jit(solution)/shard_map/all_gather | solution.py:175
  202.9 15.7 %fusion = (f32[2,256]{1,0:T(2,128)S(1)}, f32[16384,256,2]{1,0,2:T(8,128)}) fusion(pred[256,16384]{0,1:T(8,128)(4,1)} %and_or_fusion, bf16[256,2,64]{2,0,1:T(8,128)(2,1)} %get-tuple-element.50, bf16[256,2,64]{2,0,1:T(8,128)(2,1)} %get-tuple-element.49, bf16[16384,256]{0,1:T(8,128)(2,1)} %all-gather.4.cloned.1.call-done), kind=kOutput, calls=%fused_computation.2 | convolution fusion | flops 2172911104 | bytes 42207232 | tf_op jit(solution)/shard_map/qhd,kd->hqk/dot_general | solution.py:186
  218.5 15.7 %fusion.1 = f32[2,256]{1,0:T(2,128)S(1)} fusion(f32[16384,256,2]{1,0,2:T(8,128)} %get-tuple-element.98, f32[2,256]{1,0:T(2,128)S(1)} %broadcast_maximum_fusion, pred[256,16384]{0,1:T(8,128)(4,1)} %and_or_fusion), kind=kLoop, calls=%fused_computation.3 | loop fusion | flops 41942528 | bytes 37752832 | tf_op jit(solution)/shard_map/reduce_sum | solution.py:191
  234.2 17.2 %fusion.27 = bf16[256,2,128]{0,2,1:T(8,128)(2,1)S(1)} fusion(f32[16384,256,2]{1,0,2:T(8,128)} %get-tuple-element.98, f32[2,256]{1,0:T(2,128)S(1)} %broadcast_maximum_fusion, pred[256,16384]{0,1:T(8,128)(4,1)} %and_or_fusion, bf16[16384,256]{0,1:T(8,128)(2,1)} %all-gather.4.cloned.1.call-done, f32[256,2]{0,1:T(2,128)S(1)} %bitcast.367), kind=kOutput, calls=%fused_computation.30 | convolution fusion | flops 2189557760 | bytes 42078208 | tf_op jit(solution)/shard_map/hqk,kd->hqd/dot_general | solution.py:192
  251.4 2.0 fusion.100
  253.5 2.7 convolution_add_fusion
  256.2 0.7 copy.80
  256.9 0.9 add_bitcast_fusion
  257.8 40.0 %reduce-scatter.2.cloned.1.call-done = f32[256,768]{1,0:T(8,128)} async-done(((f32[256,3072]{1,0:T(8,128)}), f32[256,768]{1,0:T(8,128)}) %reduce-scatter.2.cloned.1.call-update) | async-done | bytes 786448 | tf_op jit(solution)/shard_map/reduce_scatter | solution.py:203
  297.8 2.0 fusion.40
  (134 shorter events, 20.6 us)
Async XLA Ops:
  7.2 246.3 %copy-start = (bf16[384,3072]{1,0:T(8,128)(2,1)S(1)}, bf16[384,3072]{1,0:T(8,128)(2,1)}, u32[]{:S(2)}) copy-start(bf16[384,3072]{1,0:T(8,128)(2,1)} %param.34) | copy-start | bytes 7077892
  7.2 35.5 %all-gather.6.cloned.1.call-start = ((), (), s32[]{:S(2)}) async-start(), calls=%async_computation.5 | async-start | bytes 1966080 | tf_op jit(solution)/shard_map/all_gather | solution.py:96
  10.9 46.6 %copy-start.4 = (bf16[1,256,128]{1,2,0:T(8,128)(2,1)}, bf16[1,256,128]{1,2,0:T(8,128)(2,1)S(1)}, u32[]{:S(2)}) copy-start(bf16[1,256,128]{1,2,0:T(8,128)(2,1)S(1)} %copy.66) | copy-start | bytes 196612
  10.9 46.2 %copy-start.21 = (f32[64]{0:T(128)}, f32[64]{0:T(128)S(1)}, u32[]{:S(2)}) copy-start(f32[64]{0:T(128)S(1)} %multiply_power_fusion) | copy-start | bytes 772
  11.5 45.6 %copy-start.16 = (f32[256]{0:T(256)}, f32[256]{0:T(256)S(1)}, u32[]{:S(2)}) copy-start(f32[256]{0:T(256)S(1)} %add_convert_fusion.1) | copy-start | bytes 3076
  42.7 3.9 %copy-start.25 = (bf16[3072,2,384]{2,1,0:T(2,128)(2,1)S(1)}, bf16[3072,2,384]{2,1,0:T(2,128)(2,1)}, u32[]{:S(2)}) copy-start(bf16[3072,2,384]{2,1,0:T(2,128)(2,1)} %param.25) | copy-start | bytes 14155780
  46.6 2.9 copy-start.1
  46.6 2.9 copy-start.8
  46.6 2.9 copy-start.24
  48.1 6.9 %copy-start.3 = (bf16[3072,128]{1,0:T(8,128)(2,1)S(1)}, bf16[3072,128]{1,0:T(8,128)(2,1)}, u32[]{:S(2)}) copy-start(bf16[3072,128]{1,0:T(8,128)(2,1)} %param.23) | copy-start | bytes 2359300
  51.3 7.1 %copy-start.18 = (bf16[3,384]{1,0:T(4,128)(2,1)S(1)}, bf16[3,384]{1,0:T(4,128)(2,1)}, u32[]{:S(2)}) copy-start(bf16[3,384]{1,0:T(4,128)(2,1)} %slice_bitcast_fusion.73) | copy-start | bytes 6916
  51.3 0.8 copy-start.10
  57.1 20.6 %copy-start.12 = (f32[1,512]{1,0:T(1,128)S(1)}, f32[1,512]{1,0:T(1,128)}, u32[]{:S(2)}) copy-start(f32[1,512]{1,0:T(1,128)} %get-tuple-element.90) | copy-start | bytes 6148
  57.1 20.6 %copy-start.13 = (f32[1,512]{1,0:T(1,128)S(1)}, f32[1,512]{1,0:T(1,128)}, u32[]{:S(2)}) copy-start(f32[1,512]{1,0:T(1,128)} %get-tuple-element.91) | copy-start | bytes 6148
  57.1 20.6 %copy-start.14 = (f32[1,512]{1,0:T(1,128)S(1)}, f32[1,512]{1,0:T(1,128)}, u32[]{:S(2)}) copy-start(f32[1,512]{1,0:T(1,128)} %get-tuple-element.92) | copy-start | bytes 6148
  57.1 20.6 %copy-start.15 = (f32[1,512]{1,0:T(1,128)S(1)}, f32[1,512]{1,0:T(1,128)}, u32[]{:S(2)}) copy-start(f32[1,512]{1,0:T(1,128)} %get-tuple-element.93) | copy-start | bytes 6148
  58.2 32.1 %collective-permute-start = (bf16[512,128]{0,1:T(8,128)(2,1)}, bf16[512,128]{0,1:T(8,128)(2,1)}, u32[]{:S(2)}, u32[]{:S(2)}) collective-permute-start(bf16[512,128]{0,1:T(8,128)(2,1)} %pad_maximum_fusion.1), channel_id=1, source_target_pairs={{0,2},{2,0},{4,6},{6,4},{1,3},{3,1},{5,7},{7,5},{8,10},{10,8},{12,... | collective-permute-start | bytes 393224 | tf_op jit(solution)/shard_map/ppermute | solution.py:115
  58.3 15.9 %collective-permute-start.1 = (bf16[3,384]{1,0:T(4,128)(2,1)S(1)}, bf16[3,384]{1,0:T(4,128)(2,1)S(1)}, u32[]{:S(2)}, u32[]{:S(2)}) collective-permute-start(bf16[3,384]{1,0:T(4,128)(2,1)S(1)} %copy-done.18), channel_id=1, source_target_pairs={{0,8},{8,16},{16,24},{24,32},{32,40},{40,48},{48,56},{56,64},{64,7... | collective-permute-start | bytes 6920 | tf_op jit(solution)/shard_map/ppermute | solution.py:21
  71.1 5.7 %collective-permute-start.2 = (bf16[3,512]{1,0:T(4,128)(2,1)S(1)}, bf16[3,512]{1,0:T(4,128)(2,1)S(1)}, u32[]{:S(2)}, u32[]{:S(2)}) collective-permute-start(bf16[3,512]{1,0:T(4,128)(2,1)S(1)} %slice.510), channel_id=1, source_target_pairs={{0,8},{8,16},{16,24},{24,32},{32,40},{40,48},{48,56},{56,64},{64,7... | collective-permute-start | bytes 9224 | tf_op jit(solution)/shard_map/ppermute | solution.py:21
  75.0 4.9 %copy-start.19 = (f32[3]{0:T(128)S(1)}, f32[3]{0:T(128)}, u32[]{:S(2)}) copy-start(f32[3]{0:T(128)} %exp.54) | copy-start | bytes 40
  76.8 13.4 %copy-start.5 = (bf16[1,256,128]{1,2,0:T(8,128)(2,1)S(1)}, bf16[1,256,128]{1,2,0:T(8,128)(2,1)}, u32[]{:S(2)}) copy-start(bf16[1,256,128]{1,2,0:T(8,128)(2,1)} %copy-done.4) | copy-start | bytes 196612
  77.6 14.4 %copy-start.6 = (s32[16384]{0:T(1024)S(1)}, s32[16384]{0:T(1024)}, u32[]{:S(2)}) copy-start(s32[16384]{0:T(1024)} %fusion.80) | copy-start | bytes 196612
  77.7 14.4 %copy-start.7 = (pred[16384]{0:T(1024)(128)(4,1)S(1)}, pred[16384]{0:T(1024)(128)(4,1)}, u32[]{:S(2)}) copy-start(pred[16384]{0:T(1024)(128)(4,1)} %get-tuple-element.104) | copy-start | bytes 49156
  77.7 14.4 %copy-start.22 = (s32[256]{0:T(256)S(1)}, s32[256]{0:T(256)}, u32[]{:S(2)}) copy-start(s32[256]{0:T(256)} %iota_add_fusion) | copy-start | bytes 3076
  79.5 28.2 %copy-start.23 = (bf16[384]{0:T(512)(128)(2,1)S(1)}, bf16[384]{0:T(512)(128)(2,1)}, u32[]{:S(2)}) copy-start(bf16[384]{0:T(512)(128)(2,1)} %param.33) | copy-start | bytes 2308
  80.9 30.1 %all-to-all-start = ((f32[32,3,5,256]{3,1,2,0:T(4,128)}), f32[32,3,5,256]{3,1,2,0:T(4,128)}, u32[]{:S(2)}, u32[]{:S(2)}) async-start(f32[32,3,5,256]{3,1,2,0:T(4,128)} %pad_maximum_fusion), calls=%async_computation | async-start | bytes 1310720 | tf_op jit(solution)/shard_map/all_to_all | solution.py:152
  90.2 112.7 %all-gather.4.cloned.1.call-start = ((), (), s32[]{:S(2)}) async-start(), calls=%async_computation.3 | async-start | bytes 8650752 | tf_op jit(solution)/shard_map/all_gather | solution.py:175
  134.0 20.8 %all-to-all-start.1 = ((f32[32,3,4,256]{3,2,1,0:T(4,128)}), f32[32,3,4,256]{3,2,1,0:T(4,128)}, u32[]{:S(2)}, u32[]{:S(2)}) async-start(f32[32,3,4,256]{3,2,1,0:T(4,128)} %copy.77), calls=%async_computation.1 | async-start | bytes 786432 | tf_op jit(solution)/shard_map/all_to_all | solution.py:159
  143.3 15.2 %copy-start.9 = (f32[256,3]{0,1:T(4,128)S(1)}, f32[256,3]{0,1:T(4,128)}, u32[]{:S(2)}) copy-start(f32[256,3]{0,1:T(4,128)} %get-tuple-element.94) | copy-start | bytes 9220
  143.3 16.7 %copy-start.11 = (f32[1,3,2,128]{3,1,2,0:T(4,128)S(1)}, f32[1,3,2,128]{3,1,2,0:T(4,128)}, u32[]{:S(2)}) copy-start(f32[1,3,2,128]{3,1,2,0:T(4,128)} %copy-done.10) | copy-start | bytes 9220
  143.3 16.7 %copy-start.17 = (f32[256,3]{0,1:T(4,128)S(1)}, f32[256,3]{0,1:T(4,128)}, u32[]{:S(2)}) copy-start(f32[256,3]{0,1:T(4,128)} %get-tuple-element.88) | copy-start | bytes 9220
  143.3 154.5 %reduce-scatter.2.cloned.1.call-start = ((), (), s32[]{:S(2)}) async-start(), calls=%async_computation.4 | async-start | bytes 3932160 | tf_op jit(solution)/shard_map/reduce_scatter | solution.py:203
  253.4 3.5 %copy-start.2 = (f32[3,128,256]{2,1,0:T(8,128)S(1)}, f32[3,128,256]{2,1,0:T(8,128)}, u32[]{:S(2)}) copy-start(f32[3,128,256]{2,1,0:T(8,128)} %reshape.294) | copy-start | bytes 1179652
  253.5 3.5 %copy-start.20 = (f32[3]{0:T(128)S(1)}, f32[3]{0:T(128)}, u32[]{:S(2)}) copy-start(f32[3]{0:T(128)} %exp.54) | copy-start | bytes 40
Sparse Core Ops, SparseCore 0:
  9.8 32.8 all-gather.5
  93.5 109.3 all-gather.3
  256.3 41.4 reduce-scatter.1

commit v3 on v2

--- a/solution.py
+++ b/solution.py
@@ -110,15 +110,20 @@
     kv_block = jnp.where(mp_pos % 2 == 0, roped, projected).astype(jnp.bfloat16)
     bc_block = jnp.dot(normed, w_bc, preferred_element_type=jnp.float32).astype(jnp.bfloat16)
     bc_all = lax.all_gather(bc_block, "mp", axis=1, tiled=True)
-    own_rows_kv = jnp.concatenate([cache[0], kv_block], axis=0)
     mp_size = lax.axis_size("mp")
-    partner = lax.ppermute(own_rows_kv, "mp", [(i, i ^ 1) for i in range(mp_size)])
+    pairs_of = [(i, i ^ 1) for i in range(mp_size)]
     is_key_block = mp_pos % 2 == 0
-    group_rows = jnp.where(
-        is_key_block,
-        jnp.concatenate([own_rows_kv, partner], axis=1),
-        jnp.concatenate([partner, own_rows_kv], axis=1),
-    )
+
+    def paired(own):
+        other = lax.ppermute(own, "mp", pairs_of)
+        return jnp.where(
+            is_key_block,
+            jnp.concatenate([own, other], axis=1),
+            jnp.concatenate([other, own], axis=1),
+        )
+
+    cache_all = lax.all_gather(paired(cache[0]), "seq", axis=0, tiled=True)
+    new_all = lax.all_gather(paired(kv_block), "seq", axis=0, tiled=True)
     inner = jnp.einsum("td,dkc->tkc", normed, w_inner, preferred_element_type=jnp.float32).astype(
         jnp.bfloat16
     )
@@ -172,15 +177,13 @@
     group = mp_pos * local_heads // (QH // KVH)
     query_index = seq_pos * tokens + jnp.arange(tokens, dtype=jnp.int32)
     scale = 1.0 / float(HD) ** 0.5
-    piece = lax.all_gather(group_rows, "seq", axis=0, tiled=True)
+    piece = jnp.concatenate([cache_all, new_all], axis=0)
     top = jnp.full((local_heads, tokens), negative, jnp.float32)
-    count = piece.shape[0]
-    index = jnp.arange(count, dtype=jnp.int32)
-    owner = index // shard_rows
-    offset = index % shard_rows
-    in_cache = offset < cache_rows
-    slot_ok = in_cache & (owner * cache_rows + offset < length)
-    new_index = owner * tokens + offset - cache_rows
+    total_cache = cache_all.shape[0]
+    index = jnp.arange(piece.shape[0], dtype=jnp.int32)
+    in_cache = index < total_cache
+    slot_ok = in_cache & (index < length)
+    new_index = index - total_cache
     valid = slot_ok[None, :] | (~in_cache)[None, :] & (new_index[None, :] <= query_index[:, None])
     scores = (
         jnp.einsum("qhd,kd->hqk", query, piece[:, :HD], preferred_element_type=jnp.float32) * scale

time: 308 us -> 332 us (1.078)
  waiting for transfers between devices: 108 us -> 125 us
  local copies, waits for them, and re-layouts: 19.5 us -> 28.8 us
  other arithmetic: 75.5 us -> 69.1 us
    all_gather x1 -> x2, waiting for transfers between devices: 40.1 us -> 62 us  [the longest x1 62 us: shards(): new_all = lax.all_gather(paired(kv_block), 'seq', axis=0, tiled=True)]
    all_gather x1, waiting for transfers between devices: 27 us -> 8.26 us  [shards(): whole = lax.all_gather(own_rows, 'mp', axis=1, tiled=True)]
    all_to_all x1, waiting for transfers between devices: 0.01 us -> 8.75 us  [shards(): lax.all_to_all(jnp.concatenate([pieces, decays], axis=2), 'seq', 0, 0, ti...]
    unnamed x58 -> x37, local copies, waits for them, and re-layouts: 4.97 us -> 10.8 us
    concatenate x0 -> x1, local copies, waits for them, and re-layouts: none -> 4.57 us  [shards(): piece = jnp.concatenate([cache_all, new_all], axis=0)]
  transfers between devices with their start and end apart: 8 -> 10, of which waited for: 4 -> 6; matrix products, arithmetic and copies ran while one was open for 25% -> 27% of each run, Pallas kernels for 0% -> 0%
where the time goes in v3:
time: 332 us; the launch traced here: 331 us
  waiting for transfers between devices  125 us (38%)
  other arithmetic  69.1 us (21%)
  matrix products  55.4 us (17%)
  local copies, waits for them, and re-layouts  28.8 us (9%)
  starting transfers between devices  27.1 us (8%)
  between operations  14.9 us (4%)
  blocking collectives  9.8 us (3%)
    all_gather x1, waiting for transfers between devices, shards(): new_all = lax.all_gather(paired(kv_block), 'seq', axis=0, tiled=True)  62 us
    reduce_scatter x1, waiting for transfers between devices, shards(): summed = lax.psum_scatter(term, 'mp', scatter_dimension=1, tiled=True)  42.8 us
    unnamed x31, other arithmetic  18.3 us
    dot_general x1, matrix products, shards(): jnp.einsum('qhd,kd->hqk', query, piece[:, :HD], preferred_element_type=jn...  17.3 us
    dot_general x1, matrix products, shards(): jnp.einsum('hqk,kd->hqd', weights.astype(jnp.bfloat16), piece[:, HD:2 * H...  17.2 us
    reduce_sum x1, other arithmetic, shards(): total = jnp.sum(weights, axis=-1)  15.7 us
    or x1, other arithmetic, shards(): slot_ok[None, :]  15.6 us
    unnamed x37, local copies, waits for them, and re-layouts  10.8 us
  transfers between devices with their start and end apart: 10, of which 6 were waited for; matrix products, arithmetic and copies ran while one was open for 27% of the time, Pallas kernels for 0%

profile of v3, /device:TPU:1, one launch (start us, length us, event | category | flops | bytes accessed | tf_op | source)
XLA Modules:
  0.0 330.6 jit_solution(8155268910153722102)
XLA Ops:
  7.2 0.7 all-gather.9.cloned.1.call-update
  8.0 0.9 copy.66
  8.9 2.1 collective-permute-start
  11.7 0.7 exp.48
  12.3 0.7 convert_element_type.91
  13.0 0.7 convert_element_type.78
  13.7 0.8 constant_dynamic-slice_fusion
  14.5 0.9 convert_reduce_fusion.3
  15.4 0.8 slice_convert_fusion.4
  16.8 1.3 multiply_cosine_fusion
  18.1 0.7 maximum_select_fusion
  18.8 15.6 %and_or_fusion = pred[256,16384]{0,1:T(8,128)(4,1)} fusion(s32[256]{0:T(256)S(1)} %iota_add_fusion.1, s32[16384]{0:T(1024)S(1)} %iota_add_fusion, pred[16384]{0:T(1024)(128)(4,1)S(1)} %get-tuple-element.103, pred[16384]{0:T(1024)(128)(4,1)S(1)} %get-tuple-element.104), kind=kLoop, calls=%fused_computation.7 | loop fusion | flops 12582912 | bytes 4293632 | tf_op jit(solution)/shard_map/or | solution.py:187
  34.4 8.3 %all-gather.9.cloned.1.call-done = bf16[1,256,3072]{2,1,0:T(8,128)(2,1)} async-done(((bf16[1,256,768]{2,1,0:T(8,128)(2,1)}), bf16[1,256,3072]{2,1,0:T(8,128)(2,1)}) %all-gather.9.cloned.1.call-update) | async-done | bytes 1572880 | tf_op jit(solution)/shard_map/all_gather | solution.py:96
  42.7 1.8 fusion.9
  44.5 1.9 fusion.11
  46.4 1.1 copy-done.1
  48.1 0.9 reduce-window.6
  49.5 4.3 %fusion.13 = bf16[256,2,384]{2,0,1:T(8,128)(2,1)S(1)} fusion(bf16[3072,2,384]{2,1,0:T(2,128)(2,1)} %param.25, bf16[256,3072]{1,0:T(8,128)(2,1)} %copy-done.1), kind=kOutput, calls=%fused_computation.20 | convolution fusion | flops 1208156160 | bytes 6684672 | tf_op jit(solution)/shard_map/td,dkc->tkc/dot_general | solution.py:127
  53.9 3.1 collective-permute-start.2
  57.2 0.8 slice_convert_fusion
  58.6 9.8 %all_gather.15 = bf16[256,512]{1,0:T(8,128)(2,1)S(1)} all-gather(bf16[256,128]{1,0:T(8,128)(2,1)S(1)} %convolution_convert_fusion), channel_id=1, replica_groups=mesh['seq'=32,'mp'=4,'req'=2] {'mp'}, dimensions={1}, use_global_device_ids=true | all-gather | bytes 327680 | tf_op jit(solution)/shard_map/all_gather | solution.py:112
  68.4 2.7 collective-permute-start.3
  71.5 0.9 copy.72
  72.8 1.5 fusion.45
  74.7 1.0 pad_maximum_fusion
  75.7 10.7 %all-to-all-start = ((f32[32,3,5,256]{3,1,2,0:T(4,128)}), f32[32,3,5,256]{3,1,2,0:T(4,128)}, u32[]{:S(2)}, u32[]{:S(2)}) async-start(f32[32,3,5,256]{3,1,2,0:T(4,128)} %pad_maximum_fusion), calls=%async_computation | async-start | bytes 1310720 | tf_op jit(solution)/shard_map/all_to_all | solution.py:157
  86.5 2.3 fusion.90
  89.1 1.0 collective-permute-start.1
  90.2 0.7 iota_compare_fusion
  90.8 1.5 collective-permute-done.1
  92.3 0.7 maximum_select_fusion.1
  93.0 8.7 %all-to-all-done = f32[32,3,5,256]{3,1,2,0:T(4,128)} async-done(((f32[32,3,5,256]{3,1,2,0:T(4,128)}), f32[32,3,5,256]{3,1,2,0:T(4,128)}, u32[]{:S(2)}, u32[]{:S(2)}) %all-to-all-start) | async-done | bytes 491552 | tf_op jit(solution)/shard_map/all_to_all | solution.py:157
  101.8 0.9 slice_bitcast_fusion.30
  102.8 1.0 slice_bitcast_fusion.11
  103.9 0.6 constant_dynamic-update-slice_fusion.32
  105.7 0.6 constant_dynamic-update-slice_fusion.29
  107.0 0.6 constant_dynamic-update-slice_fusion.27
  109.4 0.6 constant_dynamic-update-slice_fusion.23
  111.8 0.6 constant_dynamic-update-slice_fusion.19
  122.8 1.9 copy.77
  124.7 7.0 %all-to-all-start.1 = ((f32[32,3,4,256]{3,2,1,0:T(4,128)}), f32[32,3,4,256]{3,2,1,0:T(4,128)}, u32[]{:S(2)}, u32[]{:S(2)}) async-start(f32[32,3,4,256]{3,2,1,0:T(4,128)} %copy.77), calls=%async_computation.1 | async-start | bytes 786432 | tf_op jit(solution)/shard_map/all_to_all | solution.py:164
  132.0 2.6 fusion.91
  134.6 0.7 fusion.89
  135.3 1.0 copy.86
  136.3 1.9 copy.79
  138.2 1.7 copy.85
  140.0 1.8 subtract_convert_fusion
  142.2 1.4 all-to-all-done.1
  143.6 1.8 copy.78
  145.3 1.9 reshape.277
  147.2 1.5 convolution_multiply_fusion
  148.7 2.5 multiply_reduce_fusion
  151.4 4.6 %constant_dynamic-update-slice_fusion.1 = bf16[16384,256]{0,1:T(8,128)(2,1)} fusion(bf16[8192,256]{0,1:T(8,128)(2,1)} %all-gather.5.cloned.1.call-done), kind=kLoop, calls=%fused_computation.102 | loop fusion | bytes 8388608
  156.0 62.0 %all-gather.7.cloned.1.call-done = bf16[8192,256]{0,1:T(8,128)(2,1)} async-done(((bf16[256,256]{0,1:T(8,128)(2,1)}), bf16[8192,256]{0,1:T(8,128)(2,1)}) %all-gather.7.cloned.1.call-update) | async-done | bytes 4194320 | tf_op jit(solution)/shard_map/all_gather | solution.py:126
  218.0 4.6 %constant_dynamic-update-slice_fusion = bf16[16384,256]{0,1:T(8,128)(2,1)} fusion(bf16[16384,256]{0,1:T(8,128)(2,1)} %constant_dynamic-update-slice_fusion.1, bf16[8192,256]{0,1:T(8,128)(2,1)} %all-gather.7.cloned.1.call-done), kind=kLoop, calls=%fused_computation.101 | loop fusion | bytes 8388608 | tf_op jit(solution)/shard_map/concatenate | solution.py:180
  222.6 17.3 %fusion = (f32[2,256]{1,0:T(2,128)S(1)}, f32[16384,256,2]{1,0,2:T(8,128)}) fusion(pred[256,16384]{0,1:T(8,128)(4,1)} %and_or_fusion, bf16[256,2,64]{2,0,1:T(8,128)(2,1)S(1)} %copy-done.8, bf16[256,2,64]{2,0,1:T(8,128)(2,1)S(1)} %copy-done.7, bf16[16384,256]{0,1:T(8,128)(2,1)} %constant_dynamic-update-slice_fusion), kind=kOutput, calls=%fused_computation.2 | convolution fusion | flops 2172911104 | bytes 42076160 | tf_op jit(solution)/shard_map/qhd,kd->hqk/dot_general | solution.py:189
  239.9 15.7 %fusion.1 = f32[2,256]{1,0:T(2,128)S(1)} fusion(f32[16384,256,2]{1,0,2:T(8,128)} %get-tuple-element.98, f32[2,256]{1,0:T(2,128)S(1)} %broadcast_maximum_fusion, pred[256,16384]{0,1:T(8,128)(4,1)} %and_or_fusion), kind=kLoop, calls=%fused_computation.3 | loop fusion | flops 41942528 | bytes 37752832 | tf_op jit(solution)/shard_map/reduce_sum | solution.py:194
  255.6 17.2 %fusion.27 = bf16[256,2,128]{0,2,1:T(8,128)(2,1)S(1)} fusion(f32[16384,256,2]{1,0,2:T(8,128)} %get-tuple-element.98, f32[2,256]{1,0:T(2,128)S(1)} %broadcast_maximum_fusion, pred[256,16384]{0,1:T(8,128)(4,1)} %and_or_fusion, bf16[16384,256]{0,1:T(8,128)(2,1)} %constant_dynamic-update-slice_fusion, f32[256,2]{0,1:T(2,128)S(1)} %bitcast.367), kind=kOutput, calls=%fused_computation.30 | convolution fusion | flops 2189557760 | bytes 42078208 | tf_op jit(solution)/shard_map/hqk,kd->hqd/dot_general | solution.py:195
  272.8 2.0 fusion.92
  274.9 2.7 convolution_add_fusion
  277.6 0.7 copy.80
  278.4 0.9 add_bitcast_fusion
  279.2 42.8 %reduce-scatter.2.cloned.1.call-done = f32[256,768]{1,0:T(8,128)} async-done(((f32[256,3072]{1,0:T(8,128)}), f32[256,768]{1,0:T(8,128)}) %reduce-scatter.2.cloned.1.call-update) | async-done | bytes 786448 | tf_op jit(solution)/shard_map/reduce_scatter | solution.py:206
  322.0 2.0 fusion.40
  (119 shorter events, 20.7 us)
Async XLA Ops:
  7.2 267.7 %copy-start = (bf16[384,3072]{1,0:T(8,128)(2,1)S(1)}, bf16[384,3072]{1,0:T(8,128)(2,1)}, u32[]{:S(2)}) copy-start(bf16[384,3072]{1,0:T(8,128)(2,1)} %param.34) | copy-start | bytes 7077892
  7.2 35.5 %all-gather.9.cloned.1.call-start = ((), (), s32[]{:S(2)}) async-start(), calls=%async_computation.6 | async-start | bytes 1966080 | tf_op jit(solution)/shard_map/all_gather | solution.py:96
  7.9 143.5 %all-gather.5.cloned.1.call-start = ((), (), s32[]{:S(2)}) async-start(), calls=%async_computation.3 | async-start | bytes 4325376 | tf_op jit(solution)/shard_map/all_gather | solution.py:125
  8.9 9.2 %collective-permute-start = (bf16[256,128]{0,1:T(8,128)(2,1)S(1)}, bf16[256,128]{0,1:T(8,128)(2,1)S(1)}, u32[]{:S(2)}, u32[]{:S(2)}) collective-permute-start(bf16[256,128]{0,1:T(8,128)(2,1)S(1)} %bitcast.357), channel_id=1, source_target_pairs={{0,2},{2,0},{4,6},{6,4},{1,3},{3,1},{5,7},{7,5},{8,10},{10,8},{12,... | collective-permute-start | bytes 196616 | tf_op jit(solution)/shard_map/ppermute | solution.py:118
  18.8 28.8 %copy-start.9 = (bf16[3072,3]{0,1:T(4,128)(2,1)S(1)}, bf16[3072,3]{0,1:T(4,128)(2,1)}, u32[]{:S(2)}) copy-start(bf16[3072,3]{0,1:T(4,128)(2,1)} %param.27) | copy-start | bytes 55300
  18.8 28.8 %copy-start.14 = (f32[3]{0:T(128)S(1)}, f32[3]{0:T(128)}, u32[]{:S(2)}) copy-start(f32[3]{0:T(128)} %param.28) | copy-start | bytes 40
  46.4 1.2 copy-start.1
  49.5 8.6 %copy-start.2 = (bf16[256,3072]{1,0:T(8,128)(2,1)S(1)}, bf16[256,3072]{1,0:T(8,128)(2,1)}, u32[]{:S(2)}) copy-start(bf16[256,3072]{1,0:T(8,128)(2,1)} %copy-done.1) | copy-start | bytes 4718596
  49.5 8.6 %copy-start.4 = (bf16[3072,128]{1,0:T(8,128)(2,1)S(1)}, bf16[3072,128]{1,0:T(8,128)(2,1)}, u32[]{:S(2)}) copy-start(bf16[3072,128]{1,0:T(8,128)(2,1)} %param.26) | copy-start | bytes 2359300
  49.5 21.7 %copy-start.11 = (bf16[1,3,384]{2,1,0:T(4,128)(2,1)S(1)}, bf16[1,3,384]{2,1,0:T(4,128)(2,1)}, u32[]{:S(2)}) copy-start(bf16[1,3,384]{2,1,0:T(4,128)(2,1)} %param.37) | copy-start | bytes 6916
  53.8 18.6 %copy-start.10 = (bf16[1,3,512]{2,1,0:T(4,128)(2,1)S(1)}, bf16[1,3,512]{2,1,0:T(4,128)(2,1)}, u32[]{:S(2)}) copy-start(bf16[1,3,512]{2,1,0:T(4,128)(2,1)} %param.38) | copy-start | bytes 9220
  53.9 17.3 %collective-permute-start.2 = (bf16[3,384]{1,0:T(4,128)(2,1)S(1)}, bf16[3,384]{1,0:T(4,128)(2,1)S(1)}, u32[]{:S(2)}, u32[]{:S(2)}) collective-permute-start(bf16[3,384]{1,0:T(4,128)(2,1)S(1)} %slice_bitcast_fusion.73), channel_id=1, source_target_pairs={{0,8},{8,16},{16,24},{24,32},{32,40},{40,48},{48,56},{56,64},{64,7... | collective-permute-start | bytes 6920 | tf_op jit(solution)/shard_map/ppermute | solution.py:21
  68.4 6.2 %copy-start.12 = (f32[3]{0:T(128)}, f32[3]{0:T(128)S(1)}, u32[]{:S(2)}) copy-start(f32[3]{0:T(128)S(1)} %exp.54) | copy-start | bytes 40
  68.4 4.0 %collective-permute-start.3 = (bf16[3,512]{1,0:T(4,128)(2,1)S(1)}, bf16[3,512]{1,0:T(4,128)(2,1)S(1)}, u32[]{:S(2)}, u32[]{:S(2)}) collective-permute-start(bf16[3,512]{1,0:T(4,128)(2,1)S(1)} %slice.510), channel_id=1, source_target_pairs={{0,8},{8,16},{16,24},{24,32},{32,40},{40,48},{48,56},{56,64},{64,7... | collective-permute-start | bytes 9224 | tf_op jit(solution)/shard_map/ppermute | solution.py:21
  75.7 26.1 %all-to-all-start = ((f32[32,3,5,256]{3,1,2,0:T(4,128)}), f32[32,3,5,256]{3,1,2,0:T(4,128)}, u32[]{:S(2)}, u32[]{:S(2)}) async-start(f32[32,3,5,256]{3,1,2,0:T(4,128)} %pad_maximum_fusion), calls=%async_computation | async-start | bytes 1310720 | tf_op jit(solution)/shard_map/all_to_all | solution.py:157
  86.4 131.6 %all-gather.7.cloned.1.call-start = ((), (), s32[]{:S(2)}) async-start(), calls=%async_computation.4 | async-start | bytes 4325376 | tf_op jit(solution)/shard_map/all_gather | solution.py:126
  89.1 3.2 copy-start.5
  89.1 3.2 collective-permute-start.1
  124.7 18.9 %all-to-all-start.1 = ((f32[32,3,4,256]{3,2,1,0:T(4,128)}), f32[32,3,4,256]{3,2,1,0:T(4,128)}, u32[]{:S(2)}, u32[]{:S(2)}) async-start(f32[32,3,4,256]{3,2,1,0:T(4,128)} %copy.77), calls=%async_computation.1 | async-start | bytes 786432 | tf_op jit(solution)/shard_map/all_to_all | solution.py:164
  131.7 190.3 %reduce-scatter.2.cloned.1.call-start = ((), (), s32[]{:S(2)}) async-start(), calls=%async_computation.5 | async-start | bytes 3932160 | tf_op jit(solution)/shard_map/reduce_scatter | solution.py:206
  156.0 66.6 %copy-start.7 = (bf16[256,2,64]{2,0,1:T(8,128)(2,1)S(1)}, bf16[256,2,64]{2,0,1:T(8,128)(2,1)}, u32[]{:S(2)}) copy-start(bf16[256,2,64]{2,0,1:T(8,128)(2,1)} %get-tuple-element.49) | copy-start | bytes 196612
  156.0 66.6 %copy-start.8 = (bf16[256,2,64]{2,0,1:T(8,128)(2,1)S(1)}, bf16[256,2,64]{2,0,1:T(8,128)(2,1)}, u32[]{:S(2)}) copy-start(bf16[256,2,64]{2,0,1:T(8,128)(2,1)} %get-tuple-element.50) | copy-start | bytes 196612
  274.9 2.8 copy-start.6
  274.9 3.5 %copy-start.3 = (f32[3,128,256]{2,1,0:T(8,128)S(1)}, f32[3,128,256]{2,1,0:T(8,128)}, u32[]{:S(2)}) copy-start(f32[3,128,256]{2,1,0:T(8,128)} %reshape.277) | copy-start | bytes 1179652
  274.9 3.5 %copy-start.13 = (f32[3]{0:T(128)S(1)}, f32[3]{0:T(128)}, u32[]{:S(2)}) copy-start(f32[3]{0:T(128)} %copy-done.12) | copy-start | bytes 40
Sparse Core Ops, SparseCore 0:
  9.8 32.8 all-gather.8
  45.2 86.1 all-gather.4
  133.8 84.1 all-gather.6
  277.7 44.2 reduce-scatter.1

commit v4 on v3

--- a/solution.py
+++ b/solution.py
@@ -2,6 +2,8 @@
 import jax.numpy as jnp
 from jax import lax
 from jax.sharding import PartitionSpec as P
+from jax.experimental import pallas as pl
+from jax.experimental.pallas import tpu as pltpu
 
 HD = 128
 QH = 8
@@ -32,6 +34,68 @@
         )
 
     return lax.fori_loop(0, place, one, state)
+
+
+def gather_rows(block, axis, tag):
+    count = lax.axis_size(axis)
+    rows = block.shape[0]
+    mesh_id = pl.DeviceIdType.MESH
+
+    def where_is(place):
+        return (place, lax.axis_index("mp"), lax.axis_index("req"))
+
+    def kernel(x_ref, out_ref, local_sem, send_sem, recv_sem):
+        me = lax.axis_index(axis)
+        barrier = pltpu.get_barrier_semaphore()
+
+        def greet(step, carry):
+            pl.semaphore_signal(
+                barrier, inc=1, device_id=where_is(lax.rem(me + step, count)), device_id_type=mesh_id
+            )
+            return carry
+
+        lax.fori_loop(1, count, greet, 0)
+        pl.semaphore_wait(barrier, count - 1)
+        own = pltpu.make_async_copy(x_ref, out_ref.at[pl.ds(me * rows, rows)], local_sem)
+        own.start()
+
+        def remote(step, source, target):
+            return pltpu.make_async_remote_copy(
+                src_ref=x_ref,
+                dst_ref=out_ref.at[pl.ds(source * rows, rows)],
+                send_sem=send_sem.at[step],
+                recv_sem=recv_sem.at[step],
+                device_id=where_is(target),
+                device_id_type=mesh_id,
+            )
+
+        def send(step, carry):
+            remote(step, me, lax.rem(me + step, count)).start()
+            return carry
+
+        lax.fori_loop(1, count, send, 0)
+
+        def finish(step, carry):
+            remote(step, me, lax.rem(me + step, count)).wait_send()
+            source = lax.rem(me + count - step, count)
+            remote(step, source, source).wait_recv()
+            return carry
+
+        lax.fori_loop(1, count, finish, 0)
+        own.wait()
+
+    return pl.pallas_call(
+        kernel,
+        out_shape=jax.ShapeDtypeStruct((count * rows,) + block.shape[1:], block.dtype),
+        in_specs=[pl.BlockSpec(memory_space=pl.ANY)],
+        out_specs=pl.BlockSpec(memory_space=pl.ANY),
+        scratch_shapes=[
+            pltpu.SemaphoreType.DMA(()),
+            pltpu.SemaphoreType.DMA((count,)),
+            pltpu.SemaphoreType.DMA((count,)),
+        ],
+        compiler_params=pltpu.CompilerParams(collective_id=tag, has_side_effects=True),
+    )(block)
 
 
 def rotate(values, positions):
@@ -122,8 +186,8 @@
             jnp.concatenate([other, own], axis=1),
         )
 
-    cache_all = lax.all_gather(paired(cache[0]), "seq", axis=0, tiled=True)
-    new_all = lax.all_gather(paired(kv_block), "seq", axis=0, tiled=True)
+    cache_all = gather_rows(paired(cache[0]), "seq", 0)
+    new_all = gather_rows(paired(kv_block), "seq", 1)
     inner = jnp.einsum("td,dkc->tkc", normed, w_inner, preferred_element_type=jnp.float32).astype(
         jnp.bfloat16
     )

time: 332 us -> 467 us (1.41)
  Pallas kernels: 0 us -> 203 us
  waiting for transfers between devices: 125 us -> 48.2 us
  other arithmetic: 69.1 us -> 78.6 us
  local copies, waits for them, and re-layouts: 28.8 us -> 23.4 us
    pallas_call x0 -> x2, Pallas kernels: none -> 203 us  [gather_rows(): pl.pallas_call(kernel, out_shape=jax.ShapeDtypeStruct((count * rows,) + b...]
    all_gather x2 -> x0, waiting for transfers between devices: 62 us -> none  [the longest x1 62 us: shards(): new_all = lax.all_gather(paired(kv_block), 'seq', axis=0, tiled=True)]
    all_to_all x1, waiting for transfers between devices: 8.75 us -> 0.01 us  [shards(): lax.all_to_all(jnp.concatenate([pieces, decays], axis=2), 'seq', 0, 0, ti...]
    unnamed x37 -> x70, local copies, waits for them, and re-layouts: 10.8 us -> 2.59 us
    all_gather x1, waiting for transfers between devices: 8.26 us -> 0.02 us  [shards(): whole = lax.all_gather(own_rows, 'mp', axis=1, tiled=True)]
  transfers between devices with their start and end apart: 10 -> 8, of which waited for: 6 -> 1; matrix products, arithmetic and copies ran while one was open for 27% -> 20% of each run, Pallas kernels for 0% -> 44%
where the time goes in v4:
time: 467 us; the launch traced here: 466 us
  Pallas kernels  203 us (43%)
  other arithmetic  78.6 us (17%)
  matrix products  55.4 us (12%)
  waiting for transfers between devices  48.2 us (10%)
  starting transfers between devices  31.1 us (7%)
  local copies, waits for them, and re-layouts  23.4 us (5%)
  between operations  15.4 us (3%)
  blocking collectives  10.2 us (2%)
    pallas_call x2, Pallas kernels, gather_rows(): pl.pallas_call(kernel, out_shape=jax.ShapeDtypeStruct((count * rows,) + b...  203 us
    reduce_scatter x1, waiting for transfers between devices, shards(): summed = lax.psum_scatter(term, 'mp', scatter_dimension=1, tiled=True)  47.4 us
    unnamed x31, other arithmetic  19.2 us
    dot_general x1, matrix products, shards(): jnp.einsum('qhd,kd->hqk', query, piece[:, :HD], preferred_element_type=jn...  17.3 us
    dot_general x1, matrix products, shards(): jnp.einsum('hqk,kd->hqd', weights.astype(jnp.bfloat16), piece[:, HD:2 * H...  17.1 us
    reduce_sum x1, other arithmetic, shards(): total = jnp.sum(weights, axis=-1)  16.2 us
    or x1, other arithmetic, shards(): slot_ok[None, :]  15.5 us
    all_to_all x1, starting transfers between devices, shards(): lax.all_to_all(jnp.concatenate([pieces, decays], axis=2), 'seq', 0, 0, ti...  12.7 us
  transfers between devices with their start and end apart: 8, of which 1 were waited for; matrix products, arithmetic and copies ran while one was open for 20% of the time, Pallas kernels for 44%

profile of v4, /device:TPU:1, one launch (start us, length us, event | category | flops | bytes accessed | tf_op | source)
XLA Modules:
  0.0 465.7 jit_solution(12777396550683759967)
XLA Ops:
  7.2 0.7 all-gather.3.cloned.1.call-update
  7.9 2.1 collective-permute-start
  10.1 0.6 iota_compare_fusion
  11.4 1.1 exp.48
  12.6 1.3 convert_element_type.91
  13.8 1.4 slice_convert_fusion.4
  15.3 0.7 convert_element_type.78
  16.0 0.8 constant_dynamic-slice_fusion
  17.3 1.2 multiply_cosine_fusion
  18.6 15.5 %and_or_fusion = pred[256,16384]{0,1:T(8,128)(4,1)} fusion(s32[256]{0:T(256)S(1)} %iota_add_fusion.1, s32[16384]{0:T(1024)S(1)} %iota_add_fusion, pred[16384]{0:T(1024)(128)(4,1)S(1)} %get-tuple-element.91, pred[16384]{0:T(1024)(128)(4,1)S(1)} %get-tuple-element.92), kind=kLoop, calls=%fused_computation.7 | loop fusion | flops 12582912 | bytes 4293632 | tf_op jit(solution)/shard_map/or | solution.py:251
  34.7 0.7 maximum_select_fusion.x_ref
  35.4 101.0 %shard_map.211 = bf16[8192,256]{1,0:T(8,128)(2,1)} custom-call(bf16[256,256]{1,0:T(8,128)(2,1)} %maximum_select_fusion.x_ref), custom_call_target="tpu_custom_call" | custom-call | tf_op jit(solution)/shard_map/pallas_call | solution.py:87
  136.5 1.8 fusion.15
  138.3 1.9 fusion.17
  140.3 4.3 fusion.19
  145.2 0.7 slice_convert_fusion
  146.0 1.1 fusion.90
  147.7 2.0 reduce-window.6
  149.6 0.7 slice.509
  150.3 1.3 copy.74
  151.6 1.3 reduce-window.9
  152.9 1.3 slice.390
  154.2 1.3 copy.75
  155.5 0.9 add_bitcast_fusion.1
  157.0 0.8 slice_reduce_fusion
  157.8 2.8 convolution_convert_fusion
  160.6 2.0 fusion.103
  163.2 0.7 fusion.80
  164.2 0.7 fusion.104
  164.9 0.7 fusion.102
  165.6 2.8 collective-permute-start.2
  168.6 1.0 copy.86
  169.6 1.4 compare_select_fusion
  171.0 1.7 subtract_convert_fusion
  172.8 10.2 %all_gather.7 = bf16[256,512]{1,0:T(8,128)(2,1)S(1)} all-gather(bf16[256,128]{1,0:T(8,128)(2,1)S(1)} %copy-done.10), channel_id=1, replica_groups=mesh['seq'=32,'mp'=4,'req'=2] {'mp'}, dimensions={1}, use_global_device_ids=true | all-gather | bytes 327680 | tf_op jit(solution)/shard_map/all_gather | solution.py:176
  182.9 1.2 exp.54
  184.2 3.9 collective-permute-start.3
  188.1 0.9 copy.80
  189.0 0.7 bitcast_select_fusion.2
  189.8 0.9 divide_multiply_fusion.1
  190.7 0.9 copy.73
  193.4 0.7 broadcast_in_dim.51
  194.1 1.0 pad_maximum_fusion.1
  195.2 12.7 %all-to-all-start = ((f32[32,3,5,256]{3,1,2,0:T(4,128)}), f32[32,3,5,256]{3,1,2,0:T(4,128)}, u32[]{:S(2)}, u32[]{:S(2)}) async-start(f32[32,3,5,256]{3,1,2,0:T(4,128)} %pad_maximum_fusion.1), calls=%async_computation | async-start | bytes 1310720 | tf_op jit(solution)/shard_map/all_to_all | solution.py:221
  207.8 1.6 maximum_select_fusion.1.x_ref
  209.5 102.4 %shard_map.212 = bf16[8192,256]{1,0:T(8,128)(2,1)} custom-call(bf16[256,256]{1,0:T(8,128)(2,1)} %maximum_select_fusion.1.x_ref), custom_call_target="tpu_custom_call" | custom-call | tf_op jit(solution)/shard_map/pallas_call | solution.py:87
  311.9 17.3 %fusion = (f32[2,256]{1,0:T(2,128)}, f32[16384,256,2]{1,0,2:T(8,128)}) fusion(pred[256,16384]{0,1:T(8,128)(4,1)} %and_or_fusion, bf16[256,2,64]{2,0,1:T(8,128)(2,1)} %get-tuple-element.38, bf16[256,2,64]{2,0,1:T(8,128)(2,1)} %get-tuple-element.37, bf16[8192,256]{1,0:T(8,128)(2,1)} %shard_map.211, bf16[8192,256]{1,0:T(8,128)(2,1)} %shard_map.212), kind=kOutput, calls=%fused_computation.2 | convolution fusion | flops 2181299712 | bytes 46270464 | tf_op jit(solution)/shard_map/qhd,kd->hqk/dot_general | solution.py:253
  329.3 0.7 broadcast_maximum_fusion
  330.0 16.2 %fusion.1 = f32[2,256]{1,0:T(2,128)} fusion(f32[16384,256,2]{1,0,2:T(8,128)} %get-tuple-element.86, f32[2,256]{1,0:T(2,128)S(1)} %broadcast_maximum_fusion, pred[256,16384]{0,1:T(8,128)(4,1)} %and_or_fusion), kind=kLoop, calls=%fused_computation.3 | loop fusion | flops 41942528 | bytes 37752832 | tf_op jit(solution)/shard_map/reduce_sum | solution.py:258
  346.1 1.0 slice_bitcast_fusion.1
  347.1 0.9 slice_bitcast_fusion.20
  365.9 0.6 constant_dynamic-update-slice_fusion.1
  367.1 1.9 copy.78
  369.1 9.0 %all-to-all-start.1 = ((f32[32,3,4,256]{3,2,1,0:T(4,128)}), f32[32,3,4,256]{3,2,1,0:T(4,128)}, u32[]{:S(2)}, u32[]{:S(2)}) async-start(f32[32,3,4,256]{3,2,1,0:T(4,128)} %copy.78), calls=%async_computation.1 | async-start | bytes 786432 | tf_op jit(solution)/shard_map/all_to_all | solution.py:228
  378.3 17.1 %fusion.37 = bf16[256,2,128]{0,2,1:T(8,128)(2,1)S(1)} fusion(bf16[8192,256]{1,0:T(8,128)(2,1)} %shard_map.212, bf16[8192,256]{1,0:T(8,128)(2,1)} %shard_map.211, f32[16384,256,2]{1,0,2:T(8,128)} %get-tuple-element.86, f32[2,256]{1,0:T(2,128)S(1)} %broadcast_maximum_fusion, pred[256,16384]{0,1:T(8,128)(4,1)} %and_or_fusion, f32[256,2]{0,1:T(2,128)} %bitcast.366), kind=kOutput, calls=%fused_computation.35 | convolution fusion | flops 2197946368 | bytes 46272512 | tf_op jit(solution)/shard_map/hqk,kd->hqd/dot_general | solution.py:259
  395.5 2.2 fusion.105
  397.7 1.8 copy.79
  399.5 1.9 reshape.277
  401.4 1.7 convolution_multiply_fusion
  403.1 2.5 multiply_reduce_fusion
  405.8 2.7 convolution_add_fusion
  408.6 0.9 add_bitcast_fusion
  409.4 47.4 %reduce-scatter.2.cloned.1.call-done = f32[256,768]{1,0:T(8,128)} async-done(((f32[256,3072]{1,0:T(8,128)}), f32[256,768]{1,0:T(8,128)}) %reduce-scatter.2.cloned.1.call-update) | async-done | bytes 786448 | tf_op jit(solution)/shard_map/reduce_scatter | solution.py:270
  456.8 2.0 fusion.52
  (147 shorter events, 24.7 us)
Async XLA Ops:
  7.2 398.6 %copy-start = (bf16[384,3072]{1,0:T(8,128)(2,1)S(1)}, bf16[384,3072]{1,0:T(8,128)(2,1)}, u32[]{:S(2)}) copy-start(bf16[384,3072]{1,0:T(8,128)(2,1)} %param.34) | copy-start | bytes 7077892
  7.2 27.5 %copy-start.11 = (bf16[1,256,128]{2,1,0:T(8,128)(2,1)S(1)}, bf16[1,256,128]{2,1,0:T(8,128)(2,1)}, u32[]{:S(2)}) copy-start(bf16[1,256,128]{2,1,0:T(8,128)(2,1)} %param.35) | copy-start | bytes 196612
  7.2 26.9 %copy-start.16 = (bf16[4,384]{1,0:T(4,128)(2,1)S(1)}, bf16[4,384]{1,0:T(4,128)(2,1)}, u32[]{:S(2)}) copy-start(bf16[4,384]{1,0:T(4,128)(2,1)} %param.31) | copy-start | bytes 9220
  7.2 129.3 %all-gather.3.cloned.1.call-start = ((), (), s32[]{:S(2)}) async-start(), calls=%async_computation.4 | async-start | bytes 1966080 | tf_op jit(solution)/shard_map/all_gather | solution.py:160
  7.9 26.8 %collective-permute-start = (bf16[256,128]{1,0:T(8,128)(2,1)}, bf16[256,128]{1,0:T(8,128)(2,1)S(1)}, u32[]{:S(2)}, u32[]{:S(2)}) collective-permute-start(bf16[256,128]{1,0:T(8,128)(2,1)} %bitcast.357), channel_id=1, source_target_pairs={{0,2},{2,0},{4,6},{6,4},{1,3},{3,1},{5,7},{7,5},{8,10},{10,8},{12,... | collective-permute-start | bytes 196616 | tf_op jit(solution)/shard_map/ppermute | solution.py:182
  10.1 126.4 %copy-start.29 = (f32[64]{0:T(128)}, f32[64]{0:T(128)S(1)}, u32[]{:S(2)}) copy-start(f32[64]{0:T(128)S(1)} %multiply_power_fusion) | copy-start | bytes 772
  11.4 125.1 %copy-start.24 = (f32[256]{0:T(256)}, f32[256]{0:T(256)S(1)}, u32[]{:S(2)}) copy-start(f32[256]{0:T(256)S(1)} %add_convert_fusion.1) | copy-start | bytes 3076
  140.2 5.7 %copy-start.1 = (bf16[256,3072]{1,0:T(8,128)(2,1)}, bf16[256,3072]{1,0:T(8,128)(2,1)S(1)}, u32[]{:S(2)}) copy-start(bf16[256,3072]{1,0:T(8,128)(2,1)S(1)} %fusion.17) | copy-start | bytes 4718596
  140.3 5.7 %copy-start.13 = (bf16[3072,3]{0,1:T(4,128)(2,1)S(1)}, bf16[3072,3]{0,1:T(4,128)(2,1)}, u32[]{:S(2)}) copy-start(bf16[3072,3]{0,1:T(4,128)(2,1)} %param.27) | copy-start | bytes 55300
  140.3 5.7 %copy-start.31 = (f32[3]{0:T(128)S(1)}, f32[3]{0:T(128)}, u32[]{:S(2)}) copy-start(f32[3]{0:T(128)} %param.28) | copy-start | bytes 40
  140.3 5.7 %copy-start.32 = (f32[3]{0:T(128)S(1)}, f32[3]{0:T(128)}, u32[]{:S(2)}) copy-start(f32[3]{0:T(128)} %exp.48) | copy-start | bytes 40
  144.6 15.9 %copy-start.8 = (bf16[3072,128]{1,0:T(8,128)(2,1)S(1)}, bf16[3072,128]{1,0:T(8,128)(2,1)}, u32[]{:S(2)}) copy-start(bf16[3072,128]{1,0:T(8,128)(2,1)} %param.23) | copy-start | bytes 2359300
  149.6 4.5 copy-start.12
  155.5 7.1 %copy-start.25 = (f32[256]{0:T(256)S(1)}, f32[256]{0:T(256)}, u32[]{:S(2)}) copy-start(f32[256]{0:T(256)} %copy-done.24) | copy-start | bytes 3076
  155.5 7.1 %copy-start.30 = (f32[64]{0:T(128)S(1)}, f32[64]{0:T(128)}, u32[]{:S(2)}) copy-start(f32[64]{0:T(128)} %copy-done.29) | copy-start | bytes 772
  155.5 8.7 %copy-start.2 = (bf16[256,3072]{1,0:T(8,128)(2,1)S(1)}, bf16[256,3072]{1,0:T(8,128)(2,1)}, u32[]{:S(2)}) copy-start(bf16[256,3072]{1,0:T(8,128)(2,1)} %copy-done.1) | copy-start | bytes 4718596
  155.5 8.7 %copy-start.6 = (bf16[3072,256]{1,0:T(8,128)(2,1)S(1)}, bf16[3072,256]{1,0:T(8,128)(2,1)}, u32[]{:S(2)}) copy-start(bf16[3072,256]{1,0:T(8,128)(2,1)} %param.22) | copy-start | bytes 4718596
  156.4 0.6 copy-start.17
  162.5 10.2 %copy-start.10 = (bf16[256,128]{1,0:T(8,128)(2,1)S(1)}, bf16[256,128]{1,0:T(8,128)(2,1)}, u32[]{:S(2)}) copy-start(bf16[256,128]{1,0:T(8,128)(2,1)} %convolution_convert_fusion) | copy-start | bytes 196612
  162.6 27.2 %copy-start.9 = (bf16[256,384]{1,0:T(8,128)(2,1)S(1)}, bf16[256,384]{1,0:T(8,128)(2,1)}, u32[]{:S(2)}) copy-start(bf16[256,384]{1,0:T(8,128)(2,1)} %get-tuple-element.71) | copy-start | bytes 589828
  163.9 43.9 %collective-permute-start.1 = (bf16[256,128]{1,0:T(8,128)(2,1)}, bf16[256,128]{1,0:T(8,128)(2,1)}, u32[]{:S(2)}, u32[]{:S(2)}) collective-permute-start(bf16[256,128]{1,0:T(8,128)(2,1)} %fusion.80), channel_id=1, source_target_pairs={{0,2},{2,0},{4,6},{6,4},{1,3},{3,1},{5,7},{7,5},{8,10},{10,8},{12,... | collective-permute-start | bytes 196616 | tf_op jit(solution)/shard_map/ppermute | solution.py:182
  165.6 23.4 %collective-permute-start.2 = (bf16[3,384]{1,0:T(4,128)(2,1)}, bf16[3,384]{1,0:T(4,128)(2,1)}, u32[]{:S(2)}, u32[]{:S(2)}) collective-permute-start(bf16[3,384]{1,0:T(4,128)(2,1)} %slice_bitcast_fusion.63), channel_id=1, source_target_pairs={{0,8},{8,16},{16,24},{24,32},{32,40},{40,48},{48,56},{56,64},{64,7... | collective-permute-start | bytes 6920 | tf_op jit(solution)/shard_map/ppermute | solution.py:23
  172.7 18.9 %copy-start.26 = (bf16[1,3,512]{2,1,0:T(4,128)(2,1)S(1)}, bf16[1,3,512]{2,1,0:T(4,128)(2,1)}, u32[]{:S(2)}) copy-start(bf16[1,3,512]{2,1,0:T(4,128)(2,1)} %param.38) | copy-start | bytes 9220
  172.7 19.0 %copy-start.20 = (f32[1,512]{1,0:T(1,128)S(1)}, f32[1,512]{1,0:T(1,128)}, u32[]{:S(2)}) copy-start(f32[1,512]{1,0:T(1,128)} %get-tuple-element.78) | copy-start | bytes 6148
  172.7 19.0 %copy-start.21 = (f32[1,512]{1,0:T(1,128)S(1)}, f32[1,512]{1,0:T(1,128)}, u32[]{:S(2)}) copy-start(f32[1,512]{1,0:T(1,128)} %get-tuple-element.79) | copy-start | bytes 6148
  172.7 19.0 %copy-start.22 = (f32[1,512]{1,0:T(1,128)S(1)}, f32[1,512]{1,0:T(1,128)}, u32[]{:S(2)}) copy-start(f32[1,512]{1,0:T(1,128)} %get-tuple-element.80) | copy-start | bytes 6148
  172.7 19.0 %copy-start.23 = (f32[1,512]{1,0:T(1,128)S(1)}, f32[1,512]{1,0:T(1,128)}, u32[]{:S(2)}) copy-start(f32[1,512]{1,0:T(1,128)} %get-tuple-element.81) | copy-start | bytes 6148
  184.2 7.5 %collective-permute-start.3 = (bf16[3,512]{1,0:T(4,128)(2,1)S(1)}, bf16[3,512]{1,0:T(4,128)(2,1)S(1)}, u32[]{:S(2)}, u32[]{:S(2)}) collective-permute-start(bf16[3,512]{1,0:T(4,128)(2,1)S(1)} %slice.510), channel_id=1, source_target_pairs={{0,8},{8,16},{16,24},{24,32},{32,40},{40,48},{48,56},{56,64},{64,7... | collective-permute-start | bytes 9224 | tf_op jit(solution)/shard_map/ppermute | solution.py:23
  188.1 4.4 copy-start.15
  191.6 1.0 copy-start.5
  195.2 151.0 %all-to-all-start = ((f32[32,3,5,256]{3,1,2,0:T(4,128)}), f32[32,3,5,256]{3,1,2,0:T(4,128)}, u32[]{:S(2)}, u32[]{:S(2)}) async-start(f32[32,3,5,256]{3,1,2,0:T(4,128)} %pad_maximum_fusion.1), calls=%async_computation | async-start | bytes 1310720 | tf_op jit(solution)/shard_map/all_to_all | solution.py:221
  369.1 28.7 %all-to-all-start.1 = ((f32[32,3,4,256]{3,2,1,0:T(4,128)}), f32[32,3,4,256]{3,2,1,0:T(4,128)}, u32[]{:S(2)}, u32[]{:S(2)}) async-start(f32[32,3,4,256]{3,2,1,0:T(4,128)} %copy.78), calls=%async_computation.1 | async-start | bytes 786432 | tf_op jit(solution)/shard_map/all_to_all | solution.py:228
  378.0 78.8 %reduce-scatter.2.cloned.1.call-start = ((), (), s32[]{:S(2)}) async-start(), calls=%async_computation.3 | async-start | bytes 3932160 | tf_op jit(solution)/shard_map/reduce_scatter | solution.py:270
  378.3 17.2 %copy-start.7 = (bf16[256,3072]{1,0:T(8,128)(2,1)S(1)}, bf16[256,3072]{1,0:T(8,128)(2,1)}, u32[]{:S(2)}) copy-start(bf16[256,3072]{1,0:T(8,128)(2,1)} %param.24) | copy-start | bytes 4718596
  395.4 5.9 %copy-start.14 = (f32[256,3]{0,1:T(4,128)S(1)}, f32[256,3]{0,1:T(4,128)}, u32[]{:S(2)}) copy-start(f32[256,3]{0,1:T(4,128)} %get-tuple-element.82) | copy-start | bytes 9220
  395.5 7.6 %copy-start.18 = (f32[1,3,2,128]{3,1,2,0:T(4,128)S(1)}, f32[1,3,2,128]{3,1,2,0:T(4,128)}, u32[]{:S(2)}) copy-start(f32[1,3,2,128]{3,1,2,0:T(4,128)} %copy-done.17) | copy-start | bytes 9220
  395.5 7.6 %copy-start.27 = (f32[256,3]{0,1:T(4,128)S(1)}, f32[256,3]{0,1:T(4,128)}, u32[]{:S(2)}) copy-start(f32[256,3]{0,1:T(4,128)} %get-tuple-element.76) | copy-start | bytes 9220
  397.7 7.9 %copy-start.19 = (f32[384]{0:T(512)S(1)}, f32[384]{0:T(512)}, u32[]{:S(2)}) copy-start(f32[384]{0:T(512)} %convert_element_type.91) | copy-start | bytes 4612
  401.4 4.4 copy-start.3
  405.8 2.7 copy-start.4
  405.8 2.7 copy-start.28
Sparse Core Ops, SparseCore 0:
  9.8 32.8 all-gather.2
  408.7 48.1 reduce-scatter.1

commit v5 on v2

--- a/solution.py
+++ b/solution.py
@@ -2,6 +2,8 @@
 import jax.numpy as jnp
 from jax import lax
 from jax.sharding import PartitionSpec as P
+from jax.experimental import pallas as pl
+from jax.experimental.pallas import tpu as pltpu
 
 HD = 128
 QH = 8
@@ -32,6 +34,60 @@
         )
 
     return lax.fori_loop(0, place, one, state)
+
+
+def attend(query_rows, query_rank, pieces, key_rank, block):
+    rows = query_rows.shape[0]
+    count = pieces.shape[0]
+    steps = count // block
+    scale = 1.0 / float(HD) ** 0.5
+
+    def kernel(qr_ref, q_ref, kr_ref, kv_ref, out_ref, top_ref, total_ref, acc_ref):
+        step = pl.program_id(0)
+
+        @pl.when(step == 0)
+        def _():
+            top_ref[...] = jnp.full(top_ref.shape, negative, jnp.float32)
+            total_ref[...] = jnp.zeros(total_ref.shape, jnp.float32)
+            acc_ref[...] = jnp.zeros(acc_ref.shape, jnp.float32)
+
+        scores = lax.dot_general(
+            q_ref[...], kv_ref[:, :HD], (((1,), (1,)), ((), ())), preferred_element_type=jnp.float32
+        ) * scale
+        valid = kr_ref[...] <= qr_ref[...]
+        masked = jnp.where(valid, scores, negative)
+        old = top_ref[...]
+        new = jnp.maximum(old, jnp.max(masked, axis=1, keepdims=True))
+        weights = jnp.where(valid, jnp.exp(masked - new), 0.0)
+        alpha = jnp.exp(old - new)
+        total_ref[...] = alpha * total_ref[...] + jnp.sum(weights, axis=1, keepdims=True)
+        acc_ref[...] = alpha * acc_ref[...] + jnp.dot(
+            weights.astype(jnp.bfloat16), kv_ref[:, HD:], preferred_element_type=jnp.float32
+        )
+        top_ref[...] = new
+
+        @pl.when(step == steps - 1)
+        def _():
+            out_ref[...] = (acc_ref[...] / total_ref[...]).astype(out_ref.dtype)
+
+    return pl.pallas_call(
+        kernel,
+        grid=(steps,),
+        in_specs=[
+            pl.BlockSpec((rows, 1), lambda i: (0, 0)),
+            pl.BlockSpec((rows, HD), lambda i: (0, 0)),
+            pl.BlockSpec((1, block), lambda i: (0, i)),
+            pl.BlockSpec((block, 2 * HD), lambda i: (i, 0)),
+        ],
+        out_specs=pl.BlockSpec((rows, HD), lambda i: (0, 0)),
+        out_shape=jax.ShapeDtypeStruct((rows, HD), jnp.bfloat16),
+        scratch_shapes=[
+            pltpu.VMEM((rows, 1), jnp.float32),
+            pltpu.VMEM((rows, 1), jnp.float32),
+            pltpu.VMEM((rows, HD), jnp.float32),
+        ],
+        compiler_params=pltpu.CompilerParams(vmem_limit_bytes=48 * 1024 * 1024),
+    )(query_rank, query_rows, key_rank, pieces)
 
 
 def rotate(values, positions):
@@ -173,7 +229,6 @@
     query_index = seq_pos * tokens + jnp.arange(tokens, dtype=jnp.int32)
     scale = 1.0 / float(HD) ** 0.5
     piece = lax.all_gather(group_rows, "seq", axis=0, tiled=True)
-    top = jnp.full((local_heads, tokens), negative, jnp.float32)
     count = piece.shape[0]
     index = jnp.arange(count, dtype=jnp.int32)
     owner = index // shard_rows
@@ -181,22 +236,14 @@
     in_cache = offset < cache_rows
     slot_ok = in_cache & (owner * cache_rows + offset < length)
     new_index = owner * tokens + offset - cache_rows
-    valid = slot_ok[None, :] | (~in_cache)[None, :] & (new_index[None, :] <= query_index[:, None])
-    scores = (
-        jnp.einsum("qhd,kd->hqk", query, piece[:, :HD], preferred_element_type=jnp.float32) * scale
-    )
-    masked = jnp.where(valid[None], scores, negative)
-    new_top = jnp.maximum(top, jnp.max(masked, axis=-1))
-    weights = jnp.where(valid[None], jnp.exp(masked - new_top[:, :, None]), 0.0)
-    total = jnp.sum(weights, axis=-1)
-    accum = jnp.einsum(
-        "hqk,kd->hqd",
-        weights.astype(jnp.bfloat16),
-        piece[:, HD : 2 * HD],
-        preferred_element_type=jnp.float32,
-    )
-    top, total, accum = (new_top, total, accum)
-    attended = jnp.transpose(accum / total[:, :, None], (1, 0, 2)).reshape(tokens, local_heads * HD)
+    never = jnp.iinfo(jnp.int32).max
+    key_rank = jnp.where(in_cache, jnp.where(slot_ok, -1, never), new_index)[None, :]
+    query_rank = jnp.tile(query_index, local_heads)[:, None]
+    query_rows = jnp.transpose(query, (1, 0, 2)).reshape(local_heads * tokens, HD)
+    attended = attend(query_rows, query_rank, piece, key_rank, 4 * shard_rows)
+    attended = jnp.transpose(attended.reshape(local_heads, tokens, HD), (1, 0, 2)).reshape(
+        tokens, local_heads * HD
+    )
     attended = attended.astype(jnp.bfloat16)
     term = jnp.dot(attended, w_attn_out, preferred_element_type=jnp.float32)
     term = term + jnp.dot(mixed, w_mamba_out, preferred_element_type=jnp.float32)

time: 308 us -> 244 us (0.79)
  other arithmetic: 75.5 us -> 21.8 us
  matrix products: 53 us -> 18.2 us
  Pallas kernels: 0 us -> 21.5 us
  waiting for transfers between devices: 108 us -> 115 us
  starting transfers between devices: 25.2 us -> 20.9 us
    dot_general x2 -> x0, matrix products: 32.9 us -> none  [the longest x1 17.2 us: shards(): jnp.einsum('hqk,kd->hqd', weights.astype(jnp.bfloat16), piece[:, HD:2 * H...]
    pallas_call x0 -> x1, Pallas kernels: none -> 21.5 us  [attend(): pl.pallas_call(kernel, grid=(steps,), in_specs=[pl.BlockSpec((rows, 1), l...]
    unnamed x31, other arithmetic: 18.3 us -> 0.62 us
    all_gather x1, waiting for transfers between devices: 40.1 us -> 23.8 us  [shards(): piece = lax.all_gather(group_rows, 'seq', axis=0, tiled=True)]
    reduce_sum x1 -> x0, other arithmetic: 15.7 us -> none  [shards(): total = jnp.sum(weights, axis=-1)]
    or x1 -> x0, other arithmetic: 15.6 us -> none  [shards(): slot_ok[None, :]]
    all_to_all x1, waiting for transfers between devices: 0.01 us -> 15.6 us  [shards(): lax.all_to_all(jnp.concatenate([pieces, decays], axis=2), 'seq', 0, 0, ti...]
    all_to_all x1, waiting for transfers between devices: 0.49 us -> 9.26 us  [shards(): lax.all_to_all(jnp.stack(entering, axis=0), 'seq', 0, 0, tiled=True)]
  transfers between devices with their start and end apart: 8 -> 8, of which waited for: 4 -> 5; matrix products, arithmetic and copies ran while one was open for 25% -> 19% of each run, Pallas kernels for 0% -> 0%
where the time goes in v5:
time: 244 us; the launch traced here: 243 us
  waiting for transfers between devices  115 us (47%)
  other arithmetic  21.8 us (9%)
  Pallas kernels  21.5 us (9%)
  starting transfers between devices  20.9 us (9%)
  local copies, waits for them, and re-layouts  20.4 us (8%)
  matrix products  18.2 us (7%)
  between operations  15.3 us (6%)
  blocking collectives  9.9 us (4%)
    reduce_scatter x1, waiting for transfers between devices, shards(): summed = lax.psum_scatter(term, 'mp', scatter_dimension=1, tiled=True)  37.8 us
    all_gather x1, waiting for transfers between devices, shards(): whole = lax.all_gather(own_rows, 'mp', axis=1, tiled=True)  28.2 us
    all_gather x1, waiting for transfers between devices, shards(): piece = lax.all_gather(group_rows, 'seq', axis=0, tiled=True)  23.8 us
    pallas_call x1, Pallas kernels, attend(): pl.pallas_call(kernel, grid=(steps,), in_specs=[pl.BlockSpec((rows, 1), l...  21.5 us
    all_to_all x1, waiting for transfers between devices, shards(): lax.all_to_all(jnp.concatenate([pieces, decays], axis=2), 'seq', 0, 0, ti...  15.6 us
    all_gather x1, blocking collectives, shards(): bc_all = lax.all_gather(bc_block, 'mp', axis=1, tiled=True)  9.9 us
    all_to_all x1, waiting for transfers between devices, shards(): lax.all_to_all(jnp.stack(entering, axis=0), 'seq', 0, 0, tiled=True)  9.26 us
    all_to_all x1, starting transfers between devices, shards(): lax.all_to_all(jnp.concatenate([pieces, decays], axis=2), 'seq', 0, 0, ti...  9.14 us
  transfers between devices with their start and end apart: 8, of which 5 were waited for; matrix products, arithmetic and copies ran while one was open for 19% of the time, Pallas kernels for 0%

profile of v5, /device:TPU:1, one launch (start us, length us, event | category | flops | bytes accessed | tf_op | source)
XLA Modules:
  0.0 243.2 jit_solution(8352188238532480388)
XLA Ops:
  7.2 0.7 all-gather.6.cloned.1.call-update
  8.2 0.7 convert_element_type.69
  9.5 0.7 exp.44
  10.2 1.3 convert_element_type.79
  11.5 1.4 convert_reduce_fusion.3
  12.9 1.4 slice_convert_fusion.4
  14.5 28.2 %all-gather.6.cloned.1.call-done = bf16[1,256,3072]{2,1,0:T(8,128)(2,1)} async-done(((bf16[1,256,768]{2,1,0:T(8,128)(2,1)}), bf16[1,256,3072]{2,1,0:T(8,128)(2,1)}) %all-gather.6.cloned.1.call-update) | async-done | bytes 1572880 | tf_op jit(solution)/shard_map/all_gather | solution.py:152
  42.7 1.9 fusion.2
  44.7 0.5 fusion.4
  45.2 0.6 copy-done.7
  45.8 0.6 fusion.68
  46.4 0.6 fusion.49
  47.1 0.6 copy-done.12
  47.7 0.7 pad_maximum_fusion.2
  48.5 1.4 fusion.6
  50.0 0.6 slice_bitcast_fusion.63
  50.6 3.7 %collective-permute-start.1 = (bf16[3,384]{1,0:T(4,128)(2,1)}, bf16[3,384]{1,0:T(4,128)(2,1)}, u32[]{:S(2)}, u32[]{:S(2)}) collective-permute-start(bf16[3,384]{1,0:T(4,128)(2,1)} %slice_bitcast_fusion.63), channel_id=1, source_target_pairs={{0,8},{8,16},{16,24},{24,32},{32,40},{40,48},{48,56},{56,64},{64,7... | collective-permute-start | bytes 6920 | tf_op jit(solution)/shard_map/ppermute | solution.py:23
  54.2 0.5 fusion.59
  54.8 0.9 reduce-window.6
  56.1 2.6 %convolution_convert_fusion = bf16[256,128]{1,0:T(8,128)(2,1)} fusion(bf16[256,3072]{1,0:T(8,128)(2,1)} %copy-done.1, bf16[3072,128]{1,0:T(8,128)(2,1)S(1)} %copy-done.8), kind=kOutput, calls=%fused_computation.15 | convolution fusion | flops 201359360 | bytes 2424832 | tf_op jit(solution)/shard_map/dot_general | solution.py:167
  58.8 0.2 slice_reduce_fusion
  59.0 1.8 maximum_select_fusion
  60.8 9.9 %all_gather.11 = bf16[256,512]{1,0:T(8,128)(2,1)S(1)} all-gather(bf16[256,128]{1,0:T(8,128)(2,1)} %convolution_convert_fusion), channel_id=1, replica_groups=mesh['seq'=32,'mp'=4,'req'=2] {'mp'}, dimensions={1}, use_global_device_ids=true | all-gather | bytes 327680 | tf_op jit(solution)/shard_map/all_gather | solution.py:168
  70.7 2.6 %collective-permute-start.2 = (bf16[3,512]{1,0:T(4,128)(2,1)S(1)}, bf16[3,512]{1,0:T(4,128)(2,1)S(1)}, u32[]{:S(2)}, u32[]{:S(2)}) collective-permute-start(bf16[3,512]{1,0:T(4,128)(2,1)S(1)} %slice.500), channel_id=1, source_target_pairs={{0,8},{8,16},{16,24},{24,32},{32,40},{40,48},{48,56},{56,64},{64,7... | collective-permute-start | bytes 9224 | tf_op jit(solution)/shard_map/ppermute | solution.py:23
  73.3 1.8 slice_convert_fusion
  75.1 0.6 compare_select_fusion.1
  75.9 0.2 divide_multiply_fusion.1
  76.2 0.9 copy.71
  77.2 0.3 divide_multiply_fusion
  77.6 0.5 copy-done.6
  78.1 0.5 fusion.29
  78.6 0.8 copy-done.3
  79.4 0.3 copy.80
  79.8 1.0 pad_maximum_fusion
  80.8 9.1 %all-to-all-start = ((f32[32,3,5,256]{3,1,2,0:T(4,128)}), f32[32,3,5,256]{3,1,2,0:T(4,128)}, u32[]{:S(2)}, u32[]{:S(2)}) async-start(f32[32,3,5,256]{3,1,2,0:T(4,128)} %pad_maximum_fusion), calls=%async_computation | async-start | bytes 1310720 | tf_op jit(solution)/shard_map/all_to_all | solution.py:208
  89.9 0.8 constant_dynamic-slice_fusion
  90.7 0.6 constant_dynamic-update-slice_fusion.31
  91.3 1.2 multiply_cosine_fusion.1
  92.5 2.6 %fusion.67 = f32[256,256]{0,1:T(8,128)S(1)} fusion(bf16[256,3072]{1,0:T(8,128)(2,1)} %copy-done.1, bf16[3072,256]{1,0:T(8,128)(2,1)} %param.22), kind=kOutput, calls=%fused_computation.258 | convolution fusion | flops 402653184 | bytes 3407872 | tf_op jit(solution)/shard_map/dot_general | solution.py:159
  95.2 15.6 %all-to-all-done = f32[32,3,5,256]{3,1,2,0:T(4,128)} async-done(((f32[32,3,5,256]{3,1,2,0:T(4,128)}), f32[32,3,5,256]{3,1,2,0:T(4,128)}, u32[]{:S(2)}, u32[]{:S(2)}) %all-to-all-start) | async-done | bytes 491552 | tf_op jit(solution)/shard_map/all_to_all | solution.py:208
  110.8 1.0 slice_bitcast_fusion.1
  111.8 0.9 slice_bitcast_fusion.20
  113.6 0.9 copy.76
  114.5 5.1 %all-to-all-start.1 = ((f32[32,3,4,256]{3,2,1,0:T(4,128)}), f32[32,3,4,256]{3,2,1,0:T(4,128)}, u32[]{:S(2)}, u32[]{:S(2)}) async-start(f32[32,3,4,256]{3,2,1,0:T(4,128)} %copy.76), calls=%async_computation.1 | async-start | bytes 786432 | tf_op jit(solution)/shard_map/all_to_all | solution.py:215
  119.5 0.2 reduce-scatter.2.cloned.1.call-start
  119.8 0.7 fusion.66
  120.5 1.0 copy.82
  121.5 1.7 copy.81
  123.3 1.9 copy.78
  125.2 1.1 subtract_convert_fusion
  126.4 1.1 fusion.40
  127.5 9.3 %all-to-all-done.1 = f32[32,3,4,256]{3,2,1,0:T(4,128)} async-done(((f32[32,3,4,256]{3,2,1,0:T(4,128)}), f32[32,3,4,256]{3,2,1,0:T(4,128)}, u32[]{:S(2)}, u32[]{:S(2)}) %all-to-all-start.1) | async-done | bytes 393248 | tf_op jit(solution)/shard_map/all_to_all | solution.py:215
  136.8 1.8 copy.77
  138.6 1.9 reshape.285
  140.5 1.5 convolution_multiply_fusion
  142.0 2.6 %multiply_reduce_fusion = (f32[256,3]{0,1:T(4,128)S(1)}, f32[256,3,128]{0,2,1:T(8,128)S(1)}) fusion(f32[256,3,128]{0,2,1:T(8,128)} %bitcast.333, f32[256,3,128]{0,2,1:T(8,128)} %bitcast.328, f32[3]{0:T(128)S(1)} %copy-done.37, f32[256,3,128]{0,2,1:T(8,128)S(1)} %convolution_multiply_fusion, f32[256,3]{0,1:T(4,128)S(1)} %copy-done.29, ...), kind=kOutput, calls=%fused_computation.45 | convolution fusion | flops 303955200 | bytes 1909772 | tf_op jit(solution)/shard_map/tsh,shp->thp/dot_general | solution.py:200
  144.8 23.8 %all-gather.4.cloned.1.call-done.kv_ref = bf16[16384,256]{1,0:T(8,128)(2,1)} async-done(((bf16[512,256]{1,0:T(8,128)(2,1)}), bf16[16384,256]{1,0:T(8,128)(2,1)}) %all-gather.4.cloned.1.call-update) | async-done | bytes 8388624 | tf_op jit(solution)/shard_map/all_gather | solution.py:231
  168.6 21.5 %shard_map.211 = bf16[512,128]{1,0:T(8,128)(2,1)S(1)} custom-call(s32[512,1]{1,0:T(8,128)S(1)} %bitcast.323, bf16[512,128]{1,0:T(8,128)(2,1)S(1)} %bitcast.324, s32[1,16384]{1,0:T(1,128)S(1)} %compare_select_fusion.kr_ref, bf16[16384,256]{1,0:T(8,128)(2,1)} %all-gather.4.cloned.1.call-done.kv_ref), custom_call_target="tpu_custom_call" | custom-call | tf_op jit(solution)/shard_map/pallas_call | solution.py:73
  190.2 2.0 fusion.69
  192.2 2.7 %convolution_add_fusion = f32[256,3072]{1,0:T(8,128)} fusion(f32[256,3072]{1,0:T(8,128)S(1)} %fusion.69, bf16[256,384]{0,1:T(8,128)(2,1)S(1)} %fusion.28, bf16[384,3072]{1,0:T(8,128)(2,1)S(1)} %copy-done), kind=kOutput, calls=%fused_computation.2 | convolution fusion | flops 604766208 | bytes 8847360 | tf_op jit(solution)/shard_map/dot_general | solution.py:249
  194.9 1.0 copy-done.4
  196.0 0.9 add_bitcast_fusion
  196.9 37.8 %reduce-scatter.2.cloned.1.call-done = f32[256,768]{1,0:T(8,128)} async-done(((f32[256,3072]{1,0:T(8,128)}), f32[256,768]{1,0:T(8,128)}) %reduce-scatter.2.cloned.1.call-update) | async-done | bytes 786448 | tf_op jit(solution)/shard_map/reduce_scatter | solution.py:250
  234.6 2.0 fusion.24
  (156 shorter events, 2.7 us)
Async XLA Ops:
  7.2 185.0 %copy-start = (bf16[384,3072]{1,0:T(8,128)(2,1)S(1)}, bf16[384,3072]{1,0:T(8,128)(2,1)}, u32[]{:S(2)}) copy-start(bf16[384,3072]{1,0:T(8,128)(2,1)} %param.34) | copy-start | bytes 7077892
  7.2 35.5 %all-gather.6.cloned.1.call-start = ((), (), s32[]{:S(2)}) async-start(), calls=%async_computation.5 | async-start | bytes 1966080 | tf_op jit(solution)/shard_map/all_gather | solution.py:152
  7.9 160.7 %all-gather.4.cloned.1.call-start = ((), (), s32[]{:S(2)}) async-start(), calls=%async_computation.3 | async-start | bytes 8650752 | tf_op jit(solution)/shard_map/all_gather | solution.py:231
  11.5 34.9 %copy-start.33 = (f32[64]{0:T(128)}, f32[64]{0:T(128)S(1)}, u32[]{:S(2)}) copy-start(f32[64]{0:T(128)S(1)} %multiply_power_fusion) | copy-start | bytes 772
  11.5 34.9 %copy-start.26 = (f32[256]{0:T(256)}, f32[256]{0:T(256)S(1)}, u32[]{:S(2)}) copy-start(f32[256]{0:T(256)S(1)} %add_convert_fusion.1) | copy-start | bytes 3076
  42.7 1.9 copy-start.2
  44.6 1.1 copy-start.7
  44.7 3.9 %copy-start.36 = (bf16[3072,2,384]{2,1,0:T(2,128)(2,1)S(1)}, bf16[3072,2,384]{2,1,0:T(2,128)(2,1)}, u32[]{:S(2)}) copy-start(bf16[3072,2,384]{2,1,0:T(2,128)(2,1)} %param.25) | copy-start | bytes 14155780
  45.8 8.5 %copy-start.1 = (bf16[256,3072]{1,0:T(8,128)(2,1)}, bf16[256,3072]{1,0:T(8,128)(2,1)S(1)}, u32[]{:S(2)}) copy-start(bf16[256,3072]{1,0:T(8,128)(2,1)S(1)} %fusion.4) | copy-start | bytes 4718596
  45.8 1.9 copy-start.12
  47.1 11.9 %copy-start.9 = (bf16[256,128]{1,0:T(8,128)(2,1)}, bf16[256,128]{1,0:T(8,128)(2,1)S(1)}, u32[]{:S(2)}) copy-start(bf16[256,128]{1,0:T(8,128)(2,1)S(1)} %fusion.52) | copy-start | bytes 196612
  48.3 5.9 %copy-start.14 = (bf16[3072,3]{0,1:T(4,128)(2,1)S(1)}, bf16[3072,3]{0,1:T(4,128)(2,1)}, u32[]{:S(2)}) copy-start(bf16[3072,3]{0,1:T(4,128)(2,1)} %param.27) | copy-start | bytes 55300
  48.3 5.9 %copy-start.35 = (f32[3]{0:T(128)S(1)}, f32[3]{0:T(128)}, u32[]{:S(2)}) copy-start(f32[3]{0:T(128)} %param.28) | copy-start | bytes 40
  48.3 10.6 %collective-permute-start = (bf16[512,128]{1,0:T(8,128)(2,1)}, bf16[512,128]{1,0:T(8,128)(2,1)}, u32[]{:S(2)}, u32[]{:S(2)}) collective-permute-start(bf16[512,128]{1,0:T(8,128)(2,1)} %pad_maximum_fusion.2), channel_id=1, source_target_pairs={{0,2},{2,0},{4,6},{6,4},{1,3},{3,1},{5,7},{7,5},{8,10},{10,8},{12,... | collective-permute-start | bytes 393224 | tf_op jit(solution)/shard_map/ppermute | solution.py:171
  49.9 4.8 %copy-start.11 = (bf16[256,2,384]{2,0,1:T(8,128)(2,1)}, bf16[256,2,384]{2,0,1:T(8,128)(2,1)S(1)}, u32[]{:S(2)}) copy-start(bf16[256,2,384]{2,0,1:T(8,128)(2,1)S(1)} %fusion.6) | copy-start | bytes 1179652
  50.0 6.1 %copy-start.8 = (bf16[3072,128]{1,0:T(8,128)(2,1)S(1)}, bf16[3072,128]{1,0:T(8,128)(2,1)}, u32[]{:S(2)}) copy-start(bf16[3072,128]{1,0:T(8,128)(2,1)} %param.26) | copy-start | bytes 2359300
  50.6 25.2 %collective-permute-start.1 = (bf16[3,384]{1,0:T(4,128)(2,1)}, bf16[3,384]{1,0:T(4,128)(2,1)}, u32[]{:S(2)}, u32[]{:S(2)}) collective-permute-start(bf16[3,384]{1,0:T(4,128)(2,1)} %slice_bitcast_fusion.63), channel_id=1, source_target_pairs={{0,8},{8,16},{16,24},{24,32},{32,40},{40,48},{48,56},{56,64},{64,7... | collective-permute-start | bytes 6920 | tf_op jit(solution)/shard_map/ppermute | solution.py:23
  56.1 3.0 %copy-start.13 = (bf16[1,256,128]{2,1,0:T(8,128)(2,1)S(1)}, bf16[1,256,128]{2,1,0:T(8,128)(2,1)}, u32[]{:S(2)}) copy-start(bf16[1,256,128]{2,1,0:T(8,128)(2,1)} %param.35) | copy-start | bytes 196612
  58.7 17.0 %copy-start.30 = (bf16[1,3,384]{2,1,0:T(4,128)(2,1)S(1)}, bf16[1,3,384]{2,1,0:T(4,128)(2,1)}, u32[]{:S(2)}) copy-start(bf16[1,3,384]{2,1,0:T(4,128)(2,1)} %param.37) | copy-start | bytes 6916
  58.7 17.1 %copy-start.22 = (f32[384]{0:T(512)S(1)}, f32[384]{0:T(512)}, u32[]{:S(2)}) copy-start(f32[384]{0:T(512)} %get-tuple-element.3) | copy-start | bytes 4612
  58.7 17.1 %copy-start.23 = (f32[384]{0:T(512)S(1)}, f32[384]{0:T(512)}, u32[]{:S(2)}) copy-start(f32[384]{0:T(512)} %get-tuple-element.4) | copy-start | bytes 4612
  58.7 17.1 %copy-start.24 = (f32[384]{0:T(512)S(1)}, f32[384]{0:T(512)}, u32[]{:S(2)}) copy-start(f32[384]{0:T(512)} %get-tuple-element.5) | copy-start | bytes 4612
  58.7 17.1 %copy-start.25 = (f32[384]{0:T(512)S(1)}, f32[384]{0:T(512)}, u32[]{:S(2)}) copy-start(f32[384]{0:T(512)} %get-tuple-element.6) | copy-start | bytes 4612
  58.8 17.4 %copy-start.15 = (f32[1,3,2,128]{3,1,2,0:T(4,128)}, f32[1,3,2,128]{3,1,2,0:T(4,128)S(1)}, u32[]{:S(2)}) copy-start(f32[1,3,2,128]{3,1,2,0:T(4,128)S(1)} %copy.107) | copy-start | bytes 9220
  59.0 20.7 %copy-start.31 = (f32[3]{0:T(128)}, f32[3]{0:T(128)S(1)}, u32[]{:S(2)}) copy-start(f32[3]{0:T(128)S(1)} %exp.50) | copy-start | bytes 40
  70.7 6.4 %collective-permute-start.2 = (bf16[3,512]{1,0:T(4,128)(2,1)S(1)}, bf16[3,512]{1,0:T(4,128)(2,1)S(1)}, u32[]{:S(2)}, u32[]{:S(2)}) collective-permute-start(bf16[3,512]{1,0:T(4,128)(2,1)S(1)} %slice.500), channel_id=1, source_target_pairs={{0,8},{8,16},{16,24},{24,32},{32,40},{40,48},{48,56},{56,64},{64,7... | collective-permute-start | bytes 9224 | tf_op jit(solution)/shard_map/ppermute | solution.py:23
  75.7 1.4 copy-start.28
  75.9 1.4 copy-start.18
  75.9 1.4 copy-start.19
  75.9 1.4 copy-start.20
  75.9 1.4 copy-start.21
  77.1 1.0 copy-start.6
  78.6 0.8 copy-start.3
  79.7 11.6 %copy-start.27 = (f32[256]{0:T(256)S(1)}, f32[256]{0:T(256)}, u32[]{:S(2)}) copy-start(f32[256]{0:T(256)} %copy-done.26) | copy-start | bytes 3076
  79.7 11.6 %copy-start.34 = (f32[64]{0:T(128)S(1)}, f32[64]{0:T(128)}, u32[]{:S(2)}) copy-start(f32[64]{0:T(128)} %copy-done.33) | copy-start | bytes 772
  80.8 30.0 %all-to-all-start = ((f32[32,3,5,256]{3,1,2,0:T(4,128)}), f32[32,3,5,256]{3,1,2,0:T(4,128)}, u32[]{:S(2)}, u32[]{:S(2)}) async-start(f32[32,3,5,256]{3,1,2,0:T(4,128)} %pad_maximum_fusion), calls=%async_computation | async-start | bytes 1310720 | tf_op jit(solution)/shard_map/all_to_all | solution.py:208
  110.8 2.2 copy-start.10
  114.5 22.3 %all-to-all-start.1 = ((f32[32,3,4,256]{3,2,1,0:T(4,128)}), f32[32,3,4,256]{3,2,1,0:T(4,128)}, u32[]{:S(2)}, u32[]{:S(2)}) async-start(f32[32,3,4,256]{3,2,1,0:T(4,128)} %copy.76), calls=%async_computation.1 | async-start | bytes 786432 | tf_op jit(solution)/shard_map/all_to_all | solution.py:215
  119.5 115.1 %reduce-scatter.2.cloned.1.call-start = ((), (), s32[]{:S(2)}) async-start(), calls=%async_computation.4 | async-start | bytes 3932160 | tf_op jit(solution)/shard_map/reduce_scatter | solution.py:250
  126.4 15.6 %copy-start.16 = (f32[1,3,2,128]{3,1,2,0:T(4,128)S(1)}, f32[1,3,2,128]{3,1,2,0:T(4,128)}, u32[]{:S(2)}) copy-start(f32[1,3,2,128]{3,1,2,0:T(4,128)} %copy-done.15) | copy-start | bytes 9220
  126.4 15.6 %copy-start.29 = (f32[256,3]{0,1:T(4,128)S(1)}, f32[256,3]{0,1:T(4,128)}, u32[]{:S(2)}) copy-start(f32[256,3]{0,1:T(4,128)} %get-tuple-element.76) | copy-start | bytes 9220
  126.4 15.6 %copy-start.37 = (f32[3]{0:T(128)S(1)}, f32[3]{0:T(128)}, u32[]{:S(2)}) copy-start(f32[3]{0:T(128)} %param.30) | copy-start | bytes 40
  142.0 2.7 %copy-start.17 = (f32[384]{0:T(512)S(1)}, f32[384]{0:T(512)}, u32[]{:S(2)}) copy-start(f32[384]{0:T(512)} %convert_element_type.79) | copy-start | bytes 4612
  194.9 1.0 copy-start.4
  194.9 1.1 copy-start.5
  194.9 1.1 copy-start.32
Sparse Core Ops, SparseCore 0:
  9.8 32.8 all-gather.5
  60.9 107.6 all-gather.3
  195.0 39.5 reduce-scatter.1

commit v6 on v5

--- a/solution.py
+++ b/solution.py
@@ -6,6 +6,7 @@
 from jax.experimental.pallas import tpu as pltpu
 
 HD = 128
+SEQ = ("seq_hi", "seq_lo")
 QH = 8
 KVH = 2
 NS = 256
@@ -146,7 +147,7 @@
     high = lax.Precision.HIGHEST
     own_rows = hidden[0]
     tokens = own_rows.shape[0]
-    seq_pos = lax.axis_index("seq")
+    seq_pos = lax.axis_index(SEQ)
     mp_pos = lax.axis_index("mp")
     length = cache_len[0]
     whole = lax.all_gather(own_rows, "mp", axis=1, tiled=True)
@@ -179,7 +180,7 @@
         jnp.bfloat16
     )
     rim = CONV - 1
-    prev_x, prev_bc = shifted((inner[tokens - rim :, 1], bc_all[tokens - rim :]), "seq", 1)
+    prev_x, prev_bc = shifted((inner[tokens - rim :, 1], bc_all[tokens - rim :]), SEQ, 1)
     first_block = seq_pos == 0
     prev_x = jnp.where(first_block, tail_x[0], prev_x)
     prev_bc = jnp.where(first_block, tail_bc[0], prev_bc)
@@ -201,18 +202,18 @@
     to_end = jnp.exp(cumulative[-1][None, :] - cumulative) * step_size
     own_state = jnp.einsum("sh,shp,sn->hpn", to_end, x_conv, b_mat, precision=high)
     block_decay = jnp.exp(cumulative[-1])
-    seq_size = lax.axis_size("seq")
+    seq_size = lax.axis_size(SEQ)
     rows = HD // seq_size
     pieces = jnp.transpose(own_state.reshape(mamba_heads, seq_size, rows, NS), (1, 0, 2, 3))
     decays = jnp.broadcast_to(block_decay[None, :, None, None], (seq_size, mamba_heads, 1, NS))
-    columns = lax.all_to_all(jnp.concatenate([pieces, decays], axis=2), "seq", 0, 0, tiled=True)
+    columns = lax.all_to_all(jnp.concatenate([pieces, decays], axis=2), SEQ, 0, 0, tiled=True)
     carry = lax.dynamic_slice_in_dim(ssm_init[0], seq_pos * rows, rows, 1)
     entering = []
     for source in range(seq_size):
         entering.append(carry)
         part = columns[source]
         carry = part[:, rows:, :] * carry + part[:, :rows, :]
-    entering = lax.all_to_all(jnp.stack(entering, axis=0), "seq", 0, 0, tiled=True)
+    entering = lax.all_to_all(jnp.stack(entering, axis=0), SEQ, 0, 0, tiled=True)
     incoming = jnp.transpose(entering, (1, 0, 2, 3)).reshape(mamba_heads, HD, NS)
     carried = jnp.exp(cumulative)[:, :, None] * jnp.einsum(
         "tn,hpn->thp", c_mat, incoming, precision=high
@@ -228,7 +229,8 @@
     group = mp_pos * local_heads // (QH // KVH)
     query_index = seq_pos * tokens + jnp.arange(tokens, dtype=jnp.int32)
     scale = 1.0 / float(HD) ** 0.5
-    piece = lax.all_gather(group_rows, "seq", axis=0, tiled=True)
+    piece = lax.all_gather(group_rows, SEQ[1], axis=0, tiled=True)
+    piece = lax.all_gather(piece, SEQ[0], axis=0, tiled=True)
     count = piece.shape[0]
     index = jnp.arange(count, dtype=jnp.int32)
     owner = index // shard_rows
@@ -253,8 +255,14 @@
 
 
 def solution(mesh):
+    devices = mesh.devices
+    lanes = devices[:, 0, 0]
+    inner = len({d.coords[1] for d in lanes}) if hasattr(lanes[0], "coords") else 1
+    split = jax.sharding.Mesh(
+        devices.reshape((devices.shape[0] // inner, inner) + devices.shape[1:]), SEQ + mesh.axis_names[1:]
+    )
     placed = (
-        P("req", "seq", "mp"),
+        P("req", SEQ, "mp"),
         P(),
         P(None, "mp"),
         P(None, "mp"),
@@ -269,7 +277,7 @@
         P(),
         P("mp"),
         P("mp", None),
-        P("req", "seq", "mp"),
+        P("req", SEQ, "mp"),
         P("req"),
         P("req", None, "mp"),
         P("req", None, None),
@@ -277,8 +285,8 @@
     )
     return jax.shard_map(
         shards,
-        mesh=mesh,
+        mesh=split,
         in_specs=placed,
-        out_specs=(P("req", "seq", "mp"), P("req", "seq", "mp"), P("req", "seq", "mp", None, None)),
+        out_specs=(P("req", SEQ, "mp"), P("req", SEQ, "mp"), P("req", SEQ, "mp", None, None)),
         check_vma=False,
     )

time: 244 us -> 283 us (1.16)
  waiting for transfers between devices: 115 us -> 150 us
    all_gather x1 -> x2, waiting for transfers between devices: 23.8 us -> 57 us  [the longest x1 47.1 us: shards(): piece = lax.all_gather(piece, SEQ[0], axis=0, tiled=True)]
    unnamed x83 -> x87, local copies, waits for them, and re-layouts: 7.27 us -> 8.13 us
  transfers between devices with their start and end apart: 8 -> 9, of which waited for: 5 -> 6; matrix products, arithmetic and copies ran while one was open for 19% -> 17% of each run, Pallas kernels for 0% -> 0%
where the time goes in v6:
time: 283 us; the launch traced here: 282 us
  waiting for transfers between devices  150 us (53%)
  starting transfers between devices  22.7 us (8%)
  other arithmetic  21.9 us (8%)
  local copies, waits for them, and re-layouts  21.7 us (8%)
  Pallas kernels  21.5 us (8%)
  matrix products  18.8 us (7%)
  between operations  15.3 us (5%)
  blocking collectives  9.9 us (3%)
    all_gather x1, waiting for transfers between devices, shards(): piece = lax.all_gather(piece, SEQ[0], axis=0, tiled=True)  47.1 us
    reduce_scatter x1, waiting for transfers between devices, shards(): summed = lax.psum_scatter(term, 'mp', scatter_dimension=1, tiled=True)  37.5 us
    all_gather x1, waiting for transfers between devices, shards(): whole = lax.all_gather(own_rows, 'mp', axis=1, tiled=True)  28.2 us
    pallas_call x1, Pallas kernels, attend(): pl.pallas_call(kernel, grid=(steps,), in_specs=[pl.BlockSpec((rows, 1), l...  21.5 us
    all_to_all x1, waiting for transfers between devices, shards(): lax.all_to_all(jnp.concatenate([pieces, decays], axis=2), SEQ, 0, 0, tile...  17.1 us
    all_gather x1, waiting for transfers between devices, shards(): piece = lax.all_gather(group_rows, SEQ[1], axis=0, tiled=True)  9.9 us
    all_gather x1, blocking collectives, shards(): bc_all = lax.all_gather(bc_block, 'mp', axis=1, tiled=True)  9.9 us
    all_to_all x1, waiting for transfers between devices, shards(): lax.all_to_all(jnp.stack(entering, axis=0), SEQ, 0, 0, tiled=True)  9.76 us
  transfers between devices with their start and end apart: 9, of which 6 were waited for; matrix products, arithmetic and copies ran while one was open for 17% of the time, Pallas kernels for 0%

profile of v6, /device:TPU:1, one launch (start us, length us, event | category | flops | bytes accessed | tf_op | source)
XLA Modules:
  0.0 282.0 jit_solution(6152858143523569854)
XLA Ops:
  7.2 0.7 all-gather.9.cloned.1.call-update
  8.2 0.7 convert_element_type.69
  9.5 1.2 exp.44
  10.8 0.7 convert_element_type.79
  11.5 1.5 convert_reduce_fusion.3
  12.9 1.4 slice_convert_fusion.4
  14.5 28.2 %all-gather.9.cloned.1.call-done = bf16[1,256,3072]{2,1,0:T(8,128)(2,1)} async-done(((bf16[1,256,768]{2,1,0:T(8,128)(2,1)}), bf16[1,256,3072]{2,1,0:T(8,128)(2,1)}) %all-gather.9.cloned.1.call-update) | async-done | bytes 1572880 | tf_op jit(solution)/shard_map/all_gather | solution.py:153
  42.7 1.9 fusion.2
  44.7 0.5 fusion.4
  45.2 0.6 copy-done.11
  45.8 0.6 fusion.68
  46.4 0.6 fusion.49
  47.1 0.6 copy-done.16
  47.7 0.7 pad_maximum_fusion.2
  48.5 1.4 fusion.6
  50.0 0.6 slice_bitcast_fusion.63
  50.5 3.7 %collective-permute-start.1 = (bf16[3,384]{1,0:T(4,128)(2,1)}, bf16[3,384]{1,0:T(4,128)(2,1)}, u32[]{:S(2)}, u32[]{:S(2)}) collective-permute-start(bf16[3,384]{1,0:T(4,128)(2,1)} %slice_bitcast_fusion.63), channel_id=1, source_target_pairs={{0,8},{8,16},{16,24},{24,32},{32,40},{40,48},{48,56},{56,64},{64,7... | collective-permute-start | bytes 6920 | tf_op jit(solution)/shard_map/ppermute | solution.py:24
  54.2 0.5 fusion.59
  54.8 0.9 reduce-window.6
  55.8 0.7 copy.72
  56.5 0.7 reduce-window.9
  57.2 0.6 slice.382
  57.8 0.8 copy.73
  58.6 2.6 convolution_convert_fusion
  61.3 1.7 maximum_select_fusion
  63.3 9.9 %all_gather.15 = bf16[256,512]{1,0:T(8,128)(2,1)S(1)} all-gather(bf16[256,128]{1,0:T(8,128)(2,1)} %convolution_convert_fusion), channel_id=1, replica_groups=mesh['seq_hi'=8,'seq_lo'=4,'mp'=4,'req'=2] {'mp'}, dimensions={1}, use_global_device_ids=true | all-gather | bytes 327680 | tf_op jit(solution)/shard_map/all_gather | solution.py:169
  73.2 2.5 collective-permute-start.2
  75.8 1.8 slice_convert_fusion
  77.6 0.6 compare_select_fusion.1
  78.6 0.9 copy.71
  79.6 9.9 %all-gather.5.cloned.1.call-done = bf16[2048,256]{1,0:T(8,128)(2,1)} async-done(((bf16[512,256]{1,0:T(8,128)(2,1)}), bf16[2048,256]{1,0:T(8,128)(2,1)}) %all-gather.5.cloned.1.call-update) | async-done | bytes 1048592 | tf_op jit(solution)/shard_map/all_gather | solution.py:232
  89.6 0.3 divide_multiply_fusion
  90.0 0.8 copy-done.3
  90.8 0.5 fusion.29
  91.3 0.7 copy-done.5
  92.4 1.0 pad_maximum_fusion
  93.4 8.7 %all-to-all-start = ((f32[32,3,5,256]{3,1,2,0:T(4,128)}), f32[32,3,5,256]{3,1,2,0:T(4,128)S(1)}, u32[]{:S(2)}, u32[]{:S(2)}) async-start(f32[32,3,5,256]{3,1,2,0:T(4,128)} %pad_maximum_fusion), calls=%async_computation | async-start | bytes 1310720 | tf_op jit(solution)/shard_map/all_to_all | solution.py:209
  102.1 0.8 constant_dynamic-slice_fusion
  102.9 0.6 constant_dynamic-update-slice_fusion.31
  103.5 1.2 multiply_cosine_fusion.1
  104.8 3.3 %fusion.67 = f32[256,256]{0,1:T(8,128)} fusion(bf16[256,3072]{1,0:T(8,128)(2,1)} %copy-done.1, bf16[3072,256]{1,0:T(8,128)(2,1)} %param.22), kind=kOutput, calls=%fused_computation.258 | convolution fusion | flops 402653184 | bytes 3407872 | tf_op jit(solution)/shard_map/dot_general | solution.py:160
  108.1 17.1 %all-to-all-done = f32[32,3,5,256]{3,1,2,0:T(4,128)S(1)} async-done(((f32[32,3,5,256]{3,1,2,0:T(4,128)}), f32[32,3,5,256]{3,1,2,0:T(4,128)S(1)}, u32[]{:S(2)}, u32[]{:S(2)}) %all-to-all-start) | async-done | bytes 491552 | tf_op jit(solution)/shard_map/all_to_all | solution.py:209
  125.5 0.7 copy-done.14
  126.8 0.9 copy.76
  127.7 7.3 %all-to-all-start.1 = ((f32[32,3,4,256]{3,2,1,0:T(4,128)}), f32[32,3,4,256]{3,2,1,0:T(4,128)}, u32[]{:S(2)}, u32[]{:S(2)}) async-start(f32[32,3,4,256]{3,2,1,0:T(4,128)} %copy.76), calls=%async_computation.1 | async-start | bytes 786432 | tf_op jit(solution)/shard_map/all_to_all | solution.py:216
  135.2 0.7 fusion.66
  135.9 1.8 copy.82
  137.7 0.8 copy.81
  138.5 1.9 copy.78
  140.5 1.2 subtract_convert_fusion
  141.8 1.1 fusion.40
  142.9 9.8 %all-to-all-done.1 = f32[32,3,4,256]{3,2,1,0:T(4,128)} async-done(((f32[32,3,4,256]{3,2,1,0:T(4,128)}), f32[32,3,4,256]{3,2,1,0:T(4,128)}, u32[]{:S(2)}, u32[]{:S(2)}) %all-to-all-start.1) | async-done | bytes 393248 | tf_op jit(solution)/shard_map/all_to_all | solution.py:216
  152.7 1.8 copy.77
  154.4 1.9 reshape.285
  156.3 1.5 convolution_multiply_fusion
  157.9 2.6 multiply_reduce_fusion
  160.6 47.1 %all-gather.7.cloned.1.call-done.kv_ref = bf16[16384,256]{1,0:T(8,128)(2,1)} async-done(((bf16[2048,256]{1,0:T(8,128)(2,1)}), bf16[16384,256]{1,0:T(8,128)(2,1)}) %all-gather.7.cloned.1.call-update) | async-done | bytes 8388624 | tf_op jit(solution)/shard_map/all_gather | solution.py:233
  207.7 21.5 %shard_map.211 = bf16[512,128]{1,0:T(8,128)(2,1)S(1)} custom-call(s32[512,1]{1,0:T(8,128)S(1)} %bitcast.323, bf16[512,128]{1,0:T(8,128)(2,1)S(1)} %bitcast.324, s32[1,16384]{1,0:T(1,128)S(1)} %compare_select_fusion.kr_ref, bf16[16384,256]{1,0:T(8,128)(2,1)} %all-gather.7.cloned.1.call-done.kv_ref), custom_call_target="tpu_custom_call" | custom-call | tf_op jit(solution)/shard_map/pallas_call | solution.py:74
  229.3 2.0 fusion.69
  231.3 2.7 convolution_add_fusion
  234.0 1.0 copy-done.6
  235.1 0.9 add_bitcast_fusion
  236.0 37.5 %reduce-scatter.2.cloned.1.call-done = f32[256,768]{1,0:T(8,128)} async-done(((f32[256,3072]{1,0:T(8,128)}), f32[256,768]{1,0:T(8,128)}) %reduce-scatter.2.cloned.1.call-update) | async-done | bytes 786448 | tf_op jit(solution)/shard_map/reduce_scatter | solution.py:252
  273.5 1.9 fusion.24
  (163 shorter events, 3.5 us)
Async XLA Ops:
  7.2 224.2 %copy-start = (bf16[384,3072]{1,0:T(8,128)(2,1)S(1)}, bf16[384,3072]{1,0:T(8,128)(2,1)}, u32[]{:S(2)}) copy-start(bf16[384,3072]{1,0:T(8,128)(2,1)} %param.34) | copy-start | bytes 7077892
  7.2 35.5 %all-gather.9.cloned.1.call-start = ((), (), s32[]{:S(2)}) async-start(), calls=%async_computation.6 | async-start | bytes 1966080 | tf_op jit(solution)/shard_map/all_gather | solution.py:153
  7.9 81.6 %all-gather.5.cloned.1.call-start = ((), (), s32[]{:S(2)}) async-start(), calls=%async_computation.3 | async-start | bytes 1310720 | tf_op jit(solution)/shard_map/all_gather | solution.py:232
  11.5 34.9 %copy-start.34 = (f32[64]{0:T(128)}, f32[64]{0:T(128)S(1)}, u32[]{:S(2)}) copy-start(f32[64]{0:T(128)S(1)} %multiply_power_fusion) | copy-start | bytes 772
  11.5 34.9 %copy-start.27 = (f32[256]{0:T(256)}, f32[256]{0:T(256)S(1)}, u32[]{:S(2)}) copy-start(f32[256]{0:T(256)S(1)} %add_convert_fusion.1) | copy-start | bytes 3076
  42.7 1.9 copy-start.2
  44.6 1.1 copy-start.11
  44.7 3.9 %copy-start.38 = (bf16[3072,2,384]{2,1,0:T(2,128)(2,1)S(1)}, bf16[3072,2,384]{2,1,0:T(2,128)(2,1)}, u32[]{:S(2)}) copy-start(bf16[3072,2,384]{2,1,0:T(2,128)(2,1)} %param.25) | copy-start | bytes 14155780
  45.8 8.5 %copy-start.1 = (bf16[256,3072]{1,0:T(8,128)(2,1)}, bf16[256,3072]{1,0:T(8,128)(2,1)S(1)}, u32[]{:S(2)}) copy-start(bf16[256,3072]{1,0:T(8,128)(2,1)S(1)} %fusion.4) | copy-start | bytes 4718596
  45.8 1.9 copy-start.16
  47.1 14.2 %copy-start.13 = (bf16[256,128]{1,0:T(8,128)(2,1)}, bf16[256,128]{1,0:T(8,128)(2,1)S(1)}, u32[]{:S(2)}) copy-start(bf16[256,128]{1,0:T(8,128)(2,1)S(1)} %fusion.52) | copy-start | bytes 196612
  48.3 5.9 %copy-start.18 = (bf16[3072,3]{0,1:T(4,128)(2,1)S(1)}, bf16[3072,3]{0,1:T(4,128)(2,1)}, u32[]{:S(2)}) copy-start(bf16[3072,3]{0,1:T(4,128)(2,1)} %param.27) | copy-start | bytes 55300
  48.3 5.9 %copy-start.36 = (f32[3]{0:T(128)S(1)}, f32[3]{0:T(128)}, u32[]{:S(2)}) copy-start(f32[3]{0:T(128)} %param.28) | copy-start | bytes 40
  48.3 5.9 %copy-start.37 = (f32[3]{0:T(128)S(1)}, f32[3]{0:T(128)}, u32[]{:S(2)}) copy-start(f32[3]{0:T(128)} %exp.44) | copy-start | bytes 40
  48.4 12.9 %collective-permute-start = (bf16[512,128]{1,0:T(8,128)(2,1)}, bf16[512,128]{1,0:T(8,128)(2,1)}, u32[]{:S(2)}, u32[]{:S(2)}) collective-permute-start(bf16[512,128]{1,0:T(8,128)(2,1)} %pad_maximum_fusion.2), channel_id=1, source_target_pairs={{0,2},{2,0},{4,6},{6,4},{1,3},{3,1},{5,7},{7,5},{8,10},{10,8},{12,... | collective-permute-start | bytes 393224 | tf_op jit(solution)/shard_map/ppermute | solution.py:172
  49.9 4.9 %copy-start.15 = (bf16[256,2,384]{2,0,1:T(8,128)(2,1)}, bf16[256,2,384]{2,0,1:T(8,128)(2,1)S(1)}, u32[]{:S(2)}) copy-start(bf16[256,2,384]{2,0,1:T(8,128)(2,1)S(1)} %fusion.6) | copy-start | bytes 1179652
  50.0 8.6 %copy-start.12 = (bf16[3072,128]{1,0:T(8,128)(2,1)S(1)}, bf16[3072,128]{1,0:T(8,128)(2,1)}, u32[]{:S(2)}) copy-start(bf16[3072,128]{1,0:T(8,128)(2,1)} %param.26) | copy-start | bytes 2359300
  50.5 27.7 %collective-permute-start.1 = (bf16[3,384]{1,0:T(4,128)(2,1)}, bf16[3,384]{1,0:T(4,128)(2,1)}, u32[]{:S(2)}, u32[]{:S(2)}) collective-permute-start(bf16[3,384]{1,0:T(4,128)(2,1)} %slice_bitcast_fusion.63), channel_id=1, source_target_pairs={{0,8},{8,16},{16,24},{24,32},{32,40},{40,48},{48,56},{56,64},{64,7... | collective-permute-start | bytes 6920 | tf_op jit(solution)/shard_map/ppermute | solution.py:24
  58.6 2.7 copy-start.17
  61.2 17.0 %copy-start.31 = (bf16[1,3,384]{2,1,0:T(4,128)(2,1)S(1)}, bf16[1,3,384]{2,1,0:T(4,128)(2,1)}, u32[]{:S(2)}) copy-start(bf16[1,3,384]{2,1,0:T(4,128)(2,1)} %param.37) | copy-start | bytes 6916
  61.2 17.1 %copy-start.23 = (f32[384]{0:T(512)S(1)}, f32[384]{0:T(512)}, u32[]{:S(2)}) copy-start(f32[384]{0:T(512)} %get-tuple-element.3) | copy-start | bytes 4612
  61.2 17.1 %copy-start.24 = (f32[384]{0:T(512)S(1)}, f32[384]{0:T(512)}, u32[]{:S(2)}) copy-start(f32[384]{0:T(512)} %get-tuple-element.4) | copy-start | bytes 4612
  61.2 17.1 %copy-start.25 = (f32[384]{0:T(512)S(1)}, f32[384]{0:T(512)}, u32[]{:S(2)}) copy-start(f32[384]{0:T(512)} %get-tuple-element.5) | copy-start | bytes 4612
  61.2 17.1 %copy-start.26 = (f32[384]{0:T(512)S(1)}, f32[384]{0:T(512)}, u32[]{:S(2)}) copy-start(f32[384]{0:T(512)} %get-tuple-element.6) | copy-start | bytes 4612
  63.1 144.6 %all-gather.7.cloned.1.call-start = ((), (), s32[]{:S(2)}) async-start(), calls=%async_computation.4 | async-start | bytes 9437184 | tf_op jit(solution)/shard_map/all_gather | solution.py:233
  63.3 29.0 %copy-start.32 = (f32[3]{0:T(128)}, f32[3]{0:T(128)S(1)}, u32[]{:S(2)}) copy-start(f32[3]{0:T(128)S(1)} %exp.50) | copy-start | bytes 40
  73.2 6.3 %collective-permute-start.2 = (bf16[3,512]{1,0:T(4,128)(2,1)S(1)}, bf16[3,512]{1,0:T(4,128)(2,1)S(1)}, u32[]{:S(2)}, u32[]{:S(2)}) collective-permute-start(bf16[3,512]{1,0:T(4,128)(2,1)S(1)} %slice.500), channel_id=1, source_target_pairs={{0,8},{8,16},{16,24},{24,32},{32,40},{40,48},{48,56},{56,64},{64,7... | collective-permute-start | bytes 9224 | tf_op jit(solution)/shard_map/ppermute | solution.py:24
  78.2 1.3 copy-start.29
  78.6 11.0 %copy-start.19 = (f32[1,512]{1,0:T(1,128)S(1)}, f32[1,512]{1,0:T(1,128)}, u32[]{:S(2)}) copy-start(f32[1,512]{1,0:T(1,128)} %get-tuple-element.78) | copy-start | bytes 6148
  78.6 11.0 %copy-start.20 = (f32[1,512]{1,0:T(1,128)S(1)}, f32[1,512]{1,0:T(1,128)}, u32[]{:S(2)}) copy-start(f32[1,512]{1,0:T(1,128)} %get-tuple-element.79) | copy-start | bytes 6148
  78.6 11.0 %copy-start.21 = (f32[1,512]{1,0:T(1,128)S(1)}, f32[1,512]{1,0:T(1,128)}, u32[]{:S(2)}) copy-start(f32[1,512]{1,0:T(1,128)} %get-tuple-element.80) | copy-start | bytes 6148
  78.6 11.0 %copy-start.22 = (f32[1,512]{1,0:T(1,128)S(1)}, f32[1,512]{1,0:T(1,128)}, u32[]{:S(2)}) copy-start(f32[1,512]{1,0:T(1,128)} %get-tuple-element.81) | copy-start | bytes 6148
  89.6 1.2 copy-start.9
  89.9 0.8 copy-start.3
  91.3 0.8 copy-start.5
  92.3 11.2 %copy-start.28 = (f32[256]{0:T(256)S(1)}, f32[256]{0:T(256)}, u32[]{:S(2)}) copy-start(f32[256]{0:T(256)} %copy-done.27) | copy-start | bytes 3076
  92.3 11.2 %copy-start.35 = (f32[64]{0:T(128)S(1)}, f32[64]{0:T(128)}, u32[]{:S(2)}) copy-start(f32[64]{0:T(128)} %copy-done.34) | copy-start | bytes 772
  93.4 31.7 %all-to-all-start = ((f32[32,3,5,256]{3,1,2,0:T(4,128)}), f32[32,3,5,256]{3,1,2,0:T(4,128)S(1)}, u32[]{:S(2)}, u32[]{:S(2)}) async-start(f32[32,3,5,256]{3,1,2,0:T(4,128)} %pad_maximum_fusion), calls=%async_computation | async-start | bytes 1310720 | tf_op jit(solution)/shard_map/all_to_all | solution.py:209
  125.1 1.1 copy-start.14
  126.4 8.8 %copy-start.10 = (f32[256,256]{0,1:T(8,128)S(1)}, f32[256,256]{0,1:T(8,128)}, u32[]{:S(2)}) copy-start(f32[256,256]{0,1:T(8,128)} %fusion.67) | copy-start | bytes 786436
  127.7 25.0 %all-to-all-start.1 = ((f32[32,3,4,256]{3,2,1,0:T(4,128)}), f32[32,3,4,256]{3,2,1,0:T(4,128)}, u32[]{:S(2)}, u32[]{:S(2)}) async-start(f32[32,3,4,256]{3,2,1,0:T(4,128)} %copy.76), calls=%async_computation.1 | async-start | bytes 786432 | tf_op jit(solution)/shard_map/all_to_all | solution.py:216
  135.0 138.5 %reduce-scatter.2.cloned.1.call-start = ((), (), s32[]{:S(2)}) async-start(), calls=%async_computation.5 | async-start | bytes 3932160 | tf_op jit(solution)/shard_map/reduce_scatter | solution.py:252
  135.9 5.8 %copy-start.4 = (f32[256,512]{1,0:T(8,128)S(1)}, f32[256,512]{1,0:T(8,128)}, u32[]{:S(2)}) copy-start(f32[256,512]{1,0:T(8,128)} %copy-done.3) | copy-start | bytes 1572868
  141.8 16.1 %copy-start.30 = (f32[256,3]{0,1:T(4,128)S(1)}, f32[256,3]{0,1:T(4,128)}, u32[]{:S(2)}) copy-start(f32[256,3]{0,1:T(4,128)} %get-tuple-element.76) | copy-start | bytes 9220
  141.8 16.1 %copy-start.39 = (f32[3]{0:T(128)S(1)}, f32[3]{0:T(128)}, u32[]{:S(2)}) copy-start(f32[3]{0:T(128)} %param.30) | copy-start | bytes 40
  234.0 1.0 copy-start.6
  234.0 1.1 copy-start.7
  234.0 1.1 copy-start.33
  234.0 39.5 %copy-start.8 = (bf16[1,256,768]{2,1,0:T(8,128)(2,1)S(1)}, bf16[1,256,768]{2,1,0:T(8,128)(2,1)}, u32[]{:S(2)}) copy-start(bf16[1,256,768]{2,1,0:T(8,128)(2,1)} %param.20) | copy-start | bytes 1179652
Sparse Core Ops, SparseCore 0:
  9.8 32.8 all-gather.8
  63.2 26.3 all-gather.4
  91.3 116.3 all-gather.6
  234.2 39.2 reduce-scatter.1

commit v7 on v5

--- a/solution.py
+++ b/solution.py
@@ -247,7 +247,8 @@
     attended = attended.astype(jnp.bfloat16)
     term = jnp.dot(attended, w_attn_out, preferred_element_type=jnp.float32)
     term = term + jnp.dot(mixed, w_mamba_out, preferred_element_type=jnp.float32)
-    summed = lax.psum_scatter(term, "mp", scatter_dimension=1, tiled=True)
+    summed = lax.psum_scatter(term.astype(jnp.bfloat16), "mp", scatter_dimension=1, tiled=True)
+    summed = summed.astype(jnp.float32)
     layer = (summed + own_rows.astype(jnp.float32)).astype(jnp.bfloat16)
     return (layer[None], kv_block[None], state_after[None, None])
 

time: 244 us -> 230 us (0.943)
  waiting for transfers between devices: 115 us -> 102 us
    reduce_scatter x1, waiting for transfers between devices: 37.8 us -> 24.2 us  [shards(): lax.psum_scatter(term.astype(jnp.bfloat16), 'mp', scatter_dimension=1, ti...]
  transfers between devices with their start and end apart: 8 -> 8, of which waited for: 5 -> 5; matrix products, arithmetic and copies ran while one was open for 19% -> 20% of each run, Pallas kernels for 0% -> 0%
where the time goes in v7:
time: 230 us; the launch traced here: 229 us
  waiting for transfers between devices  102 us (44%)
  other arithmetic  21.7 us (9%)
  Pallas kernels  21.5 us (9%)
  starting transfers between devices  20.9 us (9%)
  local copies, waits for them, and re-layouts  20.4 us (9%)
  matrix products  17.7 us (8%)
  between operations  15.3 us (7%)
  blocking collectives  9.9 us (4%)
    all_gather x1, waiting for transfers between devices, shards(): whole = lax.all_gather(own_rows, 'mp', axis=1, tiled=True)  28.2 us
    reduce_scatter x1, waiting for transfers between devices, shards(): lax.psum_scatter(term.astype(jnp.bfloat16), 'mp', scatter_dimension=1, ti...  24.2 us
    all_gather x1, waiting for transfers between devices, shards(): piece = lax.all_gather(group_rows, 'seq', axis=0, tiled=True)  23.8 us
    pallas_call x1, Pallas kernels, attend(): pl.pallas_call(kernel, grid=(steps,), in_specs=[pl.BlockSpec((rows, 1), l...  21.5 us
    all_to_all x1, waiting for transfers between devices, shards(): lax.all_to_all(jnp.concatenate([pieces, decays], axis=2), 'seq', 0, 0, ti...  15.6 us
    all_gather x1, blocking collectives, shards(): bc_all = lax.all_gather(bc_block, 'mp', axis=1, tiled=True)  9.9 us
    all_to_all x1, waiting for transfers between devices, shards(): lax.all_to_all(jnp.stack(entering, axis=0), 'seq', 0, 0, tiled=True)  9.26 us
    all_to_all x1, starting transfers between devices, shards(): lax.all_to_all(jnp.concatenate([pieces, decays], axis=2), 'seq', 0, 0, ti...  9.14 us
  transfers between devices with their start and end apart: 8, of which 5 were waited for; matrix products, arithmetic and copies ran while one was open for 20% of the time, Pallas kernels for 0%

profile of v7, /device:TPU:1, one launch (start us, length us, event | category | flops | bytes accessed | tf_op | source)
XLA Modules:
  0.0 229.1 jit_solution(10675434946590536141)
XLA Ops:
  7.2 0.7 all-gather.6.cloned.1.call-update
  8.2 0.7 convert_element_type.75
  9.5 0.7 exp.44
  10.2 1.3 convert_element_type.85
  11.5 1.4 convert_reduce_fusion.3
  12.9 1.4 slice_convert_fusion.4
  14.5 28.2 %all-gather.6.cloned.1.call-done = bf16[1,256,3072]{2,1,0:T(8,128)(2,1)} async-done(((bf16[1,256,768]{2,1,0:T(8,128)(2,1)}), bf16[1,256,3072]{2,1,0:T(8,128)(2,1)}) %all-gather.6.cloned.1.call-update) | async-done | bytes 1572880 | tf_op jit(solution)/shard_map/all_gather | solution.py:152
  42.7 1.9 fusion.3
  44.7 0.5 fusion.5
  45.2 0.6 copy-done.7
  45.8 0.6 fusion.69
  46.4 0.6 fusion.50
  47.1 0.6 copy-done.12
  47.7 0.7 pad_maximum_fusion.2
  48.5 1.4 fusion.7
  50.0 0.6 slice_bitcast_fusion.63
  50.6 3.7 %collective-permute-start.1 = (bf16[3,384]{1,0:T(4,128)(2,1)}, bf16[3,384]{1,0:T(4,128)(2,1)}, u32[]{:S(2)}, u32[]{:S(2)}) collective-permute-start(bf16[3,384]{1,0:T(4,128)(2,1)} %slice_bitcast_fusion.63), channel_id=1, source_target_pairs={{0,8},{8,16},{16,24},{24,32},{32,40},{40,48},{48,56},{56,64},{64,7... | collective-permute-start | bytes 6920 | tf_op jit(solution)/shard_map/ppermute | solution.py:23
  54.2 0.5 fusion.60
  54.8 0.9 reduce-window.6
  56.1 2.6 %convolution_convert_fusion = bf16[256,128]{1,0:T(8,128)(2,1)} fusion(bf16[256,3072]{1,0:T(8,128)(2,1)} %copy-done.1, bf16[3072,128]{1,0:T(8,128)(2,1)S(1)} %copy-done.8), kind=kOutput, calls=%fused_computation.16 | convolution fusion | flops 201359360 | bytes 2424832 | tf_op jit(solution)/shard_map/dot_general | solution.py:167
  58.8 0.2 slice_reduce_fusion
  59.0 1.8 maximum_select_fusion
  60.8 9.9 %all_gather.11 = bf16[256,512]{1,0:T(8,128)(2,1)S(1)} all-gather(bf16[256,128]{1,0:T(8,128)(2,1)} %convolution_convert_fusion), channel_id=1, replica_groups=mesh['seq'=32,'mp'=4,'req'=2] {'mp'}, dimensions={1}, use_global_device_ids=true | all-gather | bytes 327680 | tf_op jit(solution)/shard_map/all_gather | solution.py:168
  70.7 2.6 %collective-permute-start.2 = (bf16[3,512]{1,0:T(4,128)(2,1)S(1)}, bf16[3,512]{1,0:T(4,128)(2,1)S(1)}, u32[]{:S(2)}, u32[]{:S(2)}) collective-permute-start(bf16[3,512]{1,0:T(4,128)(2,1)S(1)} %slice.500), channel_id=1, source_target_pairs={{0,8},{8,16},{16,24},{24,32},{32,40},{40,48},{48,56},{56,64},{64,7... | collective-permute-start | bytes 9224 | tf_op jit(solution)/shard_map/ppermute | solution.py:23
  73.3 1.8 slice_convert_fusion
  75.1 0.6 compare_select_fusion.1
  75.9 0.2 divide_multiply_fusion.1
  76.2 0.9 copy.71
  77.2 0.3 divide_multiply_fusion
  77.6 0.5 copy-done.6
  78.1 0.5 fusion.30
  78.6 0.8 copy-done.3
  79.4 0.3 copy.80
  79.8 1.0 pad_maximum_fusion
  80.8 9.1 %all-to-all-start = ((f32[32,3,5,256]{3,1,2,0:T(4,128)}), f32[32,3,5,256]{3,1,2,0:T(4,128)}, u32[]{:S(2)}, u32[]{:S(2)}) async-start(f32[32,3,5,256]{3,1,2,0:T(4,128)} %pad_maximum_fusion), calls=%async_computation | async-start | bytes 1310720 | tf_op jit(solution)/shard_map/all_to_all | solution.py:208
  89.9 0.8 constant_dynamic-slice_fusion
  90.7 0.6 constant_dynamic-update-slice_fusion.31
  91.3 1.2 multiply_cosine_fusion.1
  92.5 2.6 %fusion.68 = f32[256,256]{0,1:T(8,128)S(1)} fusion(bf16[256,3072]{1,0:T(8,128)(2,1)} %copy-done.1, bf16[3072,256]{1,0:T(8,128)(2,1)} %param.22), kind=kOutput, calls=%fused_computation.259 | convolution fusion | flops 402653184 | bytes 3407872 | tf_op jit(solution)/shard_map/dot_general | solution.py:159
  95.2 15.6 %all-to-all-done = f32[32,3,5,256]{3,1,2,0:T(4,128)} async-done(((f32[32,3,5,256]{3,1,2,0:T(4,128)}), f32[32,3,5,256]{3,1,2,0:T(4,128)}, u32[]{:S(2)}, u32[]{:S(2)}) %all-to-all-start) | async-done | bytes 491552 | tf_op jit(solution)/shard_map/all_to_all | solution.py:208
  110.8 1.0 slice_bitcast_fusion.1
  111.8 0.9 slice_bitcast_fusion.20
  113.6 0.9 copy.76
  114.5 5.1 %all-to-all-start.1 = ((f32[32,3,4,256]{3,2,1,0:T(4,128)}), f32[32,3,4,256]{3,2,1,0:T(4,128)}, u32[]{:S(2)}, u32[]{:S(2)}) async-start(f32[32,3,4,256]{3,2,1,0:T(4,128)} %copy.76), calls=%async_computation.1 | async-start | bytes 786432 | tf_op jit(solution)/shard_map/all_to_all | solution.py:215
  119.5 0.2 reduce-scatter.2.cloned.1.call-start
  119.8 0.7 fusion.67
  120.5 1.0 copy.82
  121.5 1.7 copy.81
  123.3 1.9 copy.78
  125.2 1.1 subtract_convert_fusion
  126.4 1.1 fusion.41
  127.5 9.3 %all-to-all-done.1 = f32[32,3,4,256]{3,2,1,0:T(4,128)} async-done(((f32[32,3,4,256]{3,2,1,0:T(4,128)}), f32[32,3,4,256]{3,2,1,0:T(4,128)}, u32[]{:S(2)}, u32[]{:S(2)}) %all-to-all-start.1) | async-done | bytes 393248 | tf_op jit(solution)/shard_map/all_to_all | solution.py:215
  136.8 1.8 copy.77
  138.6 1.9 reshape.285
  140.5 1.5 convolution_multiply_fusion
  142.0 2.6 %multiply_reduce_fusion = (f32[256,3]{0,1:T(4,128)S(1)}, f32[256,3,128]{0,2,1:T(8,128)S(1)}) fusion(f32[256,3,128]{0,2,1:T(8,128)} %bitcast.333, f32[256,3,128]{0,2,1:T(8,128)} %bitcast.328, f32[3]{0:T(128)S(1)} %copy-done.37, f32[256,3,128]{0,2,1:T(8,128)S(1)} %convolution_multiply_fusion, f32[256,3]{0,1:T(4,128)S(1)} %copy-done.29, ...), kind=kOutput, calls=%fused_computation.46 | convolution fusion | flops 303955200 | bytes 1909772 | tf_op jit(solution)/shard_map/tsh,shp->thp/dot_general | solution.py:200
  144.8 23.8 %all-gather.4.cloned.1.call-done.kv_ref = bf16[16384,256]{1,0:T(8,128)(2,1)} async-done(((bf16[512,256]{1,0:T(8,128)(2,1)}), bf16[16384,256]{1,0:T(8,128)(2,1)}) %all-gather.4.cloned.1.call-update) | async-done | bytes 8388624 | tf_op jit(solution)/shard_map/all_gather | solution.py:231
  168.6 21.5 %shard_map.211 = bf16[512,128]{1,0:T(8,128)(2,1)S(1)} custom-call(s32[512,1]{1,0:T(8,128)S(1)} %bitcast.323, bf16[512,128]{1,0:T(8,128)(2,1)S(1)} %bitcast.324, s32[1,16384]{1,0:T(1,128)S(1)} %compare_select_fusion.kr_ref, bf16[16384,256]{1,0:T(8,128)(2,1)} %all-gather.4.cloned.1.call-done.kv_ref), custom_call_target="tpu_custom_call" | custom-call | tf_op jit(solution)/shard_map/pallas_call | solution.py:73
  190.2 2.0 fusion.70
  192.2 2.2 fusion.2
  194.5 1.0 copy-done.4
  195.6 0.9 add_bitcast_fusion
  196.4 24.2 %reduce-scatter.2.cloned.1.call-done = bf16[256,768]{1,0:T(8,128)(2,1)} async-done(((bf16[256,3072]{1,0:T(8,128)(2,1)}), bf16[256,768]{1,0:T(8,128)(2,1)}) %reduce-scatter.2.cloned.1.call-update) | async-done | bytes 393232 | tf_op jit(solution)/shard_map/reduce_scatter | solution.py:250
  220.6 2.0 fusion.25
  (156 shorter events, 2.7 us)
Async XLA Ops:
  7.2 185.0 %copy-start = (bf16[384,3072]{1,0:T(8,128)(2,1)S(1)}, bf16[384,3072]{1,0:T(8,128)(2,1)}, u32[]{:S(2)}) copy-start(bf16[384,3072]{1,0:T(8,128)(2,1)} %param.34) | copy-start | bytes 7077892
  7.2 35.5 %all-gather.6.cloned.1.call-start = ((), (), s32[]{:S(2)}) async-start(), calls=%async_computation.5 | async-start | bytes 1966080 | tf_op jit(solution)/shard_map/all_gather | solution.py:152
  7.9 160.7 %all-gather.4.cloned.1.call-start = ((), (), s32[]{:S(2)}) async-start(), calls=%async_computation.3 | async-start | bytes 8650752 | tf_op jit(solution)/shard_map/all_gather | solution.py:231
  11.5 34.9 %copy-start.33 = (f32[64]{0:T(128)}, f32[64]{0:T(128)S(1)}, u32[]{:S(2)}) copy-start(f32[64]{0:T(128)S(1)} %multiply_power_fusion) | copy-start | bytes 772
  11.5 34.9 %copy-start.26 = (f32[256]{0:T(256)}, f32[256]{0:T(256)S(1)}, u32[]{:S(2)}) copy-start(f32[256]{0:T(256)S(1)} %add_convert_fusion.1) | copy-start | bytes 3076
  42.7 1.9 copy-start.2
  44.6 1.1 copy-start.7
  44.7 3.9 %copy-start.36 = (bf16[3072,2,384]{2,1,0:T(2,128)(2,1)S(1)}, bf16[3072,2,384]{2,1,0:T(2,128)(2,1)}, u32[]{:S(2)}) copy-start(bf16[3072,2,384]{2,1,0:T(2,128)(2,1)} %param.25) | copy-start | bytes 14155780
  45.8 8.5 %copy-start.1 = (bf16[256,3072]{1,0:T(8,128)(2,1)}, bf16[256,3072]{1,0:T(8,128)(2,1)S(1)}, u32[]{:S(2)}) copy-start(bf16[256,3072]{1,0:T(8,128)(2,1)S(1)} %fusion.5) | copy-start | bytes 4718596
  45.8 1.9 copy-start.12
  47.1 11.9 %copy-start.9 = (bf16[256,128]{1,0:T(8,128)(2,1)}, bf16[256,128]{1,0:T(8,128)(2,1)S(1)}, u32[]{:S(2)}) copy-start(bf16[256,128]{1,0:T(8,128)(2,1)S(1)} %fusion.53) | copy-start | bytes 196612
  48.3 5.9 %copy-start.14 = (bf16[3072,3]{0,1:T(4,128)(2,1)S(1)}, bf16[3072,3]{0,1:T(4,128)(2,1)}, u32[]{:S(2)}) copy-start(bf16[3072,3]{0,1:T(4,128)(2,1)} %param.27) | copy-start | bytes 55300
  48.3 5.9 %copy-start.35 = (f32[3]{0:T(128)S(1)}, f32[3]{0:T(128)}, u32[]{:S(2)}) copy-start(f32[3]{0:T(128)} %param.28) | copy-start | bytes 40
  48.3 10.6 %collective-permute-start = (bf16[512,128]{1,0:T(8,128)(2,1)}, bf16[512,128]{1,0:T(8,128)(2,1)}, u32[]{:S(2)}, u32[]{:S(2)}) collective-permute-start(bf16[512,128]{1,0:T(8,128)(2,1)} %pad_maximum_fusion.2), channel_id=1, source_target_pairs={{0,2},{2,0},{4,6},{6,4},{1,3},{3,1},{5,7},{7,5},{8,10},{10,8},{12,... | collective-permute-start | bytes 393224 | tf_op jit(solution)/shard_map/ppermute | solution.py:171
  49.9 4.8 %copy-start.11 = (bf16[256,2,384]{2,0,1:T(8,128)(2,1)}, bf16[256,2,384]{2,0,1:T(8,128)(2,1)S(1)}, u32[]{:S(2)}) copy-start(bf16[256,2,384]{2,0,1:T(8,128)(2,1)S(1)} %fusion.7) | copy-start | bytes 1179652
  50.0 6.1 %copy-start.8 = (bf16[3072,128]{1,0:T(8,128)(2,1)S(1)}, bf16[3072,128]{1,0:T(8,128)(2,1)}, u32[]{:S(2)}) copy-start(bf16[3072,128]{1,0:T(8,128)(2,1)} %param.26) | copy-start | bytes 2359300
  50.6 25.2 %collective-permute-start.1 = (bf16[3,384]{1,0:T(4,128)(2,1)}, bf16[3,384]{1,0:T(4,128)(2,1)}, u32[]{:S(2)}, u32[]{:S(2)}) collective-permute-start(bf16[3,384]{1,0:T(4,128)(2,1)} %slice_bitcast_fusion.63), channel_id=1, source_target_pairs={{0,8},{8,16},{16,24},{24,32},{32,40},{40,48},{48,56},{56,64},{64,7... | collective-permute-start | bytes 6920 | tf_op jit(solution)/shard_map/ppermute | solution.py:23
  56.1 3.0 %copy-start.13 = (bf16[1,256,128]{2,1,0:T(8,128)(2,1)S(1)}, bf16[1,256,128]{2,1,0:T(8,128)(2,1)}, u32[]{:S(2)}) copy-start(bf16[1,256,128]{2,1,0:T(8,128)(2,1)} %param.35) | copy-start | bytes 196612
  58.7 17.0 %copy-start.30 = (bf16[1,3,384]{2,1,0:T(4,128)(2,1)S(1)}, bf16[1,3,384]{2,1,0:T(4,128)(2,1)}, u32[]{:S(2)}) copy-start(bf16[1,3,384]{2,1,0:T(4,128)(2,1)} %param.37) | copy-start | bytes 6916
  58.7 17.1 %copy-start.22 = (f32[384]{0:T(512)S(1)}, f32[384]{0:T(512)}, u32[]{:S(2)}) copy-start(f32[384]{0:T(512)} %get-tuple-element.3) | copy-start | bytes 4612
  58.7 17.1 %copy-start.23 = (f32[384]{0:T(512)S(1)}, f32[384]{0:T(512)}, u32[]{:S(2)}) copy-start(f32[384]{0:T(512)} %get-tuple-element.4) | copy-start | bytes 4612
  58.7 17.1 %copy-start.24 = (f32[384]{0:T(512)S(1)}, f32[384]{0:T(512)}, u32[]{:S(2)}) copy-start(f32[384]{0:T(512)} %get-tuple-element.5) | copy-start | bytes 4612
  58.7 17.1 %copy-start.25 = (f32[384]{0:T(512)S(1)}, f32[384]{0:T(512)}, u32[]{:S(2)}) copy-start(f32[384]{0:T(512)} %get-tuple-element.6) | copy-start | bytes 4612
  58.8 17.4 %copy-start.15 = (f32[1,3,2,128]{3,1,2,0:T(4,128)}, f32[1,3,2,128]{3,1,2,0:T(4,128)S(1)}, u32[]{:S(2)}) copy-start(f32[1,3,2,128]{3,1,2,0:T(4,128)S(1)} %copy.107) | copy-start | bytes 9220
  59.0 20.7 %copy-start.31 = (f32[3]{0:T(128)}, f32[3]{0:T(128)S(1)}, u32[]{:S(2)}) copy-start(f32[3]{0:T(128)S(1)} %exp.50) | copy-start | bytes 40
  70.7 6.4 %collective-permute-start.2 = (bf16[3,512]{1,0:T(4,128)(2,1)S(1)}, bf16[3,512]{1,0:T(4,128)(2,1)S(1)}, u32[]{:S(2)}, u32[]{:S(2)}) collective-permute-start(bf16[3,512]{1,0:T(4,128)(2,1)S(1)} %slice.500), channel_id=1, source_target_pairs={{0,8},{8,16},{16,24},{24,32},{32,40},{40,48},{48,56},{56,64},{64,7... | collective-permute-start | bytes 9224 | tf_op jit(solution)/shard_map/ppermute | solution.py:23
  75.7 1.4 copy-start.28
  75.9 1.4 copy-start.18
  75.9 1.4 copy-start.19
  75.9 1.4 copy-start.20
  75.9 1.4 copy-start.21
  77.1 1.0 copy-start.6
  78.6 0.8 copy-start.3
  79.7 11.6 %copy-start.27 = (f32[256]{0:T(256)S(1)}, f32[256]{0:T(256)}, u32[]{:S(2)}) copy-start(f32[256]{0:T(256)} %copy-done.26) | copy-start | bytes 3076
  79.7 11.6 %copy-start.34 = (f32[64]{0:T(128)S(1)}, f32[64]{0:T(128)}, u32[]{:S(2)}) copy-start(f32[64]{0:T(128)} %copy-done.33) | copy-start | bytes 772
  80.8 30.0 %all-to-all-start = ((f32[32,3,5,256]{3,1,2,0:T(4,128)}), f32[32,3,5,256]{3,1,2,0:T(4,128)}, u32[]{:S(2)}, u32[]{:S(2)}) async-start(f32[32,3,5,256]{3,1,2,0:T(4,128)} %pad_maximum_fusion), calls=%async_computation | async-start | bytes 1310720 | tf_op jit(solution)/shard_map/all_to_all | solution.py:208
  110.8 2.2 copy-start.10
  114.5 22.3 %all-to-all-start.1 = ((f32[32,3,4,256]{3,2,1,0:T(4,128)}), f32[32,3,4,256]{3,2,1,0:T(4,128)}, u32[]{:S(2)}, u32[]{:S(2)}) async-start(f32[32,3,4,256]{3,2,1,0:T(4,128)} %copy.76), calls=%async_computation.1 | async-start | bytes 786432 | tf_op jit(solution)/shard_map/all_to_all | solution.py:215
  119.5 101.1 %reduce-scatter.2.cloned.1.call-start = ((), (), s32[]{:S(2)}) async-start(), calls=%async_computation.4 | async-start | bytes 1966080 | tf_op jit(solution)/shard_map/reduce_scatter | solution.py:250
  126.4 15.6 %copy-start.16 = (f32[1,3,2,128]{3,1,2,0:T(4,128)S(1)}, f32[1,3,2,128]{3,1,2,0:T(4,128)}, u32[]{:S(2)}) copy-start(f32[1,3,2,128]{3,1,2,0:T(4,128)} %copy-done.15) | copy-start | bytes 9220
  126.4 15.6 %copy-start.29 = (f32[256,3]{0,1:T(4,128)S(1)}, f32[256,3]{0,1:T(4,128)}, u32[]{:S(2)}) copy-start(f32[256,3]{0,1:T(4,128)} %get-tuple-element.76) | copy-start | bytes 9220
  126.4 15.6 %copy-start.37 = (f32[3]{0:T(128)S(1)}, f32[3]{0:T(128)}, u32[]{:S(2)}) copy-start(f32[3]{0:T(128)} %param.30) | copy-start | bytes 40
  142.0 2.7 %copy-start.17 = (f32[384]{0:T(512)S(1)}, f32[384]{0:T(512)}, u32[]{:S(2)}) copy-start(f32[384]{0:T(512)} %convert_element_type.85) | copy-start | bytes 4612
  194.4 1.0 copy-start.4
  194.5 1.1 copy-start.5
  194.5 1.1 copy-start.32
Sparse Core Ops, SparseCore 0:
  9.8 32.8 all-gather.5
  60.9 107.6 all-gather.3
  194.6 25.9 reduce-scatter.1

commit v8 on v7

--- a/solution.py
+++ b/solution.py
@@ -149,7 +149,16 @@
     seq_pos = lax.axis_index("seq")
     mp_pos = lax.axis_index("mp")
     length = cache_len[0]
-    whole = lax.all_gather(own_rows, "mp", axis=1, tiled=True)
+    mp_count = lax.axis_size("mp")
+    width = own_rows.shape[1]
+    whole = jnp.zeros((tokens, mp_count * width), own_rows.dtype)
+    for shift in range(mp_count):
+        if shift == 0:
+            part = own_rows
+        else:
+            part = lax.ppermute(own_rows, "mp", [(i, (i + shift) % mp_count) for i in range(mp_count)])
+        source = (lax.axis_index("mp") + mp_count - shift) % mp_count
+        whole = lax.dynamic_update_slice(whole, part, (0, source * width))
     normed = (rms_scale(whole.astype(jnp.float32)) * norm_gain.astype(jnp.float32)).astype(
         jnp.bfloat16
     )

time: 230 us -> 222 us (0.965)
  waiting for transfers between devices: 102 us -> 81.1 us
  starting transfers between devices: 20.9 us -> 29.1 us
  local copies, waits for them, and re-layouts: 20.4 us -> 25.2 us
    all_gather x1 -> x0, waiting for transfers between devices: 28.2 us -> none  [shards(): whole = lax.all_gather(own_rows, 'mp', axis=1, tiled=True)]
    ppermute x0 -> x3, waiting for transfers between devices: none -> 8.31 us  [shards(): lax.ppermute(own_rows, 'mp', [(i, (i + shift) % mp_count) for i in range(...]
    ppermute x0 -> x3, starting transfers between devices: none -> 5.72 us  [shards(): lax.ppermute(own_rows, 'mp', [(i, (i + shift) % mp_count) for i in range(...]
    dynamic_update_slice x0 -> x4, local copies, waits for them, and re-layouts: none -> 5.3 us  [shards(): whole = lax.dynamic_update_slice(whole, part, (0, source * width))]
    unnamed x83 -> x91, local copies, waits for them, and re-layouts: 7.27 us -> 6.1 us
  transfers between devices with their start and end apart: 8 -> 10, of which waited for: 5 -> 5; matrix products, arithmetic and copies ran while one was open for 20% -> 22% of each run, Pallas kernels for 0% -> 0%
where the time goes in v8:
time: 222 us; the launch traced here: 221 us
  waiting for transfers between devices  81.1 us (37%)
  starting transfers between devices  29.1 us (13%)
  local copies, waits for them, and re-layouts  25.2 us (11%)
  Pallas kernels  21.5 us (10%)
  other arithmetic  20.9 us (9%)
  matrix products  17.8 us (8%)
  between operations  15.7 us (7%)
  blocking collectives  9.32 us (4%)
    all_gather x1, waiting for transfers between devices, shards(): piece = lax.all_gather(group_rows, 'seq', axis=0, tiled=True)  24.5 us
    reduce_scatter x1, waiting for transfers between devices, shards(): lax.psum_scatter(term.astype(jnp.bfloat16), 'mp', scatter_dimension=1, ti...  24.1 us
    pallas_call x1, Pallas kernels, attend(): pl.pallas_call(kernel, grid=(steps,), in_specs=[pl.BlockSpec((rows, 1), l...  21.5 us
    all_to_all x1, waiting for transfers between devices, shards(): lax.all_to_all(jnp.concatenate([pieces, decays], axis=2), 'seq', 0, 0, ti...  14.8 us
    all_to_all x1, starting transfers between devices, shards(): lax.all_to_all(jnp.concatenate([pieces, decays], axis=2), 'seq', 0, 0, ti...  11.1 us
    all_to_all x1, waiting for transfers between devices, shards(): lax.all_to_all(jnp.stack(entering, axis=0), 'seq', 0, 0, tiled=True)  9.38 us
    all_gather x1, blocking collectives, shards(): bc_all = lax.all_gather(bc_block, 'mp', axis=1, tiled=True)  9.32 us
    ppermute x3, waiting for transfers between devices, shards(): lax.ppermute(own_rows, 'mp', [(i, (i + shift) % mp_count) for i in range(...  8.31 us
  transfers between devices with their start and end apart: 10, of which 5 were waited for; matrix products, arithmetic and copies ran while one was open for 22% of the time, Pallas kernels for 0%

profile of v8, /device:TPU:1, one launch (start us, length us, event | category | flops | bytes accessed | tf_op | source)
XLA Modules:
  0.0 220.6 jit_solution(7198865463694522103)
XLA Ops:
  7.3 2.1 collective-permute-start
  9.4 2.5 %collective-permute-start.1 = (bf16[256,768]{1,0:T(8,128)(2,1)}, bf16[256,768]{1,0:T(8,128)(2,1)}, u32[]{:S(2)}, u32[]{:S(2)}) collective-permute-start(bf16[256,768]{1,0:T(8,128)(2,1)} %bitcast.327), channel_id=1, source_target_pairs={{0,4},{2,6},{4,0},{6,2},{1,5},{3,7},{5,1},{7,3},{8,12},{10,14},{12... | collective-permute-start | bytes 1179656 | tf_op jit(solution)/shard_map/ppermute | solution.py:159
  11.8 1.2 collective-permute-start.2
  13.8 1.4 slice_convert_fusion.4
  15.2 1.4 broadcast_in_dim.30
  16.6 0.8 constant_dynamic-update-slice_fusion.35
  17.8 0.6 convert_element_type.85
  18.4 0.6 convert_reduce_fusion.3
  19.0 1.8 constant_dynamic-update-slice_fusion.34
  20.8 8.3 %collective-permute-done.1 = bf16[256,768]{1,0:T(8,128)(2,1)} collective-permute-done((bf16[256,768]{1,0:T(8,128)(2,1)}, bf16[256,768]{1,0:T(8,128)(2,1)}, u32[]{:S(2)}, u32[]{:S(2)}) %collective-permute-start.1) | collective-permute-done | bytes 393248 | tf_op jit(solution)/shard_map/ppermute | solution.py:159
  29.1 1.8 constant_dynamic-update-slice_fusion.33
  30.9 0.8 constant_dynamic-update-slice_fusion.32
  31.8 1.8 fusion.3
  33.6 2.0 fusion.5
  35.7 0.6 fusion.68
  36.3 0.6 fusion.49
  37.0 0.7 pad_maximum_fusion.2
  37.7 1.5 fusion.7
  39.2 0.6 slice_bitcast_fusion.63
  39.8 3.8 %collective-permute-start.4 = (bf16[3,384]{1,0:T(4,128)(2,1)}, bf16[3,384]{1,0:T(4,128)(2,1)}, u32[]{:S(2)}, u32[]{:S(2)}) collective-permute-start(bf16[3,384]{1,0:T(4,128)(2,1)} %slice_bitcast_fusion.63), channel_id=1, source_target_pairs={{0,8},{8,16},{16,24},{24,32},{32,40},{40,48},{48,56},{56,64},{64,7... | collective-permute-start | bytes 6920 | tf_op jit(solution)/shard_map/ppermute | solution.py:23
  43.5 0.5 fusion.59
  44.1 0.9 reduce-window.6
  45.4 2.6 %convolution_convert_fusion = bf16[256,128]{1,0:T(8,128)(2,1)} fusion(bf16[256,3072]{1,0:T(8,128)(2,1)} %copy-done.1, bf16[3072,128]{1,0:T(8,128)(2,1)S(1)} %copy-done.8), kind=kOutput, calls=%fused_computation.16 | convolution fusion | flops 201359360 | bytes 2424832 | tf_op jit(solution)/shard_map/dot_general | solution.py:176
  48.3 1.8 maximum_select_fusion
  50.1 9.3 %all_gather.7 = bf16[256,512]{1,0:T(8,128)(2,1)S(1)} all-gather(bf16[256,128]{1,0:T(8,128)(2,1)} %convolution_convert_fusion), channel_id=1, replica_groups=mesh['seq'=32,'mp'=4,'req'=2] {'mp'}, dimensions={1}, use_global_device_ids=true | all-gather | bytes 327680 | tf_op jit(solution)/shard_map/all_gather | solution.py:177
  59.4 2.6 %collective-permute-start.5 = (bf16[3,512]{1,0:T(4,128)(2,1)S(1)}, bf16[3,512]{1,0:T(4,128)(2,1)S(1)}, u32[]{:S(2)}, u32[]{:S(2)}) collective-permute-start(bf16[3,512]{1,0:T(4,128)(2,1)S(1)} %slice.500), channel_id=1, source_target_pairs={{0,8},{8,16},{16,24},{24,32},{32,40},{40,48},{48,56},{56,64},{64,7... | collective-permute-start | bytes 9224 | tf_op jit(solution)/shard_map/ppermute | solution.py:23
  62.1 1.8 slice_convert_fusion
  63.9 0.6 compare_select_fusion.1
  64.9 0.9 copy.71
  66.0 0.3 divide_multiply_fusion
  66.3 0.5 copy-done.5
  66.9 0.5 fusion.29
  67.4 0.8 copy-done.2
  68.1 0.3 copy.80
  68.5 1.0 pad_maximum_fusion
  69.5 11.1 %all-to-all-start = ((f32[32,3,5,256]{3,1,2,0:T(4,128)}), f32[32,3,5,256]{3,1,2,0:T(4,128)}, u32[]{:S(2)}, u32[]{:S(2)}) async-start(f32[32,3,5,256]{3,1,2,0:T(4,128)} %pad_maximum_fusion), calls=%async_computation | async-start | bytes 1310720 | tf_op jit(solution)/shard_map/all_to_all | solution.py:217
  80.6 0.8 constant_dynamic-slice_fusion
  81.4 0.6 constant_dynamic-update-slice_fusion.31
  82.0 1.2 multiply_cosine_fusion.1
  83.2 2.6 %fusion.67 = f32[256,256]{0,1:T(8,128)S(1)} fusion(bf16[256,3072]{1,0:T(8,128)(2,1)} %copy-done.1, bf16[3072,256]{1,0:T(8,128)(2,1)} %param.22), kind=kOutput, calls=%fused_computation.262 | convolution fusion | flops 402653184 | bytes 3407872 | tf_op jit(solution)/shard_map/dot_general | solution.py:168
  85.9 14.8 %all-to-all-done = f32[32,3,5,256]{3,1,2,0:T(4,128)} async-done(((f32[32,3,5,256]{3,1,2,0:T(4,128)}), f32[32,3,5,256]{3,1,2,0:T(4,128)}, u32[]{:S(2)}, u32[]{:S(2)}) %all-to-all-start) | async-done | bytes 491552 | tf_op jit(solution)/shard_map/all_to_all | solution.py:217
  100.7 1.0 slice_bitcast_fusion.1
  101.7 0.9 slice_bitcast_fusion.20
  103.5 0.9 copy.76
  104.4 5.8 %all-to-all-start.1 = ((f32[32,3,4,256]{3,2,1,0:T(4,128)}), f32[32,3,4,256]{3,2,1,0:T(4,128)}, u32[]{:S(2)}, u32[]{:S(2)}) async-start(f32[32,3,4,256]{3,2,1,0:T(4,128)} %copy.76), calls=%async_computation.1 | async-start | bytes 786432 | tf_op jit(solution)/shard_map/all_to_all | solution.py:224
  110.2 0.7 fusion.66
  110.9 1.0 copy.82
  111.9 1.7 copy.81
  113.7 1.9 copy.78
  115.6 1.1 subtract_convert_fusion
  116.8 1.1 fusion.40
  118.0 9.4 %all-to-all-done.1 = f32[32,3,4,256]{3,2,1,0:T(4,128)} async-done(((f32[32,3,4,256]{3,2,1,0:T(4,128)}), f32[32,3,4,256]{3,2,1,0:T(4,128)}, u32[]{:S(2)}, u32[]{:S(2)}) %all-to-all-start.1) | async-done | bytes 393248 | tf_op jit(solution)/shard_map/all_to_all | solution.py:224
  127.3 1.8 copy.77
  129.1 1.9 reshape.285
  131.0 1.5 convolution_multiply_fusion
  132.5 2.6 %multiply_reduce_fusion = (f32[256,3]{0,1:T(4,128)S(1)}, f32[256,3,128]{0,2,1:T(8,128)S(1)}) fusion(f32[256,3,128]{0,2,1:T(8,128)} %bitcast.332, f32[256,3,128]{0,2,1:T(8,128)} %bitcast.324, f32[3]{0:T(128)S(1)} %copy-done.41, f32[256,3,128]{0,2,1:T(8,128)S(1)} %convolution_multiply_fusion, f32[256,3]{0,1:T(4,128)S(1)} %copy-done.31, ...), kind=kOutput, calls=%fused_computation.45 | convolution fusion | flops 303955200 | bytes 1909772 | tf_op jit(solution)/shard_map/tsh,shp->thp/dot_general | solution.py:209
  135.3 24.5 %all-gather.2.cloned.1.call-done.kv_ref = bf16[16384,256]{1,0:T(8,128)(2,1)} async-done(((bf16[512,256]{1,0:T(8,128)(2,1)}), bf16[16384,256]{1,0:T(8,128)(2,1)}) %all-gather.2.cloned.1.call-update) | async-done | bytes 8388624 | tf_op jit(solution)/shard_map/all_gather | solution.py:240
  159.8 21.5 %shard_map.211 = bf16[512,128]{1,0:T(8,128)(2,1)S(1)} custom-call(s32[512,1]{1,0:T(8,128)S(1)} %bitcast.319, bf16[512,128]{1,0:T(8,128)(2,1)S(1)} %bitcast.320, s32[1,16384]{1,0:T(1,128)S(1)} %compare_select_fusion.kr_ref, bf16[16384,256]{1,0:T(8,128)(2,1)} %all-gather.2.cloned.1.call-done.kv_ref), custom_call_target="tpu_custom_call" | custom-call | tf_op jit(solution)/shard_map/pallas_call | solution.py:73
  181.4 2.0 fusion.69
  183.4 2.3 %fusion.2 = bf16[256,3072]{1,0:T(8,128)(2,1)} fusion(f32[256,3072]{1,0:T(8,128)S(1)} %fusion.69, bf16[256,384]{0,1:T(8,128)(2,1)S(1)} %fusion.28, bf16[384,3072]{1,0:T(8,128)(2,1)S(1)} %copy-done), kind=kOutput, calls=%fused_computation.5 | convolution fusion | flops 605552640 | bytes 7274496 | tf_op jit(solution)/shard_map/dot_general | solution.py:258
  185.7 1.0 copy-done.3
  186.8 0.9 add_bitcast_fusion
  187.6 24.1 %reduce-scatter.2.cloned.1.call-done = bf16[256,768]{1,0:T(8,128)(2,1)} async-done(((bf16[256,3072]{1,0:T(8,128)(2,1)}), bf16[256,768]{1,0:T(8,128)(2,1)}) %reduce-scatter.2.cloned.1.call-update) | async-done | bytes 393232 | tf_op jit(solution)/shard_map/reduce_scatter | solution.py:259
  211.8 2.0 fusion.24
  (172 shorter events, 3.0 us)
Async XLA Ops:
  7.2 176.2 %copy-start = (bf16[384,3072]{1,0:T(8,128)(2,1)S(1)}, bf16[384,3072]{1,0:T(8,128)(2,1)}, u32[]{:S(2)}) copy-start(bf16[384,3072]{1,0:T(8,128)(2,1)} %param.34) | copy-start | bytes 7077892
  7.2 9.4 %copy-start.6 = (bf16[1,256,768]{2,1,0:T(8,128)(2,1)S(1)}, bf16[1,256,768]{2,1,0:T(8,128)(2,1)}, u32[]{:S(2)}) copy-start(bf16[1,256,768]{2,1,0:T(8,128)(2,1)} %param.20) | copy-start | bytes 1179652
  7.2 10.5 %copy-start.27 = (bf16[3072]{0:T(1024)(128)(2,1)S(1)}, bf16[3072]{0:T(1024)(128)(2,1)}, u32[]{:S(2)}) copy-start(bf16[3072]{0:T(1024)(128)(2,1)} %param.21) | copy-start | bytes 18436
  7.2 10.5 %copy-start.40 = (f32[3]{0:T(128)S(1)}, f32[3]{0:T(128)}, u32[]{:S(2)}) copy-start(f32[3]{0:T(128)} %param.29) | copy-start | bytes 40
  7.2 10.5 %copy-start.37 = (bf16[384]{0:T(512)(128)(2,1)S(1)}, bf16[384]{0:T(512)(128)(2,1)}, u32[]{:S(2)}) copy-start(bf16[384]{0:T(512)(128)(2,1)} %param.33) | copy-start | bytes 2308
  7.2 11.1 %copy-start.15 = (bf16[4,384]{1,0:T(4,128)(2,1)S(1)}, bf16[4,384]{1,0:T(4,128)(2,1)}, u32[]{:S(2)}) copy-start(bf16[4,384]{1,0:T(4,128)(2,1)} %param.31) | copy-start | bytes 9220
  7.2 152.5 %all-gather.2.cloned.1.call-start = ((), (), s32[]{:S(2)}) async-start(), calls=%async_computation.3 | async-start | bytes 8650752 | tf_op jit(solution)/shard_map/all_gather | solution.py:240
  7.3 11.7 %collective-permute-start = (bf16[256,768]{1,0:T(8,128)(2,1)}, bf16[256,768]{1,0:T(8,128)(2,1)}, u32[]{:S(2)}, u32[]{:S(2)}) collective-permute-start(bf16[256,768]{1,0:T(8,128)(2,1)} %bitcast.326), channel_id=1, source_target_pairs={{0,2},{2,4},{4,6},{6,0},{1,3},{3,5},{5,7},{7,1},{8,10},{10,12},{12... | collective-permute-start | bytes 1179656 | tf_op jit(solution)/shard_map/ppermute | solution.py:159
  9.4 19.7 %collective-permute-start.1 = (bf16[256,768]{1,0:T(8,128)(2,1)}, bf16[256,768]{1,0:T(8,128)(2,1)}, u32[]{:S(2)}, u32[]{:S(2)}) collective-permute-start(bf16[256,768]{1,0:T(8,128)(2,1)} %bitcast.327), channel_id=1, source_target_pairs={{0,4},{2,6},{4,0},{6,2},{1,5},{3,7},{5,1},{7,3},{8,12},{10,14},{12... | collective-permute-start | bytes 1179656 | tf_op jit(solution)/shard_map/ppermute | solution.py:159
  11.8 19.1 %collective-permute-start.2 = (bf16[256,768]{1,0:T(8,128)(2,1)}, bf16[256,768]{1,0:T(8,128)(2,1)S(1)}, u32[]{:S(2)}, u32[]{:S(2)}) collective-permute-start(bf16[256,768]{1,0:T(8,128)(2,1)} %bitcast.328), channel_id=1, source_target_pairs={{0,6},{2,0},{4,2},{6,4},{1,7},{3,1},{5,3},{7,5},{8,14},{10,8},{12,... | collective-permute-start | bytes 1179656 | tf_op jit(solution)/shard_map/ppermute | solution.py:159
  17.5 18.8 %copy-start.28 = (f32[256]{0:T(256)}, f32[256]{0:T(256)S(1)}, u32[]{:S(2)}) copy-start(f32[256]{0:T(256)S(1)} %add_convert_fusion.2) | copy-start | bytes 3076
  17.5 18.8 %copy-start.35 = (f32[64]{0:T(128)}, f32[64]{0:T(128)S(1)}, u32[]{:S(2)}) copy-start(f32[64]{0:T(128)S(1)} %multiply_power_fusion) | copy-start | bytes 772
  33.6 2.1 copy-start.7
  33.6 4.1 %copy-start.39 = (bf16[3072,2,384]{2,1,0:T(2,128)(2,1)S(1)}, bf16[3072,2,384]{2,1,0:T(2,128)(2,1)}, u32[]{:S(2)}) copy-start(bf16[3072,2,384]{2,1,0:T(2,128)(2,1)} %param.25) | copy-start | bytes 14155780
  35.6 7.9 %copy-start.1 = (bf16[256,3072]{1,0:T(8,128)(2,1)}, bf16[256,3072]{1,0:T(8,128)(2,1)S(1)}, u32[]{:S(2)}) copy-start(bf16[256,3072]{1,0:T(8,128)(2,1)S(1)} %fusion.5) | copy-start | bytes 4718596
  35.7 1.3 copy-start.12
  37.0 11.3 %copy-start.9 = (bf16[256,128]{1,0:T(8,128)(2,1)}, bf16[256,128]{1,0:T(8,128)(2,1)S(1)}, u32[]{:S(2)}) copy-start(bf16[256,128]{1,0:T(8,128)(2,1)S(1)} %fusion.52) | copy-start | bytes 196612
  37.6 5.9 %copy-start.14 = (bf16[3072,3]{0,1:T(4,128)(2,1)S(1)}, bf16[3072,3]{0,1:T(4,128)(2,1)}, u32[]{:S(2)}) copy-start(bf16[3072,3]{0,1:T(4,128)(2,1)} %param.27) | copy-start | bytes 55300
  37.6 5.9 %copy-start.38 = (f32[3]{0:T(128)S(1)}, f32[3]{0:T(128)}, u32[]{:S(2)}) copy-start(f32[3]{0:T(128)} %param.28) | copy-start | bytes 40
  37.6 10.6 %collective-permute-start.3 = (bf16[512,128]{1,0:T(8,128)(2,1)}, bf16[512,128]{1,0:T(8,128)(2,1)}, u32[]{:S(2)}, u32[]{:S(2)}) collective-permute-start(bf16[512,128]{1,0:T(8,128)(2,1)} %pad_maximum_fusion.2), channel_id=1, source_target_pairs={{0,2},{2,0},{4,6},{6,4},{1,3},{3,1},{5,7},{7,5},{8,10},{10,8},{12,... | collective-permute-start | bytes 393224 | tf_op jit(solution)/shard_map/ppermute | solution.py:180
  39.1 5.0 %copy-start.11 = (bf16[256,2,384]{2,0,1:T(8,128)(2,1)}, bf16[256,2,384]{2,0,1:T(8,128)(2,1)S(1)}, u32[]{:S(2)}) copy-start(bf16[256,2,384]{2,0,1:T(8,128)(2,1)S(1)} %fusion.7) | copy-start | bytes 1179652
  39.1 6.2 %copy-start.8 = (bf16[3072,128]{1,0:T(8,128)(2,1)S(1)}, bf16[3072,128]{1,0:T(8,128)(2,1)}, u32[]{:S(2)}) copy-start(bf16[3072,128]{1,0:T(8,128)(2,1)} %param.26) | copy-start | bytes 2359300
  39.8 24.7 %collective-permute-start.4 = (bf16[3,384]{1,0:T(4,128)(2,1)}, bf16[3,384]{1,0:T(4,128)(2,1)}, u32[]{:S(2)}, u32[]{:S(2)}) collective-permute-start(bf16[3,384]{1,0:T(4,128)(2,1)} %slice_bitcast_fusion.63), channel_id=1, source_target_pairs={{0,8},{8,16},{16,24},{24,32},{32,40},{40,48},{48,56},{56,64},{64,7... | collective-permute-start | bytes 6920 | tf_op jit(solution)/shard_map/ppermute | solution.py:23
  45.4 3.0 %copy-start.13 = (bf16[1,256,128]{2,1,0:T(8,128)(2,1)S(1)}, bf16[1,256,128]{2,1,0:T(8,128)(2,1)}, u32[]{:S(2)}) copy-start(bf16[1,256,128]{2,1,0:T(8,128)(2,1)} %param.35) | copy-start | bytes 196612
  48.0 16.5 %copy-start.32 = (bf16[1,3,384]{2,1,0:T(4,128)(2,1)S(1)}, bf16[1,3,384]{2,1,0:T(4,128)(2,1)}, u32[]{:S(2)}) copy-start(bf16[1,3,384]{2,1,0:T(4,128)(2,1)} %param.37) | copy-start | bytes 6916
  48.0 16.6 %copy-start.23 = (f32[384]{0:T(512)S(1)}, f32[384]{0:T(512)}, u32[]{:S(2)}) copy-start(f32[384]{0:T(512)} %get-tuple-element.3) | copy-start | bytes 4612
  48.0 16.6 %copy-start.24 = (f32[384]{0:T(512)S(1)}, f32[384]{0:T(512)}, u32[]{:S(2)}) copy-start(f32[384]{0:T(512)} %get-tuple-element.4) | copy-start | bytes 4612
  48.0 16.6 %copy-start.25 = (f32[384]{0:T(512)S(1)}, f32[384]{0:T(512)}, u32[]{:S(2)}) copy-start(f32[384]{0:T(512)} %get-tuple-element.5) | copy-start | bytes 4612
  48.0 16.6 %copy-start.26 = (f32[384]{0:T(512)S(1)}, f32[384]{0:T(512)}, u32[]{:S(2)}) copy-start(f32[384]{0:T(512)} %get-tuple-element.6) | copy-start | bytes 4612
  48.1 16.8 %copy-start.16 = (f32[1,3,2,128]{3,1,2,0:T(4,128)}, f32[1,3,2,128]{3,1,2,0:T(4,128)S(1)}, u32[]{:S(2)}) copy-start(f32[1,3,2,128]{3,1,2,0:T(4,128)S(1)} %copy.107) | copy-start | bytes 9220
  48.3 20.1 %copy-start.33 = (f32[3]{0:T(128)}, f32[3]{0:T(128)S(1)}, u32[]{:S(2)}) copy-start(f32[3]{0:T(128)S(1)} %exp.50) | copy-start | bytes 40
  59.4 6.4 %collective-permute-start.5 = (bf16[3,512]{1,0:T(4,128)(2,1)S(1)}, bf16[3,512]{1,0:T(4,128)(2,1)S(1)}, u32[]{:S(2)}, u32[]{:S(2)}) collective-permute-start(bf16[3,512]{1,0:T(4,128)(2,1)S(1)} %slice.500), channel_id=1, source_target_pairs={{0,8},{8,16},{16,24},{24,32},{32,40},{40,48},{48,56},{56,64},{64,7... | collective-permute-start | bytes 9224 | tf_op jit(solution)/shard_map/ppermute | solution.py:23
  64.5 1.3 copy-start.30
  64.6 1.3 copy-start.19
  64.6 1.3 copy-start.20
  64.6 1.3 copy-start.21
  64.7 1.3 copy-start.22
  65.9 1.0 copy-start.5
  67.4 0.8 copy-start.2
  68.4 13.6 %copy-start.29 = (f32[256]{0:T(256)S(1)}, f32[256]{0:T(256)}, u32[]{:S(2)}) copy-start(f32[256]{0:T(256)} %copy-done.28) | copy-start | bytes 3076
  68.4 13.6 %copy-start.36 = (f32[64]{0:T(128)S(1)}, f32[64]{0:T(128)}, u32[]{:S(2)}) copy-start(f32[64]{0:T(128)} %copy-done.35) | copy-start | bytes 772
  69.5 31.1 %all-to-all-start = ((f32[32,3,5,256]{3,1,2,0:T(4,128)}), f32[32,3,5,256]{3,1,2,0:T(4,128)}, u32[]{:S(2)}, u32[]{:S(2)}) async-start(f32[32,3,5,256]{3,1,2,0:T(4,128)} %pad_maximum_fusion), calls=%async_computation | async-start | bytes 1310720 | tf_op jit(solution)/shard_map/all_to_all | solution.py:217
  100.7 2.2 copy-start.10
  104.4 23.0 %all-to-all-start.1 = ((f32[32,3,4,256]{3,2,1,0:T(4,128)}), f32[32,3,4,256]{3,2,1,0:T(4,128)}, u32[]{:S(2)}, u32[]{:S(2)}) async-start(f32[32,3,4,256]{3,2,1,0:T(4,128)} %copy.76), calls=%async_computation.1 | async-start | bytes 786432 | tf_op jit(solution)/shard_map/all_to_all | solution.py:224
  110.1 101.7 %reduce-scatter.2.cloned.1.call-start = ((), (), s32[]{:S(2)}) async-start(), calls=%async_computation.4 | async-start | bytes 1966080 | tf_op jit(solution)/shard_map/reduce_scatter | solution.py:259
  116.8 15.7 %copy-start.17 = (f32[1,3,2,128]{3,1,2,0:T(4,128)S(1)}, f32[1,3,2,128]{3,1,2,0:T(4,128)}, u32[]{:S(2)}) copy-start(f32[1,3,2,128]{3,1,2,0:T(4,128)} %copy-done.16) | copy-start | bytes 9220
  116.8 15.7 %copy-start.31 = (f32[256,3]{0,1:T(4,128)S(1)}, f32[256,3]{0,1:T(4,128)}, u32[]{:S(2)}) copy-start(f32[256,3]{0,1:T(4,128)} %get-tuple-element.76) | copy-start | bytes 9220
  116.8 15.7 %copy-start.41 = (f32[3]{0:T(128)S(1)}, f32[3]{0:T(128)}, u32[]{:S(2)}) copy-start(f32[3]{0:T(128)} %param.30) | copy-start | bytes 40
  132.5 2.6 %copy-start.18 = (f32[384]{0:T(512)S(1)}, f32[384]{0:T(512)}, u32[]{:S(2)}) copy-start(f32[384]{0:T(512)} %convert_element_type.85) | copy-start | bytes 4612
  185.7 1.0 copy-start.3
  185.7 1.1 copy-start.4
  185.7 1.1 copy-start.34
Sparse Core Ops, SparseCore 0:
  50.2 109.5 all-gather.1
  185.8 25.9 reduce-scatter.1

commit v9 on v8

--- a/solution.py
+++ b/solution.py
@@ -170,20 +170,26 @@
         ),
         positions,
     ).astype(jnp.bfloat16)
-    projected = jnp.dot(normed, w_keyval, preferred_element_type=jnp.float32)
-    roped = rotate(projected[:, None, :], positions)[:, 0, :]
-    kv_block = jnp.where(mp_pos % 2 == 0, roped, projected).astype(jnp.bfloat16)
+    mp_size = lax.axis_size("mp")
+    pairs_of = [(i, i ^ 1) for i in range(mp_size)]
+    is_key_block = mp_pos % 2 == 0
+
+    def paired(own):
+        other = lax.ppermute(own, "mp", pairs_of)
+        return jnp.where(
+            is_key_block,
+            jnp.concatenate([own, other], axis=1),
+            jnp.concatenate([other, own], axis=1),
+        )
+
+    cache_pair = paired(cache[0])
+    projected = jnp.dot(normed, paired(w_keyval), preferred_element_type=jnp.float32)
+    roped = rotate(projected[:, None, :HD], positions)[:, 0, :]
+    kv_pair = jnp.concatenate([roped, projected[:, HD:]], axis=1).astype(jnp.bfloat16)
+    kv_block = jnp.where(is_key_block, kv_pair[:, :HD], kv_pair[:, HD:])
+    group_rows = jnp.concatenate([cache_pair, kv_pair], axis=0)
     bc_block = jnp.dot(normed, w_bc, preferred_element_type=jnp.float32).astype(jnp.bfloat16)
     bc_all = lax.all_gather(bc_block, "mp", axis=1, tiled=True)
-    own_rows_kv = jnp.concatenate([cache[0], kv_block], axis=0)
-    mp_size = lax.axis_size("mp")
-    partner = lax.ppermute(own_rows_kv, "mp", [(i, i ^ 1) for i in range(mp_size)])
-    is_key_block = mp_pos % 2 == 0
-    group_rows = jnp.where(
-        is_key_block,
-        jnp.concatenate([own_rows_kv, partner], axis=1),
-        jnp.concatenate([partner, own_rows_kv], axis=1),
-    )
     inner = jnp.einsum("td,dkc->tkc", normed, w_inner, preferred_element_type=jnp.float32).astype(
         jnp.bfloat16
     )

time: 222 us -> 248 us (1.12)
  waiting for transfers between devices: 81.1 us -> 97.3 us
  matrix products: 17.8 us -> 24.1 us
  starting transfers between devices: 29.1 us -> 31.9 us
    ppermute x1 -> x2, waiting for transfers between devices: 0.01 us -> 23.1 us  [paired(): other = lax.ppermute(own, 'mp', pairs_of)]
    ppermute x3, waiting for transfers between devices: 8.31 us -> 0.01 us  [shards(): lax.ppermute(own_rows, 'mp', [(i, (i + shift) % mp_count) for i in range(...]
    dot_general x1, matrix products: 1.47 us -> 4.35 us  [shards(): jnp.einsum('td,dkc->tkc', normed, w_inner, preferred_element_type=jnp.flo...]
    unnamed x91 -> x75, local copies, waits for them, and re-layouts: 6.1 us -> 7.28 us
  transfers between devices with their start and end apart: 10 -> 11, of which waited for: 5 -> 5; matrix products, arithmetic and copies ran while one was open for 22% -> 24% of each run, Pallas kernels for 0% -> 0%
where the time goes in v9:
time: 248 us; the launch traced here: 247 us
  waiting for transfers between devices  97.3 us (39%)
  starting transfers between devices  31.9 us (13%)
  local copies, waits for them, and re-layouts  26.4 us (11%)
  matrix products  24.1 us (10%)
  Pallas kernels  21.5 us (9%)
  other arithmetic  19.5 us (8%)
  between operations  15.6 us (6%)
  blocking collectives  10.5 us (4%)
    all_gather x1, waiting for transfers between devices, shards(): piece = lax.all_gather(group_rows, 'seq', axis=0, tiled=True)  25.3 us
    reduce_scatter x1, waiting for transfers between devices, shards(): lax.psum_scatter(term.astype(jnp.bfloat16), 'mp', scatter_dimension=1, ti...  24.2 us
    ppermute x2, waiting for transfers between devices, paired(): other = lax.ppermute(own, 'mp', pairs_of)  23.1 us
    pallas_call x1, Pallas kernels, attend(): pl.pallas_call(kernel, grid=(steps,), in_specs=[pl.BlockSpec((rows, 1), l...  21.5 us
    all_to_all x1, waiting for transfers between devices, shards(): lax.all_to_all(jnp.concatenate([pieces, decays], axis=2), 'seq', 0, 0, ti...  15.1 us
    all_gather x1, blocking collectives, shards(): bc_all = lax.all_gather(bc_block, 'mp', axis=1, tiled=True)  10.5 us
    all_to_all x1, starting transfers between devices, shards(): lax.all_to_all(jnp.concatenate([pieces, decays], axis=2), 'seq', 0, 0, ti...  10.4 us
    all_to_all x1, waiting for transfers between devices, shards(): lax.all_to_all(jnp.stack(entering, axis=0), 'seq', 0, 0, tiled=True)  9.6 us
  transfers between devices with their start and end apart: 11, of which 5 were waited for; matrix products, arithmetic and copies ran while one was open for 24% of the time, Pallas kernels for 0%

profile of v9, /device:TPU:1, one launch (start us, length us, event | category | flops | bytes accessed | tf_op | source)
XLA Modules:
  0.0 246.8 jit_solution(14272232139504636088)
XLA Ops:
  7.3 2.1 collective-permute-start
  9.4 2.5 collective-permute-start.1
  11.8 1.2 collective-permute-start.2
  13.3 1.2 collective-permute-start.3
  15.3 1.4 slice_convert_fusion.5
  16.7 1.4 broadcast_in_dim.30
  18.1 0.8 constant_dynamic-update-slice_fusion.35
  18.9 0.6 convert_reduce_fusion.3
  19.7 0.7 convert_element_type.73
  20.4 0.7 exp.44
  21.1 0.6 convert_element_type.82
  21.7 23.1 %collective-permute-done.3 = bf16[256,128]{1,0:T(8,128)(2,1)} collective-permute-done((bf16[256,128]{1,0:T(8,128)(2,1)}, bf16[256,128]{1,0:T(8,128)(2,1)}, u32[]{:S(2)}, u32[]{:S(2)}) %collective-permute-start.3) | collective-permute-done | bytes 65568 | tf_op jit(solution)/shard_map/ppermute | solution.py:178
  44.7 0.9 maximum_select_fusion.2
  45.7 1.8 constant_dynamic-update-slice_fusion.34
  47.5 1.8 constant_dynamic-update-slice_fusion.33
  49.3 0.8 constant_dynamic-update-slice_fusion.32
  50.1 1.8 fusion.3
  52.0 4.3 %fusion.14 = bf16[256,2,384]{2,0,1:T(8,128)(2,1)S(1)} fusion(bf16[3072,2,384]{2,1,0:T(2,128)(2,1)} %param.25, bf16[256,3072]{1,0:T(8,128)(2,1)} %constant_dynamic-update-slice_fusion.32, f32[3072]{0:T(1024)S(1)} %convert_element_type.73, f32[256]{0:T(256)S(1)} %add_rsqrt_fusion.1), kind=kOutput, calls=%fused_computation.18 | convolution fusion | flops 1211301888 | bytes 6697984 | tf_op jit(solution)/shard_map/td,dkc->tkc/dot_general | solution.py:193
  56.3 0.7 copy-done.7
  57.1 5.1 %collective-permute-start.5 = (bf16[3,384]{1,0:T(4,128)(2,1)S(1)}, bf16[3,384]{1,0:T(4,128)(2,1)S(1)}, u32[]{:S(2)}, u32[]{:S(2)}) collective-permute-start(bf16[3,384]{1,0:T(4,128)(2,1)S(1)} %slice_bitcast_fusion.64), channel_id=1, source_target_pairs={{0,8},{8,16},{16,24},{24,32},{32,40},{40,48},{48,56},{56,64},{64,7... | collective-permute-start | bytes 6920 | tf_op jit(solution)/shard_map/ppermute | solution.py:23
  62.2 2.0 fusion.66
  64.3 0.9 reduce-window.6
  66.2 2.3 convolution_convert_fusion
  68.6 2.7 %fusion.6 = f32[256,256]{1,0:T(8,128)S(1)} fusion(bf16[3072,128]{1,0:T(8,128)(2,1)} %collective-permute-done.4, bf16[3072,128]{1,0:T(8,128)(2,1)S(1)} %copy-done.30, pred[]{:T(512)S(6)} %eq.14, bf16[256,3072]{1,0:T(8,128)(2,1)} %constant_dynamic-update-slice_fusion.32, f32[3072]{0:T(1024)S(1)} %convert_element_type.73, f32[256]{0:T(256)S(1)} %add_rsqrt_fusion.1), kind=kOutput, calls=%fused_computation.10 | convolution fusion | flops 412876800 | bytes 3421185 | tf_op jit(solution)/shard_map/dot_general | solution.py:186
  71.3 0.6 fusion.57
  72.0 0.7 select_bitcast_fusion
  72.7 0.7 maximum_maximum_fusion
  73.4 10.5 %all_gather.7 = bf16[256,512]{1,0:T(8,128)(2,1)S(1)} all-gather(bf16[256,128]{1,0:T(8,128)(2,1)S(1)} %convolution_convert_fusion), channel_id=1, replica_groups=mesh['seq'=32,'mp'=4,'req'=2] {'mp'}, dimensions={1}, use_global_device_ids=true | all-gather | bytes 327680 | tf_op jit(solution)/shard_map/all_gather | solution.py:192
  84.0 3.2 %collective-permute-start.6 = (bf16[3,512]{1,0:T(4,128)(2,1)S(1)}, bf16[3,512]{1,0:T(4,128)(2,1)S(1)}, u32[]{:S(2)}, u32[]{:S(2)}) collective-permute-start(bf16[3,512]{1,0:T(4,128)(2,1)S(1)} %slice.513), channel_id=1, source_target_pairs={{0,8},{8,16},{16,24},{24,32},{32,40},{40,48},{48,56},{56,64},{64,7... | collective-permute-start | bytes 9224 | tf_op jit(solution)/shard_map/ppermute | solution.py:23
  87.2 1.8 slice_convert_fusion
  89.0 0.6 compare_select_fusion.1
  90.0 0.9 copy.87
  91.4 0.6 copy-done.4
  92.5 0.8 copy-done.1
  93.6 1.0 pad_maximum_fusion
  94.7 10.4 %all-to-all-start = ((f32[32,3,5,256]{3,1,2,0:T(4,128)}), f32[32,3,5,256]{3,1,2,0:T(4,128)}, u32[]{:S(2)}, u32[]{:S(2)}) async-start(f32[32,3,5,256]{3,1,2,0:T(4,128)} %pad_maximum_fusion), calls=%async_computation | async-start | bytes 1310720 | tf_op jit(solution)/shard_map/all_to_all | solution.py:223
  105.1 0.8 constant_dynamic-slice_fusion
  105.8 0.6 constant_dynamic-update-slice_fusion.31
  106.4 1.2 multiply_cosine_fusion.1
  107.7 2.8 %fusion.78 = f32[256,256]{0,1:T(8,128)S(1)} fusion(bf16[3072,256]{1,0:T(8,128)(2,1)} %param.22, bf16[256,3072]{1,0:T(8,128)(2,1)} %constant_dynamic-update-slice_fusion.32, f32[3072]{0:T(1024)} %copy-done.10, f32[256]{0:T(256)} %copy-done.29), kind=kOutput, calls=%fused_computation.273 | convolution fusion | flops 405798912 | bytes 3421184 | tf_op jit(solution)/shard_map/dot_general | solution.py:168
  110.5 15.1 %all-to-all-done = f32[32,3,5,256]{3,1,2,0:T(4,128)} async-done(((f32[32,3,5,256]{3,1,2,0:T(4,128)}), f32[32,3,5,256]{3,1,2,0:T(4,128)}, u32[]{:S(2)}, u32[]{:S(2)}) %all-to-all-start) | async-done | bytes 491552 | tf_op jit(solution)/shard_map/all_to_all | solution.py:223
  125.6 1.0 slice_bitcast_fusion.2
  126.7 0.9 slice_bitcast_fusion.21
  128.4 0.9 copy.92
  129.3 5.9 %all-to-all-start.1 = ((f32[32,3,4,256]{3,2,1,0:T(4,128)}), f32[32,3,4,256]{3,2,1,0:T(4,128)}, u32[]{:S(2)}, u32[]{:S(2)}) async-start(f32[32,3,4,256]{3,2,1,0:T(4,128)} %copy.92), calls=%async_computation.1 | async-start | bytes 786432 | tf_op jit(solution)/shard_map/all_to_all | solution.py:230
  135.3 0.7 fusion.80
  136.0 1.0 copy.98
  137.1 1.8 copy.97
  138.8 1.9 copy.94
  140.7 1.1 subtract_convert_fusion
  142.0 1.1 fusion.47
  143.1 9.6 %all-to-all-done.1 = f32[32,3,4,256]{3,2,1,0:T(4,128)} async-done(((f32[32,3,4,256]{3,2,1,0:T(4,128)}), f32[32,3,4,256]{3,2,1,0:T(4,128)}, u32[]{:S(2)}, u32[]{:S(2)}) %all-to-all-start.1) | async-done | bytes 393248 | tf_op jit(solution)/shard_map/all_to_all | solution.py:230
  152.7 1.8 copy.93
  154.5 1.9 reshape.285
  156.4 1.5 convolution_multiply_fusion
  157.9 2.6 %multiply_reduce_fusion = (f32[256,3]{0,1:T(4,128)S(1)}, f32[256,3,128]{0,2,1:T(8,128)S(1)}) fusion(f32[256,3,128]{0,2,1:T(8,128)} %bitcast.323, f32[256,3,128]{0,2,1:T(8,128)} %bitcast.317, f32[3]{0:T(128)S(1)} %copy-done.33, f32[256,3,128]{0,2,1:T(8,128)S(1)} %convolution_multiply_fusion, f32[256,3]{0,1:T(4,128)S(1)} %copy-done.22, ...), kind=kOutput, calls=%fused_computation.53 | convolution fusion | flops 303955200 | bytes 1909772 | tf_op jit(solution)/shard_map/tsh,shp->thp/dot_general | solution.py:215
  160.7 25.3 %all-gather.2.cloned.1.call-done.kv_ref = bf16[16384,256]{1,0:T(8,128)(2,1)} async-done(((bf16[512,256]{1,0:T(8,128)(2,1)}), bf16[16384,256]{1,0:T(8,128)(2,1)}) %all-gather.2.cloned.1.call-update) | async-done | bytes 8388624 | tf_op jit(solution)/shard_map/all_gather | solution.py:246
  186.0 21.5 %shard_map.211 = bf16[512,128]{1,0:T(8,128)(2,1)S(1)} custom-call(s32[512,1]{1,0:T(8,128)S(1)} %bitcast.313, bf16[512,128]{1,0:T(8,128)(2,1)S(1)} %bitcast.314, s32[1,16384]{1,0:T(1,128)S(1)} %compare_select_fusion.kr_ref, bf16[16384,256]{1,0:T(8,128)(2,1)} %all-gather.2.cloned.1.call-done.kv_ref), custom_call_target="tpu_custom_call" | custom-call | tf_op jit(solution)/shard_map/pallas_call | solution.py:73
  207.6 2.0 fusion.81
  209.6 2.3 fusion.2
  211.9 1.0 copy-done.2
  213.0 0.9 add_bitcast_fusion
  213.9 24.2 %reduce-scatter.2.cloned.1.call-done = bf16[256,768]{1,0:T(8,128)(2,1)} async-done(((bf16[256,3072]{1,0:T(8,128)(2,1)}), bf16[256,768]{1,0:T(8,128)(2,1)}) %reduce-scatter.2.cloned.1.call-update) | async-done | bytes 393232 | tf_op jit(solution)/shard_map/reduce_scatter | solution.py:265
  238.1 2.0 fusion.31
  (158 shorter events, 4.6 us)
Async XLA Ops:
  7.2 202.5 %copy-start = (bf16[384,3072]{1,0:T(8,128)(2,1)S(1)}, bf16[384,3072]{1,0:T(8,128)(2,1)}, u32[]{:S(2)}) copy-start(bf16[384,3072]{1,0:T(8,128)(2,1)} %param.34) | copy-start | bytes 7077892
  7.2 10.9 %copy-start.5 = (bf16[1,256,768]{2,1,0:T(8,128)(2,1)S(1)}, bf16[1,256,768]{2,1,0:T(8,128)(2,1)}, u32[]{:S(2)}) copy-start(bf16[1,256,768]{2,1,0:T(8,128)(2,1)} %param.20) | copy-start | bytes 1179652
  7.2 37.5 %copy-start.8 = (bf16[1,256,128]{2,1,0:T(8,128)(2,1)S(1)}, bf16[1,256,128]{2,1,0:T(8,128)(2,1)}, u32[]{:S(2)}) copy-start(bf16[1,256,128]{2,1,0:T(8,128)(2,1)} %param.35) | copy-start | bytes 196612
  7.2 11.7 %copy-start.9 = (bf16[4,384]{1,0:T(4,128)(2,1)S(1)}, bf16[4,384]{1,0:T(4,128)(2,1)}, u32[]{:S(2)}) copy-start(bf16[4,384]{1,0:T(4,128)(2,1)} %param.31) | copy-start | bytes 9220
  7.2 13.9 %copy-start.28 = (bf16[384]{0:T(512)(128)(2,1)S(1)}, bf16[384]{0:T(512)(128)(2,1)}, u32[]{:S(2)}) copy-start(bf16[384]{0:T(512)(128)(2,1)} %param.33) | copy-start | bytes 2308
  7.2 178.8 %all-gather.2.cloned.1.call-start = ((), (), s32[]{:S(2)}) async-start(), calls=%async_computation.3 | async-start | bytes 8650752 | tf_op jit(solution)/shard_map/all_gather | solution.py:246
  7.3 38.4 %collective-permute-start = (bf16[256,768]{1,0:T(8,128)(2,1)}, bf16[256,768]{1,0:T(8,128)(2,1)}, u32[]{:S(2)}, u32[]{:S(2)}) collective-permute-start(bf16[256,768]{1,0:T(8,128)(2,1)} %bitcast.319), channel_id=1, source_target_pairs={{0,2},{2,4},{4,6},{6,0},{1,3},{3,5},{5,7},{7,1},{8,10},{10,12},{12... | collective-permute-start | bytes 1179656 | tf_op jit(solution)/shard_map/ppermute | solution.py:159
  9.4 38.2 %collective-permute-start.1 = (bf16[256,768]{1,0:T(8,128)(2,1)}, bf16[256,768]{1,0:T(8,128)(2,1)}, u32[]{:S(2)}, u32[]{:S(2)}) collective-permute-start(bf16[256,768]{1,0:T(8,128)(2,1)} %bitcast.320), channel_id=1, source_target_pairs={{0,4},{2,6},{4,0},{6,2},{1,5},{3,7},{5,1},{7,3},{8,12},{10,14},{12... | collective-permute-start | bytes 1179656 | tf_op jit(solution)/shard_map/ppermute | solution.py:159
  11.8 37.5 %collective-permute-start.2 = (bf16[256,768]{1,0:T(8,128)(2,1)}, bf16[256,768]{1,0:T(8,128)(2,1)S(1)}, u32[]{:S(2)}, u32[]{:S(2)}) collective-permute-start(bf16[256,768]{1,0:T(8,128)(2,1)} %bitcast.321), channel_id=1, source_target_pairs={{0,6},{2,0},{4,2},{6,4},{1,7},{3,1},{5,3},{7,5},{8,14},{10,8},{12,... | collective-permute-start | bytes 1179656 | tf_op jit(solution)/shard_map/ppermute | solution.py:159
  13.0 55.6 %collective-permute-start.4 = (bf16[3072,128]{1,0:T(8,128)(2,1)}, bf16[3072,128]{1,0:T(8,128)(2,1)}, u32[]{:S(2)}, u32[]{:S(2)}) collective-permute-start(bf16[3072,128]{1,0:T(8,128)(2,1)} %param.23), channel_id=1, source_target_pairs={{0,2},{2,0},{4,6},{6,4},{1,3},{3,1},{5,7},{7,5},{8,10},{10,8},{12,... | collective-permute-start | bytes 2359304 | tf_op jit(solution)/shard_map/ppermute | solution.py:178
  13.3 31.4 %collective-permute-start.3 = (bf16[256,128]{1,0:T(8,128)(2,1)}, bf16[256,128]{1,0:T(8,128)(2,1)}, u32[]{:S(2)}, u32[]{:S(2)}) collective-permute-start(bf16[256,128]{1,0:T(8,128)(2,1)} %bitcast.325), channel_id=1, source_target_pairs={{0,2},{2,0},{4,6},{6,4},{1,3},{3,1},{5,7},{7,5},{8,10},{10,8},{12,... | collective-permute-start | bytes 196616 | tf_op jit(solution)/shard_map/ppermute | solution.py:178
  19.5 51.8 %copy-start.19 = (f32[256]{0:T(256)}, f32[256]{0:T(256)S(1)}, u32[]{:S(2)}) copy-start(f32[256]{0:T(256)S(1)} %add_convert_fusion.2) | copy-start | bytes 3076
  19.5 51.8 %copy-start.26 = (f32[64]{0:T(128)}, f32[64]{0:T(128)S(1)}, u32[]{:S(2)}) copy-start(f32[64]{0:T(128)S(1)} %multiply_power_fusion) | copy-start | bytes 772
  20.4 48.2 %copy-start.10 = (f32[3072]{0:T(1024)}, f32[3072]{0:T(1024)S(1)}, u32[]{:S(2)}) copy-start(f32[3072]{0:T(1024)S(1)} %convert_element_type.73) | copy-start | bytes 36868
  51.9 16.6 %copy-start.29 = (f32[256]{0:T(256)}, f32[256]{0:T(256)S(1)}, u32[]{:S(2)}) copy-start(f32[256]{0:T(256)S(1)} %add_rsqrt_fusion.1) | copy-start | bytes 3076
  52.0 10.3 %copy-start.31 = (bf16[3072,3]{0,1:T(4,128)(2,1)S(1)}, bf16[3072,3]{0,1:T(4,128)(2,1)}, u32[]{:S(2)}) copy-start(bf16[3072,3]{0,1:T(4,128)(2,1)} %param.27) | copy-start | bytes 55300
  52.0 10.3 %copy-start.32 = (f32[3]{0:T(128)S(1)}, f32[3]{0:T(128)}, u32[]{:S(2)}) copy-start(f32[3]{0:T(128)} %param.28) | copy-start | bytes 40
  56.3 0.7 copy-start.7
  57.1 32.5 %collective-permute-start.5 = (bf16[3,384]{1,0:T(4,128)(2,1)S(1)}, bf16[3,384]{1,0:T(4,128)(2,1)S(1)}, u32[]{:S(2)}, u32[]{:S(2)}) collective-permute-start(bf16[3,384]{1,0:T(4,128)(2,1)S(1)} %slice_bitcast_fusion.64), channel_id=1, source_target_pairs={{0,8},{8,16},{16,24},{24,32},{32,40},{40,48},{48,56},{56,64},{64,7... | collective-permute-start | bytes 6920 | tf_op jit(solution)/shard_map/ppermute | solution.py:23
  65.6 0.6 copy-start.11
  66.2 27.3 %copy-start.24 = (f32[3]{0:T(128)}, f32[3]{0:T(128)S(1)}, u32[]{:S(2)}) copy-start(f32[3]{0:T(128)S(1)} %exp.50) | copy-start | bytes 40
  66.2 2.4 copy-start.30
  71.3 18.3 %copy-start.23 = (bf16[1,3,384]{2,1,0:T(4,128)(2,1)S(1)}, bf16[1,3,384]{2,1,0:T(4,128)(2,1)}, u32[]{:S(2)}) copy-start(bf16[1,3,384]{2,1,0:T(4,128)(2,1)} %param.37) | copy-start | bytes 6916
  71.9 17.8 %copy-start.15 = (f32[384]{0:T(512)S(1)}, f32[384]{0:T(512)}, u32[]{:S(2)}) copy-start(f32[384]{0:T(512)} %get-tuple-element.3) | copy-start | bytes 4612
  71.9 17.8 %copy-start.16 = (f32[384]{0:T(512)S(1)}, f32[384]{0:T(512)}, u32[]{:S(2)}) copy-start(f32[384]{0:T(512)} %get-tuple-element.4) | copy-start | bytes 4612
  71.9 17.8 %copy-start.17 = (f32[384]{0:T(512)S(1)}, f32[384]{0:T(512)}, u32[]{:S(2)}) copy-start(f32[384]{0:T(512)} %get-tuple-element.5) | copy-start | bytes 4612
  72.0 17.8 %copy-start.18 = (f32[384]{0:T(512)S(1)}, f32[384]{0:T(512)}, u32[]{:S(2)}) copy-start(f32[384]{0:T(512)} %get-tuple-element.6) | copy-start | bytes 4612
  84.0 6.9 %collective-permute-start.6 = (bf16[3,512]{1,0:T(4,128)(2,1)S(1)}, bf16[3,512]{1,0:T(4,128)(2,1)S(1)}, u32[]{:S(2)}, u32[]{:S(2)}) collective-permute-start(bf16[3,512]{1,0:T(4,128)(2,1)S(1)} %slice.513), channel_id=1, source_target_pairs={{0,8},{8,16},{16,24},{24,32},{32,40},{40,48},{48,56},{56,64},{64,7... | collective-permute-start | bytes 9224 | tf_op jit(solution)/shard_map/ppermute | solution.py:23
  89.6 1.3 copy-start.21
  89.7 1.3 copy-start.14
  91.0 1.0 copy-start.4
  92.5 0.8 copy-start.1
  93.5 12.9 %copy-start.20 = (f32[256]{0:T(256)S(1)}, f32[256]{0:T(256)}, u32[]{:S(2)}) copy-start(f32[256]{0:T(256)} %copy-done.19) | copy-start | bytes 3076
  93.5 12.9 %copy-start.27 = (f32[64]{0:T(128)S(1)}, f32[64]{0:T(128)}, u32[]{:S(2)}) copy-start(f32[64]{0:T(128)} %copy-done.26) | copy-start | bytes 772
  94.7 30.9 %all-to-all-start = ((f32[32,3,5,256]{3,1,2,0:T(4,128)}), f32[32,3,5,256]{3,1,2,0:T(4,128)}, u32[]{:S(2)}, u32[]{:S(2)}) async-start(f32[32,3,5,256]{3,1,2,0:T(4,128)} %pad_maximum_fusion), calls=%async_computation | async-start | bytes 1310720 | tf_op jit(solution)/shard_map/all_to_all | solution.py:223
  125.6 2.2 copy-start.6
  129.3 23.4 %all-to-all-start.1 = ((f32[32,3,4,256]{3,2,1,0:T(4,128)}), f32[32,3,4,256]{3,2,1,0:T(4,128)}, u32[]{:S(2)}, u32[]{:S(2)}) async-start(f32[32,3,4,256]{3,2,1,0:T(4,128)} %copy.92), calls=%async_computation.1 | async-start | bytes 786432 | tf_op jit(solution)/shard_map/all_to_all | solution.py:230
  135.3 102.8 %reduce-scatter.2.cloned.1.call-start = ((), (), s32[]{:S(2)}) async-start(), calls=%async_computation.4 | async-start | bytes 1966080 | tf_op jit(solution)/shard_map/reduce_scatter | solution.py:265
  142.0 15.9 %copy-start.12 = (f32[1,3,2,128]{3,1,2,0:T(4,128)S(1)}, f32[1,3,2,128]{3,1,2,0:T(4,128)}, u32[]{:S(2)}) copy-start(f32[1,3,2,128]{3,1,2,0:T(4,128)} %copy-done.11) | copy-start | bytes 9220
  142.0 15.9 %copy-start.22 = (f32[256,3]{0,1:T(4,128)S(1)}, f32[256,3]{0,1:T(4,128)}, u32[]{:S(2)}) copy-start(f32[256,3]{0,1:T(4,128)} %get-tuple-element.79) | copy-start | bytes 9220
  142.0 15.9 %copy-start.33 = (f32[3]{0:T(128)S(1)}, f32[3]{0:T(128)}, u32[]{:S(2)}) copy-start(f32[3]{0:T(128)} %param.30) | copy-start | bytes 40
  157.9 2.6 %copy-start.13 = (f32[384]{0:T(512)S(1)}, f32[384]{0:T(512)}, u32[]{:S(2)}) copy-start(f32[384]{0:T(512)} %convert_element_type.82) | copy-start | bytes 4612
  211.9 1.0 copy-start.2
  211.9 1.1 copy-start.3
  211.9 1.1 copy-start.25
Sparse Core Ops, SparseCore 0:
  73.6 112.3 all-gather.1
  212.1 25.9 reduce-scatter.1

commit v10 on v8

--- a/solution.py
+++ b/solution.py
@@ -249,7 +249,7 @@
     key_rank = jnp.where(in_cache, jnp.where(slot_ok, -1, never), new_index)[None, :]
     query_rank = jnp.tile(query_index, local_heads)[:, None]
     query_rows = jnp.transpose(query, (1, 0, 2)).reshape(local_heads * tokens, HD)
-    attended = attend(query_rows, query_rank, piece, key_rank, 4 * shard_rows)
+    attended = attend(query_rows, query_rank, piece, key_rank, 8 * shard_rows)
     attended = jnp.transpose(attended.reshape(local_heads, tokens, HD), (1, 0, 2)).reshape(
         tokens, local_heads * HD
     )

time: 222 us -> 220 us (level)
  no operation moved by 1% of the time
where the time goes in v10:
time: 220 us; the launch traced here: 219 us
  waiting for transfers between devices  81.1 us (37%)
  starting transfers between devices  29.1 us (13%)
  local copies, waits for them, and re-layouts  25.2 us (11%)
  other arithmetic  20.9 us (10%)
  Pallas kernels  19.7 us (9%)
  matrix products  17.8 us (8%)
  between operations  15.7 us (7%)
  blocking collectives  9.32 us (4%)
    all_gather x1, waiting for transfers between devices, shards(): piece = lax.all_gather(group_rows, 'seq', axis=0, tiled=True)  24.5 us
    reduce_scatter x1, waiting for transfers between devices, shards(): lax.psum_scatter(term.astype(jnp.bfloat16), 'mp', scatter_dimension=1, ti...  24.1 us
    pallas_call x1, Pallas kernels, attend(): pl.pallas_call(kernel, grid=(steps,), in_specs=[pl.BlockSpec((rows, 1), l...  19.7 us
    all_to_all x1, waiting for transfers between devices, shards(): lax.all_to_all(jnp.concatenate([pieces, decays], axis=2), 'seq', 0, 0, ti...  14.8 us
    all_to_all x1, starting transfers between devices, shards(): lax.all_to_all(jnp.concatenate([pieces, decays], axis=2), 'seq', 0, 0, ti...  11.1 us
    all_to_all x1, waiting for transfers between devices, shards(): lax.all_to_all(jnp.stack(entering, axis=0), 'seq', 0, 0, tiled=True)  9.38 us
    all_gather x1, blocking collectives, shards(): bc_all = lax.all_gather(bc_block, 'mp', axis=1, tiled=True)  9.32 us
    ppermute x3, waiting for transfers between devices, shards(): lax.ppermute(own_rows, 'mp', [(i, (i + shift) % mp_count) for i in range(...  8.31 us
  transfers between devices with their start and end apart: 10, of which 5 were waited for; matrix products, arithmetic and copies ran while one was open for 22% of the time, Pallas kernels for 0%

profile of v10, /device:TPU:1, one launch (start us, length us, event | category | flops | bytes accessed | tf_op | source)
XLA Modules:
  0.0 218.8 jit_solution(12821266706951444598)
XLA Ops:
  7.3 2.1 collective-permute-start
  9.4 2.5 %collective-permute-start.1 = (bf16[256,768]{1,0:T(8,128)(2,1)}, bf16[256,768]{1,0:T(8,128)(2,1)}, u32[]{:S(2)}, u32[]{:S(2)}) collective-permute-start(bf16[256,768]{1,0:T(8,128)(2,1)} %bitcast.327), channel_id=1, source_target_pairs={{0,4},{2,6},{4,0},{6,2},{1,5},{3,7},{5,1},{7,3},{8,12},{10,14},{12... | collective-permute-start | bytes 1179656 | tf_op jit(solution)/shard_map/ppermute | solution.py:159
  11.8 1.2 collective-permute-start.2
  13.8 1.4 slice_convert_fusion.4
  15.2 1.4 broadcast_in_dim.30
  16.6 0.8 constant_dynamic-update-slice_fusion.35
  17.8 0.6 convert_element_type.85
  18.4 0.6 convert_reduce_fusion.3
  19.0 1.8 constant_dynamic-update-slice_fusion.34
  20.8 8.3 %collective-permute-done.1 = bf16[256,768]{1,0:T(8,128)(2,1)} collective-permute-done((bf16[256,768]{1,0:T(8,128)(2,1)}, bf16[256,768]{1,0:T(8,128)(2,1)}, u32[]{:S(2)}, u32[]{:S(2)}) %collective-permute-start.1) | collective-permute-done | bytes 393248 | tf_op jit(solution)/shard_map/ppermute | solution.py:159
  29.1 1.8 constant_dynamic-update-slice_fusion.33
  30.9 0.8 constant_dynamic-update-slice_fusion.32
  31.8 1.8 fusion.3
  33.6 2.0 fusion.5
  35.7 0.6 fusion.68
  36.3 0.6 fusion.49
  37.0 0.7 pad_maximum_fusion.2
  37.7 1.5 fusion.7
  39.2 0.6 slice_bitcast_fusion.63
  39.8 3.8 %collective-permute-start.4 = (bf16[3,384]{1,0:T(4,128)(2,1)}, bf16[3,384]{1,0:T(4,128)(2,1)}, u32[]{:S(2)}, u32[]{:S(2)}) collective-permute-start(bf16[3,384]{1,0:T(4,128)(2,1)} %slice_bitcast_fusion.63), channel_id=1, source_target_pairs={{0,8},{8,16},{16,24},{24,32},{32,40},{40,48},{48,56},{56,64},{64,7... | collective-permute-start | bytes 6920 | tf_op jit(solution)/shard_map/ppermute | solution.py:23
  43.5 0.5 fusion.59
  44.1 0.9 reduce-window.6
  45.4 2.6 %convolution_convert_fusion = bf16[256,128]{1,0:T(8,128)(2,1)} fusion(bf16[256,3072]{1,0:T(8,128)(2,1)} %copy-done.1, bf16[3072,128]{1,0:T(8,128)(2,1)S(1)} %copy-done.8), kind=kOutput, calls=%fused_computation.16 | convolution fusion | flops 201359360 | bytes 2424832 | tf_op jit(solution)/shard_map/dot_general | solution.py:176
  48.3 1.8 maximum_select_fusion
  50.1 9.3 %all_gather.7 = bf16[256,512]{1,0:T(8,128)(2,1)S(1)} all-gather(bf16[256,128]{1,0:T(8,128)(2,1)} %convolution_convert_fusion), channel_id=1, replica_groups=mesh['seq'=32,'mp'=4,'req'=2] {'mp'}, dimensions={1}, use_global_device_ids=true | all-gather | bytes 327680 | tf_op jit(solution)/shard_map/all_gather | solution.py:177
  59.4 2.6 %collective-permute-start.5 = (bf16[3,512]{1,0:T(4,128)(2,1)S(1)}, bf16[3,512]{1,0:T(4,128)(2,1)S(1)}, u32[]{:S(2)}, u32[]{:S(2)}) collective-permute-start(bf16[3,512]{1,0:T(4,128)(2,1)S(1)} %slice.500), channel_id=1, source_target_pairs={{0,8},{8,16},{16,24},{24,32},{32,40},{40,48},{48,56},{56,64},{64,7... | collective-permute-start | bytes 9224 | tf_op jit(solution)/shard_map/ppermute | solution.py:23
  62.1 1.8 slice_convert_fusion
  63.9 0.6 compare_select_fusion.1
  64.9 0.9 copy.71
  66.0 0.3 divide_multiply_fusion
  66.3 0.5 copy-done.5
  66.9 0.5 fusion.29
  67.4 0.8 copy-done.2
  68.1 0.3 copy.80
  68.5 1.0 pad_maximum_fusion
  69.5 11.1 %all-to-all-start = ((f32[32,3,5,256]{3,1,2,0:T(4,128)}), f32[32,3,5,256]{3,1,2,0:T(4,128)}, u32[]{:S(2)}, u32[]{:S(2)}) async-start(f32[32,3,5,256]{3,1,2,0:T(4,128)} %pad_maximum_fusion), calls=%async_computation | async-start | bytes 1310720 | tf_op jit(solution)/shard_map/all_to_all | solution.py:217
  80.6 0.8 constant_dynamic-slice_fusion
  81.4 0.6 constant_dynamic-update-slice_fusion.31
  82.0 1.2 multiply_cosine_fusion.1
  83.2 2.6 %fusion.67 = f32[256,256]{0,1:T(8,128)S(1)} fusion(bf16[256,3072]{1,0:T(8,128)(2,1)} %copy-done.1, bf16[3072,256]{1,0:T(8,128)(2,1)} %param.22), kind=kOutput, calls=%fused_computation.262 | convolution fusion | flops 402653184 | bytes 3407872 | tf_op jit(solution)/shard_map/dot_general | solution.py:168
  85.9 14.8 %all-to-all-done = f32[32,3,5,256]{3,1,2,0:T(4,128)} async-done(((f32[32,3,5,256]{3,1,2,0:T(4,128)}), f32[32,3,5,256]{3,1,2,0:T(4,128)}, u32[]{:S(2)}, u32[]{:S(2)}) %all-to-all-start) | async-done | bytes 491552 | tf_op jit(solution)/shard_map/all_to_all | solution.py:217
  100.7 1.0 slice_bitcast_fusion.1
  101.7 0.9 slice_bitcast_fusion.20
  103.5 0.9 copy.76
  104.4 5.8 %all-to-all-start.1 = ((f32[32,3,4,256]{3,2,1,0:T(4,128)}), f32[32,3,4,256]{3,2,1,0:T(4,128)}, u32[]{:S(2)}, u32[]{:S(2)}) async-start(f32[32,3,4,256]{3,2,1,0:T(4,128)} %copy.76), calls=%async_computation.1 | async-start | bytes 786432 | tf_op jit(solution)/shard_map/all_to_all | solution.py:224
  110.2 0.7 fusion.66
  110.9 1.0 copy.82
  111.9 1.7 copy.81
  113.7 1.9 copy.78
  115.6 1.1 subtract_convert_fusion
  116.8 1.1 fusion.40
  118.0 9.4 %all-to-all-done.1 = f32[32,3,4,256]{3,2,1,0:T(4,128)} async-done(((f32[32,3,4,256]{3,2,1,0:T(4,128)}), f32[32,3,4,256]{3,2,1,0:T(4,128)}, u32[]{:S(2)}, u32[]{:S(2)}) %all-to-all-start.1) | async-done | bytes 393248 | tf_op jit(solution)/shard_map/all_to_all | solution.py:224
  127.3 1.8 copy.77
  129.1 1.9 reshape.285
  131.0 1.5 convolution_multiply_fusion
  132.5 2.6 %multiply_reduce_fusion = (f32[256,3]{0,1:T(4,128)S(1)}, f32[256,3,128]{0,2,1:T(8,128)S(1)}) fusion(f32[256,3,128]{0,2,1:T(8,128)} %bitcast.332, f32[256,3,128]{0,2,1:T(8,128)} %bitcast.324, f32[3]{0:T(128)S(1)} %copy-done.41, f32[256,3,128]{0,2,1:T(8,128)S(1)} %convolution_multiply_fusion, f32[256,3]{0,1:T(4,128)S(1)} %copy-done.31, ...), kind=kOutput, calls=%fused_computation.45 | convolution fusion | flops 303955200 | bytes 1909772 | tf_op jit(solution)/shard_map/tsh,shp->thp/dot_general | solution.py:209
  135.3 24.5 %all-gather.2.cloned.1.call-done.kv_ref = bf16[16384,256]{1,0:T(8,128)(2,1)} async-done(((bf16[512,256]{1,0:T(8,128)(2,1)}), bf16[16384,256]{1,0:T(8,128)(2,1)}) %all-gather.2.cloned.1.call-update) | async-done | bytes 8388624 | tf_op jit(solution)/shard_map/all_gather | solution.py:240
  159.8 19.7 %shard_map.211 = bf16[512,128]{1,0:T(8,128)(2,1)S(1)} custom-call(s32[512,1]{1,0:T(8,128)S(1)} %bitcast.319, bf16[512,128]{1,0:T(8,128)(2,1)S(1)} %bitcast.320, s32[1,16384]{1,0:T(1,128)S(1)} %compare_select_fusion.kr_ref, bf16[16384,256]{1,0:T(8,128)(2,1)} %all-gather.2.cloned.1.call-done.kv_ref), custom_call_target="tpu_custom_call" | custom-call | tf_op jit(solution)/shard_map/pallas_call | solution.py:73
  179.6 2.0 fusion.69
  181.6 2.3 %fusion.2 = bf16[256,3072]{1,0:T(8,128)(2,1)} fusion(f32[256,3072]{1,0:T(8,128)S(1)} %fusion.69, bf16[256,384]{0,1:T(8,128)(2,1)S(1)} %fusion.28, bf16[384,3072]{1,0:T(8,128)(2,1)S(1)} %copy-done), kind=kOutput, calls=%fused_computation.5 | convolution fusion | flops 605552640 | bytes 7274496 | tf_op jit(solution)/shard_map/dot_general | solution.py:258
  183.9 1.0 copy-done.3
  185.0 0.9 add_bitcast_fusion
  185.8 24.1 %reduce-scatter.2.cloned.1.call-done = bf16[256,768]{1,0:T(8,128)(2,1)} async-done(((bf16[256,3072]{1,0:T(8,128)(2,1)}), bf16[256,768]{1,0:T(8,128)(2,1)}) %reduce-scatter.2.cloned.1.call-update) | async-done | bytes 393232 | tf_op jit(solution)/shard_map/reduce_scatter | solution.py:259
  210.0 2.0 fusion.24
  (172 shorter events, 3.0 us)
Async XLA Ops:
  7.2 174.4 %copy-start = (bf16[384,3072]{1,0:T(8,128)(2,1)S(1)}, bf16[384,3072]{1,0:T(8,128)(2,1)}, u32[]{:S(2)}) copy-start(bf16[384,3072]{1,0:T(8,128)(2,1)} %param.34) | copy-start | bytes 7077892
  7.2 9.4 %copy-start.6 = (bf16[1,256,768]{2,1,0:T(8,128)(2,1)S(1)}, bf16[1,256,768]{2,1,0:T(8,128)(2,1)}, u32[]{:S(2)}) copy-start(bf16[1,256,768]{2,1,0:T(8,128)(2,1)} %param.20) | copy-start | bytes 1179652
  7.2 10.5 %copy-start.27 = (bf16[3072]{0:T(1024)(128)(2,1)S(1)}, bf16[3072]{0:T(1024)(128)(2,1)}, u32[]{:S(2)}) copy-start(bf16[3072]{0:T(1024)(128)(2,1)} %param.21) | copy-start | bytes 18436
  7.2 10.5 %copy-start.40 = (f32[3]{0:T(128)S(1)}, f32[3]{0:T(128)}, u32[]{:S(2)}) copy-start(f32[3]{0:T(128)} %param.29) | copy-start | bytes 40
  7.2 10.5 %copy-start.37 = (bf16[384]{0:T(512)(128)(2,1)S(1)}, bf16[384]{0:T(512)(128)(2,1)}, u32[]{:S(2)}) copy-start(bf16[384]{0:T(512)(128)(2,1)} %param.33) | copy-start | bytes 2308
  7.2 11.1 %copy-start.15 = (bf16[4,384]{1,0:T(4,128)(2,1)S(1)}, bf16[4,384]{1,0:T(4,128)(2,1)}, u32[]{:S(2)}) copy-start(bf16[4,384]{1,0:T(4,128)(2,1)} %param.31) | copy-start | bytes 9220
  7.2 152.5 %all-gather.2.cloned.1.call-start = ((), (), s32[]{:S(2)}) async-start(), calls=%async_computation.3 | async-start | bytes 8650752 | tf_op jit(solution)/shard_map/all_gather | solution.py:240
  7.3 11.7 %collective-permute-start = (bf16[256,768]{1,0:T(8,128)(2,1)}, bf16[256,768]{1,0:T(8,128)(2,1)}, u32[]{:S(2)}, u32[]{:S(2)}) collective-permute-start(bf16[256,768]{1,0:T(8,128)(2,1)} %bitcast.326), channel_id=1, source_target_pairs={{0,2},{2,4},{4,6},{6,0},{1,3},{3,5},{5,7},{7,1},{8,10},{10,12},{12... | collective-permute-start | bytes 1179656 | tf_op jit(solution)/shard_map/ppermute | solution.py:159
  9.4 19.7 %collective-permute-start.1 = (bf16[256,768]{1,0:T(8,128)(2,1)}, bf16[256,768]{1,0:T(8,128)(2,1)}, u32[]{:S(2)}, u32[]{:S(2)}) collective-permute-start(bf16[256,768]{1,0:T(8,128)(2,1)} %bitcast.327), channel_id=1, source_target_pairs={{0,4},{2,6},{4,0},{6,2},{1,5},{3,7},{5,1},{7,3},{8,12},{10,14},{12... | collective-permute-start | bytes 1179656 | tf_op jit(solution)/shard_map/ppermute | solution.py:159
  11.8 19.1 %collective-permute-start.2 = (bf16[256,768]{1,0:T(8,128)(2,1)}, bf16[256,768]{1,0:T(8,128)(2,1)S(1)}, u32[]{:S(2)}, u32[]{:S(2)}) collective-permute-start(bf16[256,768]{1,0:T(8,128)(2,1)} %bitcast.328), channel_id=1, source_target_pairs={{0,6},{2,0},{4,2},{6,4},{1,7},{3,1},{5,3},{7,5},{8,14},{10,8},{12,... | collective-permute-start | bytes 1179656 | tf_op jit(solution)/shard_map/ppermute | solution.py:159
  17.5 18.8 %copy-start.28 = (f32[256]{0:T(256)}, f32[256]{0:T(256)S(1)}, u32[]{:S(2)}) copy-start(f32[256]{0:T(256)S(1)} %add_convert_fusion.2) | copy-start | bytes 3076
  17.5 18.8 %copy-start.35 = (f32[64]{0:T(128)}, f32[64]{0:T(128)S(1)}, u32[]{:S(2)}) copy-start(f32[64]{0:T(128)S(1)} %multiply_power_fusion) | copy-start | bytes 772
  33.6 2.1 copy-start.7
  33.6 4.1 %copy-start.39 = (bf16[3072,2,384]{2,1,0:T(2,128)(2,1)S(1)}, bf16[3072,2,384]{2,1,0:T(2,128)(2,1)}, u32[]{:S(2)}) copy-start(bf16[3072,2,384]{2,1,0:T(2,128)(2,1)} %param.25) | copy-start | bytes 14155780
  35.6 7.9 %copy-start.1 = (bf16[256,3072]{1,0:T(8,128)(2,1)}, bf16[256,3072]{1,0:T(8,128)(2,1)S(1)}, u32[]{:S(2)}) copy-start(bf16[256,3072]{1,0:T(8,128)(2,1)S(1)} %fusion.5) | copy-start | bytes 4718596
  35.7 1.3 copy-start.12
  37.0 11.3 %copy-start.9 = (bf16[256,128]{1,0:T(8,128)(2,1)}, bf16[256,128]{1,0:T(8,128)(2,1)S(1)}, u32[]{:S(2)}) copy-start(bf16[256,128]{1,0:T(8,128)(2,1)S(1)} %fusion.52) | copy-start | bytes 196612
  37.6 5.9 %copy-start.14 = (bf16[3072,3]{0,1:T(4,128)(2,1)S(1)}, bf16[3072,3]{0,1:T(4,128)(2,1)}, u32[]{:S(2)}) copy-start(bf16[3072,3]{0,1:T(4,128)(2,1)} %param.27) | copy-start | bytes 55300
  37.6 5.9 %copy-start.38 = (f32[3]{0:T(128)S(1)}, f32[3]{0:T(128)}, u32[]{:S(2)}) copy-start(f32[3]{0:T(128)} %param.28) | copy-start | bytes 40
  37.6 10.6 %collective-permute-start.3 = (bf16[512,128]{1,0:T(8,128)(2,1)}, bf16[512,128]{1,0:T(8,128)(2,1)}, u32[]{:S(2)}, u32[]{:S(2)}) collective-permute-start(bf16[512,128]{1,0:T(8,128)(2,1)} %pad_maximum_fusion.2), channel_id=1, source_target_pairs={{0,2},{2,0},{4,6},{6,4},{1,3},{3,1},{5,7},{7,5},{8,10},{10,8},{12,... | collective-permute-start | bytes 393224 | tf_op jit(solution)/shard_map/ppermute | solution.py:180
  39.1 5.0 %copy-start.11 = (bf16[256,2,384]{2,0,1:T(8,128)(2,1)}, bf16[256,2,384]{2,0,1:T(8,128)(2,1)S(1)}, u32[]{:S(2)}) copy-start(bf16[256,2,384]{2,0,1:T(8,128)(2,1)S(1)} %fusion.7) | copy-start | bytes 1179652
  39.1 6.2 %copy-start.8 = (bf16[3072,128]{1,0:T(8,128)(2,1)S(1)}, bf16[3072,128]{1,0:T(8,128)(2,1)}, u32[]{:S(2)}) copy-start(bf16[3072,128]{1,0:T(8,128)(2,1)} %param.26) | copy-start | bytes 2359300
  39.8 24.7 %collective-permute-start.4 = (bf16[3,384]{1,0:T(4,128)(2,1)}, bf16[3,384]{1,0:T(4,128)(2,1)}, u32[]{:S(2)}, u32[]{:S(2)}) collective-permute-start(bf16[3,384]{1,0:T(4,128)(2,1)} %slice_bitcast_fusion.63), channel_id=1, source_target_pairs={{0,8},{8,16},{16,24},{24,32},{32,40},{40,48},{48,56},{56,64},{64,7... | collective-permute-start | bytes 6920 | tf_op jit(solution)/shard_map/ppermute | solution.py:23
  45.4 3.0 %copy-start.13 = (bf16[1,256,128]{2,1,0:T(8,128)(2,1)S(1)}, bf16[1,256,128]{2,1,0:T(8,128)(2,1)}, u32[]{:S(2)}) copy-start(bf16[1,256,128]{2,1,0:T(8,128)(2,1)} %param.35) | copy-start | bytes 196612
  48.0 16.5 %copy-start.32 = (bf16[1,3,384]{2,1,0:T(4,128)(2,1)S(1)}, bf16[1,3,384]{2,1,0:T(4,128)(2,1)}, u32[]{:S(2)}) copy-start(bf16[1,3,384]{2,1,0:T(4,128)(2,1)} %param.37) | copy-start | bytes 6916
  48.0 16.6 %copy-start.23 = (f32[384]{0:T(512)S(1)}, f32[384]{0:T(512)}, u32[]{:S(2)}) copy-start(f32[384]{0:T(512)} %get-tuple-element.3) | copy-start | bytes 4612
  48.0 16.6 %copy-start.24 = (f32[384]{0:T(512)S(1)}, f32[384]{0:T(512)}, u32[]{:S(2)}) copy-start(f32[384]{0:T(512)} %get-tuple-element.4) | copy-start | bytes 4612
  48.0 16.6 %copy-start.25 = (f32[384]{0:T(512)S(1)}, f32[384]{0:T(512)}, u32[]{:S(2)}) copy-start(f32[384]{0:T(512)} %get-tuple-element.5) | copy-start | bytes 4612
  48.0 16.6 %copy-start.26 = (f32[384]{0:T(512)S(1)}, f32[384]{0:T(512)}, u32[]{:S(2)}) copy-start(f32[384]{0:T(512)} %get-tuple-element.6) | copy-start | bytes 4612
  48.1 16.8 %copy-start.16 = (f32[1,3,2,128]{3,1,2,0:T(4,128)}, f32[1,3,2,128]{3,1,2,0:T(4,128)S(1)}, u32[]{:S(2)}) copy-start(f32[1,3,2,128]{3,1,2,0:T(4,128)S(1)} %copy.107) | copy-start | bytes 9220
  48.3 20.1 %copy-start.33 = (f32[3]{0:T(128)}, f32[3]{0:T(128)S(1)}, u32[]{:S(2)}) copy-start(f32[3]{0:T(128)S(1)} %exp.50) | copy-start | bytes 40
  59.4 6.4 %collective-permute-start.5 = (bf16[3,512]{1,0:T(4,128)(2,1)S(1)}, bf16[3,512]{1,0:T(4,128)(2,1)S(1)}, u32[]{:S(2)}, u32[]{:S(2)}) collective-permute-start(bf16[3,512]{1,0:T(4,128)(2,1)S(1)} %slice.500), channel_id=1, source_target_pairs={{0,8},{8,16},{16,24},{24,32},{32,40},{40,48},{48,56},{56,64},{64,7... | collective-permute-start | bytes 9224 | tf_op jit(solution)/shard_map/ppermute | solution.py:23
  64.5 1.3 copy-start.30
  64.6 1.3 copy-start.19
  64.6 1.3 copy-start.20
  64.6 1.3 copy-start.21
  64.7 1.3 copy-start.22
  65.9 1.0 copy-start.5
  67.4 0.8 copy-start.2
  68.4 13.6 %copy-start.29 = (f32[256]{0:T(256)S(1)}, f32[256]{0:T(256)}, u32[]{:S(2)}) copy-start(f32[256]{0:T(256)} %copy-done.28) | copy-start | bytes 3076
  68.4 13.6 %copy-start.36 = (f32[64]{0:T(128)S(1)}, f32[64]{0:T(128)}, u32[]{:S(2)}) copy-start(f32[64]{0:T(128)} %copy-done.35) | copy-start | bytes 772
  69.5 31.1 %all-to-all-start = ((f32[32,3,5,256]{3,1,2,0:T(4,128)}), f32[32,3,5,256]{3,1,2,0:T(4,128)}, u32[]{:S(2)}, u32[]{:S(2)}) async-start(f32[32,3,5,256]{3,1,2,0:T(4,128)} %pad_maximum_fusion), calls=%async_computation | async-start | bytes 1310720 | tf_op jit(solution)/shard_map/all_to_all | solution.py:217
  100.7 2.2 %copy-start.10 = (f32[32,3,4,256]{3,1,2,0:T(4,128)S(1)}, f32[32,3,4,256]{3,1,2,0:T(4,128)}, u32[]{:S(2)}) copy-start(f32[32,3,4,256]{3,1,2,0:T(4,128)} %constant_dynamic-update-slice_fusion.31) | copy-start | bytes 1179652
  104.4 23.0 %all-to-all-start.1 = ((f32[32,3,4,256]{3,2,1,0:T(4,128)}), f32[32,3,4,256]{3,2,1,0:T(4,128)}, u32[]{:S(2)}, u32[]{:S(2)}) async-start(f32[32,3,4,256]{3,2,1,0:T(4,128)} %copy.76), calls=%async_computation.1 | async-start | bytes 786432 | tf_op jit(solution)/shard_map/all_to_all | solution.py:224
  110.1 99.9 %reduce-scatter.2.cloned.1.call-start = ((), (), s32[]{:S(2)}) async-start(), calls=%async_computation.4 | async-start | bytes 1966080 | tf_op jit(solution)/shard_map/reduce_scatter | solution.py:259
  116.8 15.7 %copy-start.17 = (f32[1,3,2,128]{3,1,2,0:T(4,128)S(1)}, f32[1,3,2,128]{3,1,2,0:T(4,128)}, u32[]{:S(2)}) copy-start(f32[1,3,2,128]{3,1,2,0:T(4,128)} %copy-done.16) | copy-start | bytes 9220
  116.8 15.7 %copy-start.31 = (f32[256,3]{0,1:T(4,128)S(1)}, f32[256,3]{0,1:T(4,128)}, u32[]{:S(2)}) copy-start(f32[256,3]{0,1:T(4,128)} %get-tuple-element.76) | copy-start | bytes 9220
  116.8 15.7 %copy-start.41 = (f32[3]{0:T(128)S(1)}, f32[3]{0:T(128)}, u32[]{:S(2)}) copy-start(f32[3]{0:T(128)} %param.30) | copy-start | bytes 40
  132.5 2.6 %copy-start.18 = (f32[384]{0:T(512)S(1)}, f32[384]{0:T(512)}, u32[]{:S(2)}) copy-start(f32[384]{0:T(512)} %convert_element_type.85) | copy-start | bytes 4612
  183.9 1.0 copy-start.3
  183.9 1.1 copy-start.4
  183.9 1.1 copy-start.34
Sparse Core Ops, SparseCore 0:
  50.2 109.5 all-gather.1
  184.0 25.9 reduce-scatter.1

commit v11 on v10

--- a/solution.py
+++ b/solution.py
@@ -254,10 +254,17 @@
         tokens, local_heads * HD
     )
     attended = attended.astype(jnp.bfloat16)
-    term = jnp.dot(attended, w_attn_out, preferred_element_type=jnp.float32)
-    term = term + jnp.dot(mixed, w_mamba_out, preferred_element_type=jnp.float32)
-    summed = lax.psum_scatter(term.astype(jnp.bfloat16), "mp", scatter_dimension=1, tiled=True)
-    summed = summed.astype(jnp.float32)
+    mp_count = lax.axis_size("mp")
+    out_cols = w_attn_out.shape[1] // mp_count
+    attn_cols = lax.all_to_all(
+        w_attn_out.reshape(w_attn_out.shape[0], mp_count, out_cols), "mp", 1, 0, tiled=True
+    ).reshape(w_attn_out.shape[0] * mp_count, out_cols)
+    mamba_term = jnp.dot(mixed, w_mamba_out, preferred_element_type=jnp.float32)
+    summed = lax.psum_scatter(mamba_term.astype(jnp.bfloat16), "mp", scatter_dimension=1, tiled=True)
+    attended_all = lax.all_gather(attended, "mp", axis=1, tiled=True)
+    summed = summed.astype(jnp.float32) + jnp.dot(
+        attended_all, attn_cols, preferred_element_type=jnp.float32
+    )
     layer = (summed + own_rows.astype(jnp.float32)).astype(jnp.bfloat16)
     return (layer[None], kv_block[None], state_after[None, None])
 

time: 220 us -> 212 us (0.964)
  waiting for transfers between devices: 81.1 us -> 51.5 us
  blocking collectives: 9.32 us -> 21.9 us
  starting transfers between devices: 29.1 us -> 34.7 us
  local copies, waits for them, and re-layouts: 25.2 us -> 27.8 us
    reduce_scatter x1, waiting for transfers between devices: 24.1 us -> 0.01 us  [shards(): lax.psum_scatter(mamba_term.astype(jnp.bfloat16), 'mp', scatter_dimension...]
    all_gather x0 -> x1, blocking collectives: none -> 11.3 us  [shards(): attended_all = lax.all_gather(attended, 'mp', axis=1, tiled=True)]
    all_gather x1, waiting for transfers between devices: 24.5 us -> 16.4 us  [shards(): piece = lax.all_gather(group_rows, 'seq', axis=0, tiled=True)]
    all_to_all x1, waiting for transfers between devices: 14.8 us -> 21.7 us  [shards(): lax.all_to_all(jnp.concatenate([pieces, decays], axis=2), 'seq', 0, 0, ti...]
    all_to_all x0 -> x1, starting transfers between devices: none -> 4.37 us  [shards(): lax.all_to_all(w_attn_out.reshape(w_attn_out.shape[0], mp_count, out_cols...]
    all_to_all x1, waiting for transfers between devices: 9.38 us -> 5.2 us  [shards(): lax.all_to_all(jnp.stack(entering, axis=0), 'seq', 0, 0, tiled=True)]
    all_to_all x0 -> x1, local copies, waits for them, and re-layouts: none -> 2.62 us  [shards(): lax.all_to_all(w_attn_out.reshape(w_attn_out.shape[0], mp_count, out_cols...]
    unnamed x91 -> x74, local copies, waits for them, and re-layouts: 6.1 us -> 6.42 us
  transfers between devices with their start and end apart: 10 -> 11, of which waited for: 5 -> 4; matrix products, arithmetic and copies ran while one was open for 22% -> 26% of each run, Pallas kernels for 0% -> 9%
where the time goes in v11:
time: 212 us; the launch traced here: 209 us
  waiting for transfers between devices  51.5 us (24%)
  starting transfers between devices  34.7 us (16%)
  local copies, waits for them, and re-layouts  27.8 us (13%)
  blocking collectives  21.9 us (10%)
  Pallas kernels  19.7 us (9%)
  other arithmetic  19.5 us (9%)
  matrix products  17.2 us (8%)
  between operations  17.1 us (8%)
    all_to_all x1, waiting for transfers between devices, shards(): lax.all_to_all(jnp.concatenate([pieces, decays], axis=2), 'seq', 0, 0, ti...  21.7 us
    pallas_call x1, Pallas kernels, attend(): pl.pallas_call(kernel, grid=(steps,), in_specs=[pl.BlockSpec((rows, 1), l...  19.7 us
    all_gather x1, waiting for transfers between devices, shards(): piece = lax.all_gather(group_rows, 'seq', axis=0, tiled=True)  16.4 us
    all_gather x1, blocking collectives, shards(): attended_all = lax.all_gather(attended, 'mp', axis=1, tiled=True)  11.3 us
    all_gather x1, blocking collectives, shards(): bc_all = lax.all_gather(bc_block, 'mp', axis=1, tiled=True)  10.6 us
    all_to_all x1, starting transfers between devices, shards(): lax.all_to_all(jnp.concatenate([pieces, decays], axis=2), 'seq', 0, 0, ti...  10.2 us
    ppermute x3, waiting for transfers between devices, shards(): lax.ppermute(own_rows, 'mp', [(i, (i + shift) % mp_count) for i in range(...  8.1 us
    all_to_all x1, starting transfers between devices, shards(): lax.all_to_all(jnp.stack(entering, axis=0), 'seq', 0, 0, tiled=True)  7.29 us
  transfers between devices with their start and end apart: 11, of which 4 were waited for; matrix products, arithmetic and copies ran while one was open for 26% of the time, Pallas kernels for 9%

profile of v11, /device:TPU:1, one launch (start us, length us, event | category | flops | bytes accessed | tf_op | source)
XLA Modules:
  0.0 209.4 jit_solution(12033615300662222559)
XLA Ops:
  8.1 2.1 %collective-permute-start = (bf16[256,768]{1,0:T(8,128)(2,1)}, bf16[256,768]{1,0:T(8,128)(2,1)}, u32[]{:S(2)}, u32[]{:S(2)}) collective-permute-start(bf16[256,768]{1,0:T(8,128)(2,1)} %bitcast.331), channel_id=1, source_target_pairs={{0,2},{2,4},{4,6},{6,0},{1,3},{3,5},{5,7},{7,1},{8,10},{10,12},{12... | collective-permute-start | bytes 1179656 | tf_op jit(solution)/shard_map/ppermute | solution.py:159
  10.2 2.5 %collective-permute-start.1 = (bf16[256,768]{1,0:T(8,128)(2,1)}, bf16[256,768]{1,0:T(8,128)(2,1)S(1)}, u32[]{:S(2)}, u32[]{:S(2)}) collective-permute-start(bf16[256,768]{1,0:T(8,128)(2,1)} %bitcast.332), channel_id=1, source_target_pairs={{0,4},{2,6},{4,0},{6,2},{1,5},{3,7},{5,1},{7,3},{8,12},{10,14},{12... | collective-permute-start | bytes 1179656 | tf_op jit(solution)/shard_map/ppermute | solution.py:159
  12.7 1.2 collective-permute-start.2
  13.8 1.4 broadcast_in_dim.30
  15.2 0.8 constant_dynamic-update-slice_fusion.35
  16.0 0.6 slice_convert_fusion.4
  17.4 0.7 convert_element_type.75
  18.0 1.2 exp.44
  19.3 0.6 convert_reduce_fusion.3
  19.9 1.8 constant_dynamic-update-slice_fusion.34
  21.7 8.1 %collective-permute-done.1 = bf16[256,768]{1,0:T(8,128)(2,1)S(1)} collective-permute-done((bf16[256,768]{1,0:T(8,128)(2,1)}, bf16[256,768]{1,0:T(8,128)(2,1)S(1)}, u32[]{:S(2)}, u32[]{:S(2)}) %collective-permute-start.1) | collective-permute-done | bytes 393248 | tf_op jit(solution)/shard_map/ppermute | solution.py:159
  29.8 0.8 constant_dynamic-update-slice_fusion.33
  30.6 0.9 constant_dynamic-update-slice_fusion.32
  31.5 1.8 fusion.2
  33.3 2.0 fusion.4
  35.4 0.6 fusion.69
  36.0 0.6 fusion.50
  36.7 0.7 pad_maximum_fusion.2
  37.7 1.4 fusion.8
  39.2 3.5 %collective-permute-start.3 = (bf16[3,384]{1,0:T(4,128)(2,1)S(1)}, bf16[3,384]{1,0:T(4,128)(2,1)S(1)}, u32[]{:S(2)}, u32[]{:S(2)}) collective-permute-start(bf16[3,384]{1,0:T(4,128)(2,1)S(1)} %slice_bitcast_fusion.63), channel_id=1, source_target_pairs={{0,8},{8,16},{16,24},{24,32},{32,40},{40,48},{48,56},{56,64},{64,7... | collective-permute-start | bytes 6920 | tf_op jit(solution)/shard_map/ppermute | solution.py:23
  42.8 0.5 fusion.60
  43.3 0.9 reduce-window.6
  44.6 2.0 convolution_convert_fusion.1
  46.9 10.6 %all_gather.9 = bf16[256,512]{1,0:T(8,128)(2,1)S(1)} all-gather(bf16[256,128]{1,0:T(8,128)(2,1)S(1)} %convolution_convert_fusion.1), channel_id=1, replica_groups=mesh['seq'=32,'mp'=4,'req'=2] {'mp'}, dimensions={1}, use_global_device_ids=true | all-gather | bytes 327680 | tf_op jit(solution)/shard_map/all_gather | solution.py:177
  57.5 3.2 %collective-permute-start.4 = (bf16[3,512]{1,0:T(4,128)(2,1)S(1)}, bf16[3,512]{1,0:T(4,128)(2,1)S(1)}, u32[]{:S(2)}, u32[]{:S(2)}) collective-permute-start(bf16[3,512]{1,0:T(4,128)(2,1)S(1)} %slice.496), channel_id=1, source_target_pairs={{0,8},{8,16},{16,24},{24,32},{32,40},{40,48},{48,56},{56,64},{64,7... | collective-permute-start | bytes 9224 | tf_op jit(solution)/shard_map/ppermute | solution.py:23
  60.7 0.8 maximum_select_fusion
  61.5 1.8 slice_convert_fusion
  63.3 0.6 compare_select_fusion.1
  64.3 0.9 copy.82
  65.7 0.6 copy-done.3
  66.3 0.5 fusion.30
  67.1 1.0 pad_maximum_fusion
  68.1 10.2 %all-to-all-start = ((f32[32,3,5,256]{3,1,2,0:T(4,128)}), f32[32,3,5,256]{3,1,2,0:T(4,128)}, u32[]{:S(2)}, u32[]{:S(2)}) async-start(f32[32,3,5,256]{3,1,2,0:T(4,128)} %pad_maximum_fusion), calls=%async_computation | async-start | bytes 1310720 | tf_op jit(solution)/shard_map/all_to_all | solution.py:217
  78.4 0.8 constant_dynamic-slice_fusion
  79.2 0.6 constant_dynamic-update-slice_fusion.31
  79.8 21.7 %all-to-all-done = f32[32,3,5,256]{3,1,2,0:T(4,128)} async-done(((f32[32,3,5,256]{3,1,2,0:T(4,128)}), f32[32,3,5,256]{3,1,2,0:T(4,128)}, u32[]{:S(2)}, u32[]{:S(2)}) %all-to-all-start) | async-done | bytes 491552 | tf_op jit(solution)/shard_map/all_to_all | solution.py:217
  101.5 1.0 slice_bitcast_fusion.1
  102.5 0.9 slice_bitcast_fusion.20
  104.3 0.9 copy.87
  105.2 7.3 %all-to-all-start.1 = ((f32[32,3,4,256]{3,2,1,0:T(4,128)}), f32[32,3,4,256]{3,2,1,0:T(4,128)}, u32[]{:S(2)}, u32[]{:S(2)}) async-start(f32[32,3,4,256]{3,2,1,0:T(4,128)} %copy.87), calls=%async_computation.1 | async-start | bytes 786432 | tf_op jit(solution)/shard_map/all_to_all | solution.py:224
  112.5 2.6 %copy.96 = bf16[256,3072]{0,1:T(8,128)(2,1)} copy(bf16[256,3072]{1,0:T(8,128)(2,1)} %param.24) | data formatting | bytes 3145728 | tf_op args[4]
  115.1 0.6 iota_add_fusion
  115.7 0.6 iota_compare_fusion
  116.3 1.9 copy.89
  118.7 5.2 %all-to-all-done.1 = f32[32,3,4,256]{3,2,1,0:T(4,128)} async-done(((f32[32,3,4,256]{3,2,1,0:T(4,128)}), f32[32,3,4,256]{3,2,1,0:T(4,128)}, u32[]{:S(2)}, u32[]{:S(2)}) %all-to-all-start.1) | async-done | bytes 393248 | tf_op jit(solution)/shard_map/all_to_all | solution.py:224
  123.8 4.4 %all-to-all-start.2 = ((bf16[256,4,768]{0,2,1:T(8,128)(2,1)}), bf16[256,4,768]{0,2,1:T(8,128)(2,1)}, u32[]{:S(2)}, u32[]{:S(2)}) async-start(bf16[256,4,768]{0,2,1:T(8,128)(2,1)} %bitcast.327), calls=%async_computation.3 | async-start | bytes 3145728 | tf_op jit(solution)/shard_map/all_to_all | solution.py:259
  128.3 1.8 copy.88
  130.1 1.9 reshape.288
  132.0 1.5 convolution_multiply_fusion
  133.5 2.6 %multiply_reduce_fusion = (f32[256,3]{0,1:T(4,128)S(1)}, f32[256,3,128]{0,2,1:T(8,128)S(1)}) fusion(f32[256,3,128]{0,2,1:T(8,128)} %bitcast.339, f32[256,3,128]{0,2,1:T(8,128)} %bitcast.334, f32[3]{0:T(128)} %param.30, f32[256,3,128]{0,2,1:T(8,128)S(1)} %convolution_multiply_fusion, f32[256,3]{0,1:T(4,128)S(1)} %copy-done.22, f32[256,256]{1,0:T(8,128)S(1)} %fusion.41, ...), kind=kOutput, calls=%fused_computation.46 | convolution fusion | flops 303955200 | bytes 1909772 | tf_op jit(solution)/shard_map/tsh,shp->thp/dot_general | solution.py:209
  136.2 2.1 %convolution_convert_fusion = bf16[256,3072]{1,0:T(8,128)(2,1)} fusion(bf16[256,384]{0,1:T(8,128)(2,1)S(1)} %fusion.29, bf16[384,3072]{1,0:T(8,128)(2,1)S(1)} %copy-done), kind=kOutput, calls=%fused_computation.4 | convolution fusion | flops 604766208 | bytes 4128768 | tf_op jit(solution)/shard_map/dot_general | solution.py:262
  138.6 0.5 copy-done.29
  139.3 1.2 multiply_cosine_fusion.1
  140.5 2.7 %fusion.68 = f32[256,256]{0,1:T(8,128)S(1)} fusion(bf16[256,3072]{1,0:T(8,128)(2,1)} %copy-done.1, bf16[3072,256]{1,0:T(8,128)(2,1)} %param.22), kind=kOutput, calls=%fused_computation.263 | convolution fusion | flops 402653184 | bytes 3407872 | tf_op jit(solution)/shard_map/dot_general | solution.py:168
  143.2 0.7 fusion.67
  143.8 1.0 copy.102
  144.9 0.8 copy.101
  145.7 1.1 subtract_convert_fusion
  147.0 2.6 %copy.97 = bf16[4,256,1,768]{3,1,0,2:T(8,128)(2,1)} copy(bf16[4,256,1,768]{1,3,0,2:T(8,128)(2,1)} %bitcast.128) | data formatting | bytes 3145728 | tf_op jit(solution)/shard_map/all_to_all | solution.py:259
  149.6 1.9 add_bitcast_fusion
  151.5 16.4 %all-gather.2.cloned.1.call-done.kv_ref = bf16[16384,256]{1,0:T(8,128)(2,1)} async-done(((bf16[512,256]{1,0:T(8,128)(2,1)}), bf16[16384,256]{1,0:T(8,128)(2,1)}) %all-gather.2.cloned.1.call-update) | async-done | bytes 8388624 | tf_op jit(solution)/shard_map/all_gather | solution.py:240
  167.9 19.7 %shard_map.211 = bf16[512,128]{1,0:T(8,128)(2,1)S(1)} custom-call(s32[512,1]{1,0:T(8,128)S(1)} %bitcast.324, bf16[512,128]{1,0:T(8,128)(2,1)S(1)} %bitcast.325, s32[1,16384]{1,0:T(1,128)S(1)} %compare_select_fusion.kr_ref, bf16[16384,256]{1,0:T(8,128)(2,1)} %all-gather.2.cloned.1.call-done.kv_ref), custom_call_target="tpu_custom_call" | custom-call | tf_op jit(solution)/shard_map/pallas_call | solution.py:73
  187.7 11.3 %all_gather.11 = bf16[256,1024]{0,1:T(8,128)(2,1)S(1)} all-gather(bf16[256,256]{0,1:T(8,128)(2,1)S(1)} %bitcast.338), channel_id=1, replica_groups=mesh['seq'=32,'mp'=4,'req'=2] {'mp'}, dimensions={1}, use_global_device_ids=true | all-gather | bytes 655360 | tf_op jit(solution)/shard_map/all_gather | solution.py:264
  199.0 3.0 %fusion.13 = bf16[1,256,768]{2,1,0:T(8,128)(2,1)} fusion(bf16[256,1024]{0,1:T(8,128)(2,1)S(1)} %all_gather.11, bf16[1024,768]{1,0:T(8,128)(2,1)} %bitcast.328, bf16[256,768]{1,0:T(8,128)(2,1)} %reduce-scatter.2.cloned.1.call-done, bf16[1,256,768]{2,1,0:T(8,128)(2,1)} %param.20), kind=kOutput, calls=%fused_computation.13 | convolution fusion | flops 403636224 | bytes 3276800 | tf_op jit(solution)/shard_map/dot_general | solution.py:265
  (158 shorter events, 4.1 us)
Async XLA Ops:
  8.0 128.2 %copy-start = (bf16[384,3072]{1,0:T(8,128)(2,1)S(1)}, bf16[384,3072]{1,0:T(8,128)(2,1)}, u32[]{:S(2)}) copy-start(bf16[384,3072]{1,0:T(8,128)(2,1)} %param.34) | copy-start | bytes 7077892
  8.0 7.2 %copy-start.2 = (bf16[1,256,768]{2,1,0:T(8,128)(2,1)S(1)}, bf16[1,256,768]{2,1,0:T(8,128)(2,1)}, u32[]{:S(2)}) copy-start(bf16[1,256,768]{2,1,0:T(8,128)(2,1)} %param.20) | copy-start | bytes 1179652
  8.0 8.0 %copy-start.11 = (bf16[4,512]{1,0:T(4,128)(2,1)S(1)}, bf16[4,512]{1,0:T(4,128)(2,1)}, u32[]{:S(2)}) copy-start(bf16[4,512]{1,0:T(4,128)(2,1)} %param.32) | copy-start | bytes 12292
  8.0 11.3 %copy-start.12 = (bf16[4,384]{1,0:T(4,128)(2,1)S(1)}, bf16[4,384]{1,0:T(4,128)(2,1)}, u32[]{:S(2)}) copy-start(bf16[4,384]{1,0:T(4,128)(2,1)} %param.31) | copy-start | bytes 9220
  8.0 159.9 %all-gather.2.cloned.1.call-start = ((), (), s32[]{:S(2)}) async-start(), calls=%async_computation.5 | async-start | bytes 8650752 | tf_op jit(solution)/shard_map/all_gather | solution.py:240
  8.1 11.8 %collective-permute-start = (bf16[256,768]{1,0:T(8,128)(2,1)}, bf16[256,768]{1,0:T(8,128)(2,1)}, u32[]{:S(2)}, u32[]{:S(2)}) collective-permute-start(bf16[256,768]{1,0:T(8,128)(2,1)} %bitcast.331), channel_id=1, source_target_pairs={{0,2},{2,4},{4,6},{6,0},{1,3},{3,5},{5,7},{7,1},{8,10},{10,12},{12... | collective-permute-start | bytes 1179656 | tf_op jit(solution)/shard_map/ppermute | solution.py:159
  10.2 19.6 %collective-permute-start.1 = (bf16[256,768]{1,0:T(8,128)(2,1)}, bf16[256,768]{1,0:T(8,128)(2,1)S(1)}, u32[]{:S(2)}, u32[]{:S(2)}) collective-permute-start(bf16[256,768]{1,0:T(8,128)(2,1)} %bitcast.332), channel_id=1, source_target_pairs={{0,4},{2,6},{4,0},{6,2},{1,5},{3,7},{5,1},{7,3},{8,12},{10,14},{12... | collective-permute-start | bytes 1179656 | tf_op jit(solution)/shard_map/ppermute | solution.py:159
  12.7 18.0 %collective-permute-start.2 = (bf16[256,768]{1,0:T(8,128)(2,1)}, bf16[256,768]{1,0:T(8,128)(2,1)S(1)}, u32[]{:S(2)}, u32[]{:S(2)}) collective-permute-start(bf16[256,768]{1,0:T(8,128)(2,1)} %bitcast.333), channel_id=1, source_target_pairs={{0,6},{2,0},{4,2},{6,4},{1,7},{3,1},{5,3},{7,5},{8,14},{10,8},{12,... | collective-permute-start | bytes 1179656 | tf_op jit(solution)/shard_map/ppermute | solution.py:159
  17.3 18.8 %copy-start.19 = (f32[256]{0:T(256)}, f32[256]{0:T(256)S(1)}, u32[]{:S(2)}) copy-start(f32[256]{0:T(256)S(1)} %add_convert_fusion.1) | copy-start | bytes 3076
  17.3 18.7 %copy-start.24 = (f32[64]{0:T(128)}, f32[64]{0:T(128)S(1)}, u32[]{:S(2)}) copy-start(f32[64]{0:T(128)S(1)} %multiply_power_fusion) | copy-start | bytes 772
  33.3 2.1 copy-start.4
  33.3 4.4 %copy-start.32 = (bf16[3072,2,384]{2,1,0:T(2,128)(2,1)S(1)}, bf16[3072,2,384]{2,1,0:T(2,128)(2,1)}, u32[]{:S(2)}) copy-start(bf16[3072,2,384]{2,1,0:T(2,128)(2,1)} %param.25) | copy-start | bytes 14155780
  35.4 7.3 %copy-start.1 = (bf16[256,3072]{1,0:T(8,128)(2,1)}, bf16[256,3072]{1,0:T(8,128)(2,1)S(1)}, u32[]{:S(2)}) copy-start(bf16[256,3072]{1,0:T(8,128)(2,1)S(1)} %fusion.4) | copy-start | bytes 4718596
  35.4 1.3 copy-start.9
  36.7 24.0 %copy-start.6 = (bf16[256,128]{1,0:T(8,128)(2,1)}, bf16[256,128]{1,0:T(8,128)(2,1)S(1)}, u32[]{:S(2)}) copy-start(bf16[256,128]{1,0:T(8,128)(2,1)S(1)} %fusion.53) | copy-start | bytes 196612
  37.4 5.3 %copy-start.10 = (bf16[3072,3]{0,1:T(4,128)(2,1)S(1)}, bf16[3072,3]{0,1:T(4,128)(2,1)}, u32[]{:S(2)}) copy-start(bf16[3072,3]{0,1:T(4,128)(2,1)} %param.27) | copy-start | bytes 55300
  37.4 5.3 %copy-start.30 = (f32[3]{0:T(128)S(1)}, f32[3]{0:T(128)}, u32[]{:S(2)}) copy-start(f32[3]{0:T(128)} %param.28) | copy-start | bytes 40
  37.4 5.3 %copy-start.31 = (f32[3]{0:T(128)S(1)}, f32[3]{0:T(128)}, u32[]{:S(2)}) copy-start(f32[3]{0:T(128)} %exp.44) | copy-start | bytes 40
  37.4 23.3 %collective-permute-start.5 = (bf16[512,128]{1,0:T(8,128)(2,1)}, bf16[512,128]{1,0:T(8,128)(2,1)S(1)}, u32[]{:S(2)}, u32[]{:S(2)}) collective-permute-start(bf16[512,128]{1,0:T(8,128)(2,1)} %pad_maximum_fusion.2), channel_id=1, source_target_pairs={{0,2},{2,0},{4,6},{6,4},{1,3},{3,1},{5,7},{7,5},{8,10},{10,8},{12,... | collective-permute-start | bytes 393224 | tf_op jit(solution)/shard_map/ppermute | solution.py:180
  39.1 4.2 %copy-start.8 = (bf16[256,2,384]{2,0,1:T(8,128)(2,1)}, bf16[256,2,384]{2,0,1:T(8,128)(2,1)S(1)}, u32[]{:S(2)}) copy-start(bf16[256,2,384]{2,0,1:T(8,128)(2,1)S(1)} %fusion.8) | copy-start | bytes 1179652
  39.2 5.5 %copy-start.5 = (bf16[3072,128]{1,0:T(8,128)(2,1)S(1)}, bf16[3072,128]{1,0:T(8,128)(2,1)}, u32[]{:S(2)}) copy-start(bf16[3072,128]{1,0:T(8,128)(2,1)} %param.26) | copy-start | bytes 2359300
  39.2 24.8 %collective-permute-start.3 = (bf16[3,384]{1,0:T(4,128)(2,1)S(1)}, bf16[3,384]{1,0:T(4,128)(2,1)S(1)}, u32[]{:S(2)}, u32[]{:S(2)}) collective-permute-start(bf16[3,384]{1,0:T(4,128)(2,1)S(1)} %slice_bitcast_fusion.63), channel_id=1, source_target_pairs={{0,8},{8,16},{16,24},{24,32},{32,40},{40,48},{48,56},{56,64},{64,7... | collective-permute-start | bytes 6920 | tf_op jit(solution)/shard_map/ppermute | solution.py:23
  46.6 17.3 %copy-start.23 = (bf16[1,3,384]{2,1,0:T(4,128)(2,1)S(1)}, bf16[1,3,384]{2,1,0:T(4,128)(2,1)}, u32[]{:S(2)}) copy-start(bf16[1,3,384]{2,1,0:T(4,128)(2,1)} %param.37) | copy-start | bytes 6916
  46.6 17.4 %copy-start.15 = (f32[384]{0:T(512)S(1)}, f32[384]{0:T(512)}, u32[]{:S(2)}) copy-start(f32[384]{0:T(512)} %get-tuple-element.3) | copy-start | bytes 4612
  46.6 17.4 %copy-start.16 = (f32[384]{0:T(512)S(1)}, f32[384]{0:T(512)}, u32[]{:S(2)}) copy-start(f32[384]{0:T(512)} %get-tuple-element.4) | copy-start | bytes 4612
  46.7 17.4 %copy-start.17 = (f32[384]{0:T(512)S(1)}, f32[384]{0:T(512)}, u32[]{:S(2)}) copy-start(f32[384]{0:T(512)} %get-tuple-element.5) | copy-start | bytes 4612
  46.7 17.4 %copy-start.18 = (f32[384]{0:T(512)S(1)}, f32[384]{0:T(512)}, u32[]{:S(2)}) copy-start(f32[384]{0:T(512)} %get-tuple-element.6) | copy-start | bytes 4612
  46.9 20.2 %copy-start.26 = (f32[3]{0:T(128)}, f32[3]{0:T(128)S(1)}, u32[]{:S(2)}) copy-start(f32[3]{0:T(128)S(1)} %exp.50) | copy-start | bytes 40
  57.5 7.8 %collective-permute-start.4 = (bf16[3,512]{1,0:T(4,128)(2,1)S(1)}, bf16[3,512]{1,0:T(4,128)(2,1)S(1)}, u32[]{:S(2)}, u32[]{:S(2)}) collective-permute-start(bf16[3,512]{1,0:T(4,128)(2,1)S(1)} %slice.496), channel_id=1, source_target_pairs={{0,8},{8,16},{16,24},{24,32},{32,40},{40,48},{48,56},{56,64},{64,7... | collective-permute-start | bytes 9224 | tf_op jit(solution)/shard_map/ppermute | solution.py:23
  64.0 1.3 copy-start.21
  64.1 1.3 copy-start.13
  64.1 1.3 copy-start.14
  65.3 1.0 copy-start.3
  68.1 33.3 %all-to-all-start = ((f32[32,3,5,256]{3,1,2,0:T(4,128)}), f32[32,3,5,256]{3,1,2,0:T(4,128)}, u32[]{:S(2)}, u32[]{:S(2)}) async-start(f32[32,3,5,256]{3,1,2,0:T(4,128)} %pad_maximum_fusion), calls=%async_computation | async-start | bytes 1310720 | tf_op jit(solution)/shard_map/all_to_all | solution.py:217
  101.5 2.2 %copy-start.7 = (f32[32,3,4,256]{3,1,2,0:T(4,128)S(1)}, f32[32,3,4,256]{3,1,2,0:T(4,128)}, u32[]{:S(2)}) copy-start(f32[32,3,4,256]{3,1,2,0:T(4,128)} %constant_dynamic-update-slice_fusion.31) | copy-start | bytes 1179652
  105.2 18.7 %all-to-all-start.1 = ((f32[32,3,4,256]{3,2,1,0:T(4,128)}), f32[32,3,4,256]{3,2,1,0:T(4,128)}, u32[]{:S(2)}, u32[]{:S(2)}) async-start(f32[32,3,4,256]{3,2,1,0:T(4,128)} %copy.87), calls=%async_computation.1 | async-start | bytes 786432 | tf_op jit(solution)/shard_map/all_to_all | solution.py:224
  112.5 2.6 %copy-start.28 = (bf16[384]{0:T(512)(128)(2,1)S(1)}, bf16[384]{0:T(512)(128)(2,1)}, u32[]{:S(2)}) copy-start(bf16[384]{0:T(512)(128)(2,1)} %param.33) | copy-start | bytes 2308
  123.8 23.1 %all-to-all-start.2 = ((bf16[256,4,768]{0,2,1:T(8,128)(2,1)}), bf16[256,4,768]{0,2,1:T(8,128)(2,1)}, u32[]{:S(2)}, u32[]{:S(2)}) async-start(bf16[256,4,768]{0,2,1:T(8,128)(2,1)} %bitcast.327), calls=%async_computation.3 | async-start | bytes 3145728 | tf_op jit(solution)/shard_map/all_to_all | solution.py:259
  128.2 5.3 %copy-start.22 = (f32[256,3]{0,1:T(4,128)S(1)}, f32[256,3]{0,1:T(4,128)}, u32[]{:S(2)}) copy-start(f32[256,3]{0,1:T(4,128)} %get-tuple-element.76) | copy-start | bytes 9220
  128.2 70.8 %reduce-scatter.2.cloned.1.call-start = ((), (), s32[]{:S(2)}) async-start(), calls=%async_computation.4 | async-start | bytes 1966080 | tf_op jit(solution)/shard_map/reduce_scatter | solution.py:263
  138.4 0.7 copy-start.29
  138.4 0.8 copy-start.20
  138.4 0.9 copy-start.25
  147.0 2.6 %copy-start.27 = (f32[3]{0:T(128)S(1)}, f32[3]{0:T(128)}, u32[]{:S(2)}) copy-start(f32[3]{0:T(128)} %copy-done.26) | copy-start | bytes 40
Sparse Core Ops, SparseCore 0:
  61.6 106.2 all-gather.1
Sparse Core Ops, SparseCore 1:
  138.5 28.3 reduce-scatter.1

commit v12 on v11

--- a/solution.py
+++ b/solution.py
@@ -261,7 +261,15 @@
     ).reshape(w_attn_out.shape[0] * mp_count, out_cols)
     mamba_term = jnp.dot(mixed, w_mamba_out, preferred_element_type=jnp.float32)
     summed = lax.psum_scatter(mamba_term.astype(jnp.bfloat16), "mp", scatter_dimension=1, tiled=True)
-    attended_all = lax.all_gather(attended, "mp", axis=1, tiled=True)
+    head_cols = attended.shape[1]
+    attended_all = jnp.zeros((tokens, mp_count * head_cols), attended.dtype)
+    for shift in range(mp_count):
+        if shift == 0:
+            part = attended
+        else:
+            part = lax.ppermute(attended, "mp", [(i, (i + shift) % mp_count) for i in range(mp_count)])
+        source = (mp_pos + mp_count - shift) % mp_count
+        attended_all = lax.dynamic_update_slice(attended_all, part, (0, source * head_cols))
     summed = summed.astype(jnp.float32) + jnp.dot(
         attended_all, attn_cols, preferred_element_type=jnp.float32
     )

time: 212 us -> 205 us (0.967)
  blocking collectives: 21.9 us -> 10.2 us
  starting transfers between devices: 34.7 us -> 40.3 us
  matrix products: 17.2 us -> 19.8 us
    all_gather x1 -> x0, blocking collectives: 11.3 us -> none  [shards(): attended_all = lax.all_gather(attended, 'mp', axis=1, tiled=True)]
    all_gather x1, waiting for transfers between devices: 16.4 us -> 7.76 us  [shards(): piece = lax.all_gather(group_rows, 'seq', axis=0, tiled=True)]
    all_to_all x1, waiting for transfers between devices: 5.2 us -> 10.7 us  [shards(): lax.all_to_all(jnp.stack(entering, axis=0), 'seq', 0, 0, tiled=True)]
    ppermute x0 -> x3, starting transfers between devices: none -> 4.84 us  [shards(): lax.ppermute(attended, 'mp', [(i, (i + shift) % mp_count) for i in range(...]
    ppermute x0 -> x3, waiting for transfers between devices: none -> 4.22 us  [shards(): lax.ppermute(attended, 'mp', [(i, (i + shift) % mp_count) for i in range(...]
    all_to_all x1, waiting for transfers between devices: 21.7 us -> 18.9 us  [shards(): lax.all_to_all(jnp.concatenate([pieces, decays], axis=2), 'seq', 0, 0, ti...]
    dot_general x1, matrix products: 1.42 us -> 3.84 us  [shards(): jnp.einsum('td,dkc->tkc', normed, w_inner, preferred_element_type=jnp.flo...]
    all_to_all x1, starting transfers between devices: 10.2 us -> 12.5 us  [shards(): lax.all_to_all(jnp.concatenate([pieces, decays], axis=2), 'seq', 0, 0, ti...]
  transfers between devices with their start and end apart: 11 -> 14, of which waited for: 4 -> 6; matrix products, arithmetic and copies ran while one was open for 26% -> 24% of each run, Pallas kernels for 9% -> 10%
where the time goes in v12:
time: 205 us; the launch traced here: 204 us
  waiting for transfers between devices  49.5 us (24%)
  starting transfers between devices  40.3 us (20%)
  local copies, waits for them, and re-layouts  28.9 us (14%)
  matrix products  19.8 us (10%)
  Pallas kernels  19.7 us (10%)
  other arithmetic  18.1 us (9%)
  between operations  17.1 us (8%)
  blocking collectives  10.2 us (5%)
    pallas_call x1, Pallas kernels, attend(): pl.pallas_call(kernel, grid=(steps,), in_specs=[pl.BlockSpec((rows, 1), l...  19.7 us
    all_to_all x1, waiting for transfers between devices, shards(): lax.all_to_all(jnp.concatenate([pieces, decays], axis=2), 'seq', 0, 0, ti...  18.9 us
    all_to_all x1, starting transfers between devices, shards(): lax.all_to_all(jnp.concatenate([pieces, decays], axis=2), 'seq', 0, 0, ti...  12.5 us
    all_to_all x1, waiting for transfers between devices, shards(): lax.all_to_all(jnp.stack(entering, axis=0), 'seq', 0, 0, tiled=True)  10.7 us
    all_gather x1, blocking collectives, shards(): bc_all = lax.all_gather(bc_block, 'mp', axis=1, tiled=True)  10.2 us
    ppermute x3, waiting for transfers between devices, shards(): lax.ppermute(own_rows, 'mp', [(i, (i + shift) % mp_count) for i in range(...  7.8 us
    all_gather x1, waiting for transfers between devices, shards(): piece = lax.all_gather(group_rows, 'seq', axis=0, tiled=True)  7.76 us
    unnamed x72, local copies, waits for them, and re-layouts  7.59 us
  transfers between devices with their start and end apart: 14, of which 6 were waited for; matrix products, arithmetic and copies ran while one was open for 24% of the time, Pallas kernels for 10%

profile of v12, /device:TPU:1, one launch (start us, length us, event | category | flops | bytes accessed | tf_op | source)
XLA Modules:
  0.0 203.7 jit_solution(16062219992516722926)
XLA Ops:
  8.1 2.1 %collective-permute-start = (bf16[256,768]{1,0:T(8,128)(2,1)}, bf16[256,768]{1,0:T(8,128)(2,1)}, u32[]{:S(2)}, u32[]{:S(2)}) collective-permute-start(bf16[256,768]{1,0:T(8,128)(2,1)} %bitcast.331), channel_id=1, source_target_pairs={{0,2},{2,4},{4,6},{6,0},{1,3},{3,5},{5,7},{7,1},{8,10},{10,12},{12... | collective-permute-start | bytes 1179656 | tf_op jit(solution)/shard_map/ppermute | solution.py:159
  10.2 2.5 %collective-permute-start.1 = (bf16[256,768]{1,0:T(8,128)(2,1)}, bf16[256,768]{1,0:T(8,128)(2,1)S(1)}, u32[]{:S(2)}, u32[]{:S(2)}) collective-permute-start(bf16[256,768]{1,0:T(8,128)(2,1)} %bitcast.332), channel_id=1, source_target_pairs={{0,4},{2,6},{4,0},{6,2},{1,5},{3,7},{5,1},{7,3},{8,12},{10,14},{12... | collective-permute-start | bytes 1179656 | tf_op jit(solution)/shard_map/ppermute | solution.py:159
  12.7 1.2 collective-permute-start.2
  13.8 1.4 broadcast_in_dim.36
  15.2 0.8 constant_dynamic-update-slice_fusion.39
  17.8 0.7 convert_element_type.75
  18.5 1.2 exp.44
  19.6 0.6 convert_reduce_fusion.3
  20.2 1.8 constant_dynamic-update-slice_fusion.38
  22.0 7.8 %collective-permute-done.1 = bf16[256,768]{1,0:T(8,128)(2,1)S(1)} collective-permute-done((bf16[256,768]{1,0:T(8,128)(2,1)}, bf16[256,768]{1,0:T(8,128)(2,1)S(1)}, u32[]{:S(2)}, u32[]{:S(2)}) %collective-permute-start.1) | collective-permute-done | bytes 393248 | tf_op jit(solution)/shard_map/ppermute | solution.py:159
  29.8 0.9 constant_dynamic-update-slice_fusion.37
  30.7 0.8 constant_dynamic-update-slice_fusion.36
  31.5 1.8 fusion.2
  33.4 1.9 fusion.4
  35.3 1.2 copy-done.1
  37.0 0.9 reduce-window.6
  38.3 2.1 %convolution_convert_fusion.1 = bf16[256,128]{1,0:T(8,128)(2,1)S(1)} fusion(bf16[256,3072]{1,0:T(8,128)(2,1)} %copy-done.1, bf16[3072,128]{1,0:T(8,128)(2,1)S(1)} %copy-done.6), kind=kOutput, calls=%fused_computation.19 | convolution fusion | flops 201359360 | bytes 2424832 | tf_op jit(solution)/shard_map/dot_general | solution.py:176
  40.4 3.8 %fusion.8 = bf16[256,2,384]{2,0,1:T(8,128)(2,1)S(1)} fusion(bf16[3072,2,384]{2,1,0:T(2,128)(2,1)} %param.25, bf16[256,3072]{1,0:T(8,128)(2,1)S(1)} %copy-done.2), kind=kOutput, calls=%fused_computation.12 | convolution fusion | flops 1208156160 | bytes 6684672 | tf_op jit(solution)/shard_map/td,dkc->tkc/dot_general | solution.py:187
  44.3 0.6 fusion.69
  44.9 0.6 fusion.50
  46.2 3.4 %collective-permute-start.3 = (bf16[3,384]{1,0:T(4,128)(2,1)S(1)}, bf16[3,384]{1,0:T(4,128)(2,1)S(1)}, u32[]{:S(2)}, u32[]{:S(2)}) collective-permute-start(bf16[3,384]{1,0:T(4,128)(2,1)S(1)} %slice_bitcast_fusion.63), channel_id=1, source_target_pairs={{0,8},{8,16},{16,24},{24,32},{32,40},{40,48},{48,56},{56,64},{64,7... | collective-permute-start | bytes 6920 | tf_op jit(solution)/shard_map/ppermute | solution.py:23
  49.8 0.8 maximum_select_fusion
  50.6 0.6 compare_select_fusion.1
  51.2 0.8 slice_convert_fusion
  52.0 10.2 %all_gather.6 = bf16[256,512]{1,0:T(8,128)(2,1)S(1)} all-gather(bf16[256,128]{1,0:T(8,128)(2,1)S(1)} %convolution_convert_fusion.1), channel_id=1, replica_groups=mesh['seq'=32,'mp'=4,'req'=2] {'mp'}, dimensions={1}, use_global_device_ids=true | all-gather | bytes 327680 | tf_op jit(solution)/shard_map/all_gather | solution.py:177
  62.2 3.0 %collective-permute-start.4 = (bf16[3,512]{1,0:T(4,128)(2,1)S(1)}, bf16[3,512]{1,0:T(4,128)(2,1)S(1)}, u32[]{:S(2)}, u32[]{:S(2)}) collective-permute-start(bf16[3,512]{1,0:T(4,128)(2,1)S(1)} %slice.496), channel_id=1, source_target_pairs={{0,8},{8,16},{16,24},{24,32},{32,40},{40,48},{48,56},{56,64},{64,7... | collective-permute-start | bytes 9224 | tf_op jit(solution)/shard_map/ppermute | solution.py:23
  65.7 0.9 copy.82
  67.1 0.6 copy-done.4
  68.5 1.0 pad_maximum_fusion
  69.5 12.5 %all-to-all-start = ((f32[32,3,5,256]{3,1,2,0:T(4,128)}), f32[32,3,5,256]{3,1,2,0:T(4,128)}, u32[]{:S(2)}, u32[]{:S(2)}) async-start(f32[32,3,5,256]{3,1,2,0:T(4,128)} %pad_maximum_fusion), calls=%async_computation | async-start | bytes 1310720 | tf_op jit(solution)/shard_map/all_to_all | solution.py:217
  82.0 0.8 constant_dynamic-slice_fusion
  82.7 0.6 constant_dynamic-update-slice_fusion.31
  83.3 18.9 %all-to-all-done = f32[32,3,5,256]{3,1,2,0:T(4,128)} async-done(((f32[32,3,5,256]{3,1,2,0:T(4,128)}), f32[32,3,5,256]{3,1,2,0:T(4,128)}, u32[]{:S(2)}, u32[]{:S(2)}) %all-to-all-start) | async-done | bytes 491552 | tf_op jit(solution)/shard_map/all_to_all | solution.py:217
  102.3 1.0 slice_bitcast_fusion.1
  103.4 0.9 slice_bitcast_fusion.20
  105.1 0.9 copy.87
  106.0 6.0 %all-to-all-start.1 = ((f32[32,3,4,256]{3,2,1,0:T(4,128)}), f32[32,3,4,256]{3,2,1,0:T(4,128)}, u32[]{:S(2)}, u32[]{:S(2)}) async-start(f32[32,3,4,256]{3,2,1,0:T(4,128)} %copy.87), calls=%async_computation.1 | async-start | bytes 786432 | tf_op jit(solution)/shard_map/all_to_all | solution.py:224
  112.0 2.6 %copy.96 = bf16[256,3072]{0,1:T(8,128)(2,1)} copy(bf16[256,3072]{1,0:T(8,128)(2,1)} %param.24) | data formatting | bytes 3145728 | tf_op args[4]
  114.6 0.6 iota_add_fusion
  115.2 0.6 iota_compare_fusion
  115.8 1.9 copy.89
  118.2 10.7 %all-to-all-done.1 = f32[32,3,4,256]{3,2,1,0:T(4,128)} async-done(((f32[32,3,4,256]{3,2,1,0:T(4,128)}), f32[32,3,4,256]{3,2,1,0:T(4,128)}, u32[]{:S(2)}, u32[]{:S(2)}) %all-to-all-start.1) | async-done | bytes 393248 | tf_op jit(solution)/shard_map/all_to_all | solution.py:224
  128.9 4.4 %all-to-all-start.2 = ((bf16[256,4,768]{0,2,1:T(8,128)(2,1)}), bf16[256,4,768]{0,2,1:T(8,128)(2,1)}, u32[]{:S(2)}, u32[]{:S(2)}) async-start(bf16[256,4,768]{0,2,1:T(8,128)(2,1)} %bitcast.327), calls=%async_computation.3 | async-start | bytes 3145728 | tf_op jit(solution)/shard_map/all_to_all | solution.py:259
  133.3 1.8 copy.88
  135.1 1.9 reshape.288
  136.9 1.5 convolution_multiply_fusion
  138.5 2.6 %multiply_reduce_fusion = (f32[256,3]{0,1:T(4,128)S(1)}, f32[256,3,128]{0,2,1:T(8,128)S(1)}) fusion(f32[256,3,128]{0,2,1:T(8,128)} %bitcast.342, f32[256,3,128]{0,2,1:T(8,128)} %bitcast.334, f32[3]{0:T(128)} %param.30, f32[256,3,128]{0,2,1:T(8,128)S(1)} %convolution_multiply_fusion, f32[256,3]{0,1:T(4,128)S(1)} %copy-done.22, f32[256,256]{1,0:T(8,128)S(1)} %fusion.41, ...), kind=kOutput, calls=%fused_computation.46 | convolution fusion | flops 303955200 | bytes 1909772 | tf_op jit(solution)/shard_map/tsh,shp->thp/dot_general | solution.py:209
  141.2 2.2 %convolution_convert_fusion = bf16[256,3072]{1,0:T(8,128)(2,1)} fusion(bf16[256,384]{0,1:T(8,128)(2,1)S(1)} %fusion.29, bf16[384,3072]{1,0:T(8,128)(2,1)S(1)} %copy-done), kind=kOutput, calls=%fused_computation.4 | convolution fusion | flops 604766208 | bytes 4128768 | tf_op jit(solution)/shard_map/dot_general | solution.py:262
  144.3 1.2 multiply_cosine_fusion.1
  145.5 2.6 %fusion.68 = f32[256,256]{0,1:T(8,128)S(1)} fusion(bf16[256,3072]{1,0:T(8,128)(2,1)} %copy-done.1, bf16[3072,256]{1,0:T(8,128)(2,1)} %param.22), kind=kOutput, calls=%fused_computation.267 | convolution fusion | flops 402653184 | bytes 3407872 | tf_op jit(solution)/shard_map/dot_general | solution.py:168
  148.1 0.7 fusion.67
  148.8 1.0 copy.101
  149.8 0.8 copy.102
  150.7 1.1 subtract_convert_fusion
  151.9 2.6 %copy.97 = bf16[4,256,1,768]{3,1,0,2:T(8,128)(2,1)} copy(bf16[4,256,1,768]{1,3,0,2:T(8,128)(2,1)} %bitcast.129) | data formatting | bytes 3145728 | tf_op jit(solution)/shard_map/all_to_all | solution.py:259
  154.6 7.8 %all-gather.2.cloned.1.call-done.kv_ref = bf16[16384,256]{1,0:T(8,128)(2,1)} async-done(((bf16[512,256]{1,0:T(8,128)(2,1)}), bf16[16384,256]{1,0:T(8,128)(2,1)}) %all-gather.2.cloned.1.call-update) | async-done | bytes 8388624 | tf_op jit(solution)/shard_map/all_gather | solution.py:240
  162.3 19.7 %shard_map.211 = bf16[512,128]{1,0:T(8,128)(2,1)S(1)} custom-call(s32[512,1]{1,0:T(8,128)S(1)} %bitcast.324, bf16[512,128]{1,0:T(8,128)(2,1)S(1)} %bitcast.325, s32[1,16384]{1,0:T(1,128)S(1)} %compare_select_fusion.kr_ref, bf16[16384,256]{1,0:T(8,128)(2,1)} %all-gather.2.cloned.1.call-done.kv_ref), custom_call_target="tpu_custom_call" | custom-call | tf_op jit(solution)/shard_map/pallas_call | solution.py:73
  182.2 1.3 collective-permute-start.6
  183.5 1.9 add_bitcast_fusion
  185.3 2.4 %collective-permute-start.7 = (bf16[256,256]{0,1:T(8,128)(2,1)S(1)}, bf16[256,256]{0,1:T(8,128)(2,1)S(1)}, u32[]{:S(2)}, u32[]{:S(2)}) collective-permute-start(bf16[256,256]{0,1:T(8,128)(2,1)S(1)} %bitcast.339), channel_id=1, source_target_pairs={{0,4},{2,6},{4,0},{6,2},{1,5},{3,7},{5,1},{7,3},{8,12},{10,14},{12... | collective-permute-start | bytes 393224 | tf_op jit(solution)/shard_map/ppermute | solution.py:270
  187.7 1.2 collective-permute-start.8
  189.0 2.5 %collective-permute-done.7 = bf16[256,256]{0,1:T(8,128)(2,1)S(1)} collective-permute-done((bf16[256,256]{0,1:T(8,128)(2,1)S(1)}, bf16[256,256]{0,1:T(8,128)(2,1)S(1)}, u32[]{:S(2)}, u32[]{:S(2)}) %collective-permute-start.7) | collective-permute-done | bytes 131104 | tf_op jit(solution)/shard_map/ppermute | solution.py:270
  191.5 1.7 collective-permute-done.8
  193.3 3.0 %fusion.13 = bf16[1,256,768]{2,1,0:T(8,128)(2,1)} fusion(bf16[256,1024]{0,1:T(8,128)(2,1)S(1)} %constant_dynamic-update-slice_fusion.32, bf16[1024,768]{1,0:T(8,128)(2,1)} %bitcast.328, bf16[256,768]{1,0:T(8,128)(2,1)} %reduce-scatter.2.cloned.1.call-done, bf16[1,256,768]{2,1,0:T(8,128)(2,1)} %param.20), kind=kOutput, calls=%fused_computation.13 | convolution fusion | flops 403636224 | bytes 3276800 | tf_op jit(solution)/shard_map/dot_general | solution.py:273
  (166 shorter events, 7.0 us)
Async XLA Ops:
  8.0 133.2 %copy-start = (bf16[384,3072]{1,0:T(8,128)(2,1)S(1)}, bf16[384,3072]{1,0:T(8,128)(2,1)}, u32[]{:S(2)}) copy-start(bf16[384,3072]{1,0:T(8,128)(2,1)} %param.34) | copy-start | bytes 7077892
  8.0 7.2 %copy-start.3 = (bf16[1,256,768]{2,1,0:T(8,128)(2,1)S(1)}, bf16[1,256,768]{2,1,0:T(8,128)(2,1)}, u32[]{:S(2)}) copy-start(bf16[1,256,768]{2,1,0:T(8,128)(2,1)} %param.20) | copy-start | bytes 1179652
  8.0 8.0 %copy-start.11 = (bf16[4,512]{1,0:T(4,128)(2,1)S(1)}, bf16[4,512]{1,0:T(4,128)(2,1)}, u32[]{:S(2)}) copy-start(bf16[4,512]{1,0:T(4,128)(2,1)} %param.32) | copy-start | bytes 12292
  8.0 11.6 %copy-start.12 = (bf16[4,384]{1,0:T(4,128)(2,1)S(1)}, bf16[4,384]{1,0:T(4,128)(2,1)}, u32[]{:S(2)}) copy-start(bf16[4,384]{1,0:T(4,128)(2,1)} %param.31) | copy-start | bytes 9220
  8.0 154.3 %all-gather.2.cloned.1.call-start = ((), (), s32[]{:S(2)}) async-start(), calls=%async_computation.5 | async-start | bytes 8650752 | tf_op jit(solution)/shard_map/all_gather | solution.py:240
  8.1 12.1 %collective-permute-start = (bf16[256,768]{1,0:T(8,128)(2,1)}, bf16[256,768]{1,0:T(8,128)(2,1)}, u32[]{:S(2)}, u32[]{:S(2)}) collective-permute-start(bf16[256,768]{1,0:T(8,128)(2,1)} %bitcast.331), channel_id=1, source_target_pairs={{0,2},{2,4},{4,6},{6,0},{1,3},{3,5},{5,7},{7,1},{8,10},{10,12},{12... | collective-permute-start | bytes 1179656 | tf_op jit(solution)/shard_map/ppermute | solution.py:159
  10.2 19.6 %collective-permute-start.1 = (bf16[256,768]{1,0:T(8,128)(2,1)}, bf16[256,768]{1,0:T(8,128)(2,1)S(1)}, u32[]{:S(2)}, u32[]{:S(2)}) collective-permute-start(bf16[256,768]{1,0:T(8,128)(2,1)} %bitcast.332), channel_id=1, source_target_pairs={{0,4},{2,6},{4,0},{6,2},{1,5},{3,7},{5,1},{7,3},{8,12},{10,14},{12... | collective-permute-start | bytes 1179656 | tf_op jit(solution)/shard_map/ppermute | solution.py:159
  12.7 18.1 %collective-permute-start.2 = (bf16[256,768]{1,0:T(8,128)(2,1)}, bf16[256,768]{1,0:T(8,128)(2,1)S(1)}, u32[]{:S(2)}, u32[]{:S(2)}) collective-permute-start(bf16[256,768]{1,0:T(8,128)(2,1)} %bitcast.333), channel_id=1, source_target_pairs={{0,6},{2,0},{4,2},{6,4},{1,7},{3,1},{5,3},{7,5},{8,14},{10,8},{12,... | collective-permute-start | bytes 1179656 | tf_op jit(solution)/shard_map/ppermute | solution.py:159
  17.2 27.7 %copy-start.19 = (f32[256]{0:T(256)}, f32[256]{0:T(256)S(1)}, u32[]{:S(2)}) copy-start(f32[256]{0:T(256)S(1)} %add_convert_fusion.1) | copy-start | bytes 3076
  33.3 3.1 %copy-start.10 = (bf16[3072,3]{0,1:T(4,128)(2,1)S(1)}, bf16[3072,3]{0,1:T(4,128)(2,1)}, u32[]{:S(2)}) copy-start(bf16[3072,3]{0,1:T(4,128)(2,1)} %param.27) | copy-start | bytes 55300
  33.3 3.1 %copy-start.30 = (f32[3]{0:T(128)S(1)}, f32[3]{0:T(128)}, u32[]{:S(2)}) copy-start(f32[3]{0:T(128)} %param.28) | copy-start | bytes 40
  33.3 3.1 %copy-start.31 = (f32[3]{0:T(128)S(1)}, f32[3]{0:T(128)}, u32[]{:S(2)}) copy-start(f32[3]{0:T(128)} %exp.44) | copy-start | bytes 40
  35.3 1.2 copy-start.1
  36.5 1.8 copy-start.6
  38.3 2.1 %copy-start.2 = (bf16[256,3072]{1,0:T(8,128)(2,1)S(1)}, bf16[256,3072]{1,0:T(8,128)(2,1)}, u32[]{:S(2)}) copy-start(bf16[256,3072]{1,0:T(8,128)(2,1)} %copy-done.1) | copy-start | bytes 4718596
  40.4 3.9 %copy-start.5 = (bf16[3072,128]{1,0:T(8,128)(2,1)S(1)}, bf16[3072,128]{1,0:T(8,128)(2,1)}, u32[]{:S(2)}) copy-start(bf16[3072,128]{1,0:T(8,128)(2,1)} %param.23) | copy-start | bytes 2359300
  44.2 0.6 copy-start.24
  44.3 1.4 copy-start.9
  44.9 20.4 %copy-start.23 = (bf16[1,3,384]{2,1,0:T(4,128)(2,1)S(1)}, bf16[1,3,384]{2,1,0:T(4,128)(2,1)}, u32[]{:S(2)}) copy-start(bf16[1,3,384]{2,1,0:T(4,128)(2,1)} %param.37) | copy-start | bytes 6916
  45.6 20.1 %copy-start.7 = (bf16[256,128]{1,0:T(8,128)(2,1)}, bf16[256,128]{1,0:T(8,128)(2,1)S(1)}, u32[]{:S(2)}) copy-start(bf16[256,128]{1,0:T(8,128)(2,1)S(1)} %fusion.53) | copy-start | bytes 196612
  45.6 19.8 %copy-start.15 = (f32[384]{0:T(512)S(1)}, f32[384]{0:T(512)}, u32[]{:S(2)}) copy-start(f32[384]{0:T(512)} %get-tuple-element.3) | copy-start | bytes 4612
  45.6 19.8 %copy-start.16 = (f32[384]{0:T(512)S(1)}, f32[384]{0:T(512)}, u32[]{:S(2)}) copy-start(f32[384]{0:T(512)} %get-tuple-element.4) | copy-start | bytes 4612
  45.6 19.8 %copy-start.17 = (f32[384]{0:T(512)S(1)}, f32[384]{0:T(512)}, u32[]{:S(2)}) copy-start(f32[384]{0:T(512)} %get-tuple-element.5) | copy-start | bytes 4612
  45.6 19.8 %copy-start.18 = (f32[384]{0:T(512)S(1)}, f32[384]{0:T(512)}, u32[]{:S(2)}) copy-start(f32[384]{0:T(512)} %get-tuple-element.6) | copy-start | bytes 4612
  45.7 4.1 %collective-permute-start.5 = (bf16[512,128]{1,0:T(8,128)(2,1)S(1)}, bf16[512,128]{1,0:T(8,128)(2,1)S(1)}, u32[]{:S(2)}, u32[]{:S(2)}) collective-permute-start(bf16[512,128]{1,0:T(8,128)(2,1)S(1)} %pad_maximum_fusion.2), channel_id=1, source_target_pairs={{0,2},{2,0},{4,6},{6,4},{1,3},{3,1},{5,7},{7,5},{8,10},{10,8},{12,... | collective-permute-start | bytes 393224 | tf_op jit(solution)/shard_map/ppermute | solution.py:180
  46.2 19.1 %collective-permute-start.3 = (bf16[3,384]{1,0:T(4,128)(2,1)S(1)}, bf16[3,384]{1,0:T(4,128)(2,1)S(1)}, u32[]{:S(2)}, u32[]{:S(2)}) collective-permute-start(bf16[3,384]{1,0:T(4,128)(2,1)S(1)} %slice_bitcast_fusion.63), channel_id=1, source_target_pairs={{0,8},{8,16},{16,24},{24,32},{32,40},{40,48},{48,56},{56,64},{64,7... | collective-permute-start | bytes 6920 | tf_op jit(solution)/shard_map/ppermute | solution.py:23
  62.2 6.2 %copy-start.26 = (f32[3]{0:T(128)}, f32[3]{0:T(128)S(1)}, u32[]{:S(2)}) copy-start(f32[3]{0:T(128)S(1)} %exp.50) | copy-start | bytes 40
  62.2 4.4 %collective-permute-start.4 = (bf16[3,512]{1,0:T(4,128)(2,1)S(1)}, bf16[3,512]{1,0:T(4,128)(2,1)S(1)}, u32[]{:S(2)}, u32[]{:S(2)}) collective-permute-start(bf16[3,512]{1,0:T(4,128)(2,1)S(1)} %slice.496), channel_id=1, source_target_pairs={{0,8},{8,16},{16,24},{24,32},{32,40},{40,48},{48,56},{56,64},{64,7... | collective-permute-start | bytes 9224 | tf_op jit(solution)/shard_map/ppermute | solution.py:23
  65.3 1.3 copy-start.21
  65.4 1.3 copy-start.13
  65.5 1.3 copy-start.14
  66.6 1.0 copy-start.4
  69.5 32.7 %all-to-all-start = ((f32[32,3,5,256]{3,1,2,0:T(4,128)}), f32[32,3,5,256]{3,1,2,0:T(4,128)}, u32[]{:S(2)}, u32[]{:S(2)}) async-start(f32[32,3,5,256]{3,1,2,0:T(4,128)} %pad_maximum_fusion), calls=%async_computation | async-start | bytes 1310720 | tf_op jit(solution)/shard_map/all_to_all | solution.py:217
  102.3 2.2 %copy-start.8 = (f32[32,3,4,256]{3,1,2,0:T(4,128)S(1)}, f32[32,3,4,256]{3,1,2,0:T(4,128)}, u32[]{:S(2)}) copy-start(f32[32,3,4,256]{3,1,2,0:T(4,128)} %constant_dynamic-update-slice_fusion.31) | copy-start | bytes 1179652
  104.7 7.3 %copy-start.28 = (bf16[384]{0:T(512)(128)(2,1)S(1)}, bf16[384]{0:T(512)(128)(2,1)}, u32[]{:S(2)}) copy-start(bf16[384]{0:T(512)(128)(2,1)} %param.33) | copy-start | bytes 2308
  106.0 22.9 %all-to-all-start.1 = ((f32[32,3,4,256]{3,2,1,0:T(4,128)}), f32[32,3,4,256]{3,2,1,0:T(4,128)}, u32[]{:S(2)}, u32[]{:S(2)}) async-start(f32[32,3,4,256]{3,2,1,0:T(4,128)} %copy.87), calls=%async_computation.1 | async-start | bytes 786432 | tf_op jit(solution)/shard_map/all_to_all | solution.py:224
  128.9 23.1 %all-to-all-start.2 = ((bf16[256,4,768]{0,2,1:T(8,128)(2,1)}), bf16[256,4,768]{0,2,1:T(8,128)(2,1)}, u32[]{:S(2)}, u32[]{:S(2)}) async-start(bf16[256,4,768]{0,2,1:T(8,128)(2,1)} %bitcast.327), calls=%async_computation.3 | async-start | bytes 3145728 | tf_op jit(solution)/shard_map/all_to_all | solution.py:259
  133.2 5.3 %copy-start.22 = (f32[256,3]{0,1:T(4,128)S(1)}, f32[256,3]{0,1:T(4,128)}, u32[]{:S(2)}) copy-start(f32[256,3]{0,1:T(4,128)} %get-tuple-element.76) | copy-start | bytes 9220
  133.2 60.0 %reduce-scatter.2.cloned.1.call-start = ((), (), s32[]{:S(2)}) async-start(), calls=%async_computation.4 | async-start | bytes 1966080 | tf_op jit(solution)/shard_map/reduce_scatter | solution.py:263
  143.4 0.7 copy-start.29
  143.4 0.8 copy-start.20
  143.4 0.9 copy-start.25
  162.3 21.1 %copy-start.27 = (f32[3]{0:T(128)S(1)}, f32[3]{0:T(128)}, u32[]{:S(2)}) copy-start(f32[3]{0:T(128)} %copy-done.26) | copy-start | bytes 40
  182.2 6.8 %collective-permute-start.6 = (bf16[256,256]{0,1:T(8,128)(2,1)S(1)}, bf16[256,256]{0,1:T(8,128)(2,1)S(1)}, u32[]{:S(2)}, u32[]{:S(2)}) collective-permute-start(bf16[256,256]{0,1:T(8,128)(2,1)S(1)} %bitcast.338), channel_id=1, source_target_pairs={{0,2},{2,4},{4,6},{6,0},{1,3},{3,5},{5,7},{7,1},{8,10},{10,12},{12... | collective-permute-start | bytes 393224 | tf_op jit(solution)/shard_map/ppermute | solution.py:270
  185.3 6.2 %collective-permute-start.7 = (bf16[256,256]{0,1:T(8,128)(2,1)S(1)}, bf16[256,256]{0,1:T(8,128)(2,1)S(1)}, u32[]{:S(2)}, u32[]{:S(2)}) collective-permute-start(bf16[256,256]{0,1:T(8,128)(2,1)S(1)} %bitcast.339), channel_id=1, source_target_pairs={{0,4},{2,6},{4,0},{6,2},{1,5},{3,7},{5,1},{7,3},{8,12},{10,14},{12... | collective-permute-start | bytes 393224 | tf_op jit(solution)/shard_map/ppermute | solution.py:270
  187.7 5.5 %collective-permute-start.8 = (bf16[256,256]{0,1:T(8,128)(2,1)S(1)}, bf16[256,256]{0,1:T(8,128)(2,1)S(1)}, u32[]{:S(2)}, u32[]{:S(2)}) collective-permute-start(bf16[256,256]{0,1:T(8,128)(2,1)S(1)} %bitcast.340), channel_id=1, source_target_pairs={{0,6},{2,0},{4,2},{6,4},{1,7},{3,1},{5,3},{7,5},{8,14},{10,8},{12,... | collective-permute-start | bytes 393224 | tf_op jit(solution)/shard_map/ppermute | solution.py:270
Sparse Core Ops, SparseCore 0:
  50.7 111.5 all-gather.1
Sparse Core Ops, SparseCore 1:
  143.5 27.4 reduce-scatter.1
